TPU v7x, 256 devices: a whole 4x4x8 slice. The times are simulated.
256 devices in a mesh: sweep: 8 (over y, core), layer: 32 (over z, x).
Axes of the slice: x: 4, y: 4, z: 8, core: 2. Of those that a mesh axis runs over, the one named last changes fastest.
Arguments:
- face_rhs: float32 [8, 16, 128, 384], P('sweep', None, 'layer'), may hold values from -6 to 6
- res_rows: float32 [131072, 384], P(('sweep', 'layer')), may hold values from -4 to 4
- row_owner: int32 [131072, 1], P(('sweep', 'layer')), may hold values from 0 to 31; in each aligned block of 512 rows (0 to 511, 512 to 1023, ...) at most 32 rows name the same one
- row_slot: int32 [131072], P(('sweep', 'layer')), may hold values from 0 to 63
- inv_blocks: bfloat16 [8, 128, 384, 384], P('sweep', 'layer'), may hold values from -0.3125 to 0.3125
- couple_in: bfloat16 [8, 1536, 49152], P('sweep', None, 'layer'), may hold values from -0.15625 to 0.15625
- couple_out: bfloat16 [8, 49152, 1536], P('sweep', 'layer'), may hold values from -0.02734375 to 0.02734375
Outputs:
- solved: float32 [8, 16, 128, 384], P('sweep', None, 'layer')
Inputs may be any that keep to these rules, and one draw needn't show every extreme that they name: `row_owner`: among the 512 rows of one device no owner is named by more than 32 rows, a bound that some block reaches.
All inputs are finite; a program needn't handle non-finite values.
Results may differ from a plain program's by a relative error of at most 0.02.
Values may be sent and summed in bfloat16 or wider, within the bound.
No kernel may reach another device: no remote copies, remote signals or barrier semaphores. Data moves between devices by JAX's collectives and lax.ppermute only.
A program may use at most 64 MiB of HBM per device.

v0:
```python
import jax
import jax.numpy as jnp
from jax import lax
from jax.sharding import PartitionSpec as P


def shifted(block, axis, distance):
    devices = range(lax.axis_size(axis))
    route = [(i - distance, i) for i in devices if i - distance in devices]
    return lax.ppermute(block, axis, route)


def on_device(face_rhs, res_rows, row_owner, row_slot, inv_blocks, couple_in, couple_out):
    group_size = lax.axis_size("layer")
    rhs_count = face_rhs.shape[1]
    face_dev = face_rhs.shape[2]
    face_width = face_rhs.shape[3]
    slot_count = rhs_count * face_dev
    row_total = res_rows.shape[0]
    owners = row_owner[:, 0]
    capacity = 2 * row_total // group_size
    matches = (owners[:, None] == jnp.arange(group_size, dtype=jnp.int32)[None, :]).astype(
        jnp.int32
    )
    earlier = jnp.cumsum(matches, axis=0) - matches
    position = jnp.sum(earlier * matches, axis=1)
    destination = owners * capacity + position
    send_rows = (
        jnp.zeros((group_size * capacity, face_width), jnp.float32).at[destination].set(res_rows)
    )
    send_slots = jnp.full((group_size * capacity,), -1, jnp.int32).at[destination].set(row_slot)
    got_rows, got_slots = (
        lax.all_to_all(
            send_rows.reshape(group_size, capacity, face_width),
            "layer",
            split_axis=0,
            concat_axis=0,
            tiled=True,
        ),
        lax.all_to_all(
            send_slots.reshape(group_size, capacity),
            "layer",
            split_axis=0,
            concat_axis=0,
            tiled=True,
        ),
    )
    one_hot = (jnp.arange(slot_count, dtype=jnp.int32)[:, None] == got_slots.reshape(1, -1)).astype(
        jnp.float32
    )
    added_rows = jnp.dot(one_hot, got_rows.reshape(-1, face_width), precision=lax.Precision.HIGHEST)
    assembled = face_rhs[0] + added_rows.reshape(rhs_count, face_dev, face_width)
    coupling_in = couple_in[0]
    coupling_out = couple_out[0]
    inverse = inv_blocks[0]
    sections = lax.axis_size("sweep")
    panel_in = jnp.zeros((rhs_count, coupling_in.shape[0]), jnp.bfloat16)
    solved = jnp.zeros_like(assembled)
    panel_part = jnp.zeros((rhs_count, coupling_in.shape[0]), jnp.float32)
    for step_index in range(sections):
        coupled = jnp.dot(panel_in, coupling_in, preferred_element_type=jnp.float32)
        local_part = (assembled - coupled.reshape(rhs_count, face_dev, face_width)).astype(
            jnp.bfloat16
        )
        solve_solved = jnp.einsum(
            "rfw,fwv->rfv", local_part, inverse, preferred_element_type=jnp.float32
        )
        flattened = solve_solved.astype(jnp.bfloat16).reshape(rhs_count, face_dev * face_width)
        solve_panel_part = jnp.dot(flattened, coupling_out, preferred_element_type=jnp.float32)
        solved = solve_solved
        panel_part = solve_panel_part
        if step_index + 1 < sections:
            summed = lax.psum(panel_part, "layer").astype(jnp.bfloat16)
            arrived = shifted(summed, "sweep", 1)
            panel_in = arrived
    return solved[None]


def solution(mesh):
    return jax.shard_map(
        on_device,
        mesh=mesh,
        in_specs=(
            P("sweep", None, "layer", None),
            P(("sweep", "layer"), None),
            P(("sweep", "layer"), None),
            P(("sweep", "layer")),
            P("sweep", "layer", None, None),
            P("sweep", None, "layer"),
            P("sweep", "layer", None),
        ),
        out_specs=P("sweep", None, "layer", None),
        check_vma=False,
    )
```

profile of v0, /device:TPU:1, one launch (start us, length us, event | category | flops | bytes accessed | tf_op | source)
XLA Modules:
  0.0 1123.9 jit_solution(9724480542182899194)
XLA Ops:
  0.0 0.0 copy-start
  0.0 0.0 copy-start.1
  0.0 0.8 fusion.171
  0.8 1.2 reduce-window.6
  2.0 0.2 slice_reduce_fusion
  2.2 0.8 fusion.170
  3.0 0.7 compare_select_fusion
  3.7 2.6 scatter_custom_fusion
  6.3 0.7 all_to_all.9
  7.0 11.9 %all-to-all-start = ((s32[32,1,32]{2,1,0:T(1,128)}), s32[32,1,32]{2,1,0:T(1,128)S(1)}, u32[]{:S(2)}, u32[]{:S(2)}) async-start(s32[32,1,32]{2,1,0:T(1,128)} %all_to_all.9), calls=%async_computation | async-start | bytes 32768 | tf_op jit(solution)/shard_map/all_to_all | solution.py:40
  18.9 4.0 scatter_custom_fusion.1
  22.9 4.5 all-to-all-done
  27.4 4.7 all-to-all-start.1
  32.1 0.5 broadcast.58
  32.7 0.7 reduce.5
  33.3 0.1 eq.63
  33.4 35.1 %all-to-all-done.1 = f32[32,32,384]{2,1,0:T(8,128)S(1)} async-done(((f32[32,32,384]{2,1,0:T(8,128)}), f32[32,32,384]{2,1,0:T(8,128)S(1)}, u32[]{:S(2)}, u32[]{:S(2)}) %all-to-all-start.1) | async-done | bytes 1572896 | tf_op jit(solution)/shard_map/all_to_all | solution.py:33
  68.5 0.0 copy-done.1
  68.5 0.7 convolution_add_fusion
  69.2 0.0 copy-done
  69.2 3.2 fusion.136
  72.4 3.1 fusion.28
  75.5 112.3 %psum.49 = bf16[16,1536]{1,0:T(8,128)(2,1)S(1)} all-reduce(f32[16,1536]{1,0:T(8,128)S(1)} %fusion.28), channel_id=1, replica_groups=mesh['sweep'=8,'layer'=32] {'layer'}, use_global_device_ids=true, to_apply=%region_5.6 | all-reduce | flops 24576 | bytes 147456 | tf_op jit(solution)/shard_map/psum | solution.py:73
  187.8 34.2 %collective-permute-start = (bf16[16,1536]{1,0:T(8,128)(2,1)S(1)}, bf16[16,1536]{1,0:T(8,128)(2,1)S(1)}, u32[]{:S(2)}, u32[]{:S(2)}) collective-permute-start(bf16[16,1536]{1,0:T(8,128)(2,1)S(1)} %psum.49), channel_id=1, source_target_pairs={{0,32},{32,64},{64,96},{96,128},{128,160},{160,192},{192,224},{1,3... | collective-permute-start | bytes 147464 | tf_op jit(solution)/shard_map/ppermute | solution.py:10
  222.0 1.2 collective-permute-done
  223.2 3.2 fusion.133
  226.4 3.1 fusion.26
  229.5 110.7 %psum.50 = bf16[16,1536]{1,0:T(8,128)(2,1)S(1)} all-reduce(f32[16,1536]{1,0:T(8,128)S(1)} %fusion.26), channel_id=1, replica_groups=mesh['sweep'=8,'layer'=32] {'layer'}, use_global_device_ids=true, to_apply=%region_6.7 | all-reduce | flops 24576 | bytes 147456 | tf_op jit(solution)/shard_map/psum | solution.py:73
  340.2 31.3 %collective-permute-start.1 = (bf16[16,1536]{1,0:T(8,128)(2,1)S(1)}, bf16[16,1536]{1,0:T(8,128)(2,1)S(1)}, u32[]{:S(2)}, u32[]{:S(2)}) collective-permute-start(bf16[16,1536]{1,0:T(8,128)(2,1)S(1)} %psum.50), channel_id=1, source_target_pairs={{0,32},{32,64},{64,96},{96,128},{128,160},{160,192},{192,224},{1,3... | collective-permute-start | bytes 147464 | tf_op jit(solution)/shard_map/ppermute | solution.py:10
  371.5 1.2 collective-permute-done.1
  372.6 3.2 fusion.130
  375.9 3.1 fusion.24
  378.9 110.1 %psum.51 = bf16[16,1536]{1,0:T(8,128)(2,1)S(1)} all-reduce(f32[16,1536]{1,0:T(8,128)S(1)} %fusion.24), channel_id=1, replica_groups=mesh['sweep'=8,'layer'=32] {'layer'}, use_global_device_ids=true, to_apply=%region_7.8 | all-reduce | flops 24576 | bytes 147456 | tf_op jit(solution)/shard_map/psum | solution.py:73
  489.0 31.9 %collective-permute-start.2 = (bf16[16,1536]{1,0:T(8,128)(2,1)S(1)}, bf16[16,1536]{1,0:T(8,128)(2,1)S(1)}, u32[]{:S(2)}, u32[]{:S(2)}) collective-permute-start(bf16[16,1536]{1,0:T(8,128)(2,1)S(1)} %psum.51), channel_id=1, source_target_pairs={{0,32},{32,64},{64,96},{96,128},{128,160},{160,192},{192,224},{1,3... | collective-permute-start | bytes 147464 | tf_op jit(solution)/shard_map/ppermute | solution.py:10
  520.9 1.2 collective-permute-done.2
  522.1 3.2 fusion.127
  525.3 3.1 fusion.22
  528.4 110.1 %psum.52 = bf16[16,1536]{1,0:T(8,128)(2,1)S(1)} all-reduce(f32[16,1536]{1,0:T(8,128)S(1)} %fusion.22), channel_id=1, replica_groups=mesh['sweep'=8,'layer'=32] {'layer'}, use_global_device_ids=true, to_apply=%region_8.9 | all-reduce | flops 24576 | bytes 147456 | tf_op jit(solution)/shard_map/psum | solution.py:73
  638.6 32.0 %collective-permute-start.3 = (bf16[16,1536]{1,0:T(8,128)(2,1)S(1)}, bf16[16,1536]{1,0:T(8,128)(2,1)S(1)}, u32[]{:S(2)}, u32[]{:S(2)}) collective-permute-start(bf16[16,1536]{1,0:T(8,128)(2,1)S(1)} %psum.52), channel_id=1, source_target_pairs={{0,32},{32,64},{64,96},{96,128},{128,160},{160,192},{192,224},{1,3... | collective-permute-start | bytes 147464 | tf_op jit(solution)/shard_map/ppermute | solution.py:10
  670.6 1.0 collective-permute-done.3
  671.6 3.2 fusion.124
  674.8 3.1 fusion.20
  677.9 110.4 %psum.53 = bf16[16,1536]{1,0:T(8,128)(2,1)S(1)} all-reduce(f32[16,1536]{1,0:T(8,128)S(1)} %fusion.20), channel_id=1, replica_groups=mesh['sweep'=8,'layer'=32] {'layer'}, use_global_device_ids=true, to_apply=%region_9.10 | all-reduce | flops 24576 | bytes 147456 | tf_op jit(solution)/shard_map/psum | solution.py:73
  788.2 31.6 %collective-permute-start.4 = (bf16[16,1536]{1,0:T(8,128)(2,1)S(1)}, bf16[16,1536]{1,0:T(8,128)(2,1)S(1)}, u32[]{:S(2)}, u32[]{:S(2)}) collective-permute-start(bf16[16,1536]{1,0:T(8,128)(2,1)S(1)} %psum.53), channel_id=1, source_target_pairs={{0,32},{32,64},{64,96},{96,128},{128,160},{160,192},{192,224},{1,3... | collective-permute-start | bytes 147464 | tf_op jit(solution)/shard_map/ppermute | solution.py:10
  819.9 1.2 collective-permute-done.4
  821.0 3.2 fusion.121
  824.3 3.1 fusion.18
  827.3 110.5 %psum.54 = bf16[16,1536]{1,0:T(8,128)(2,1)S(1)} all-reduce(f32[16,1536]{1,0:T(8,128)S(1)} %fusion.18), channel_id=1, replica_groups=mesh['sweep'=8,'layer'=32] {'layer'}, use_global_device_ids=true, to_apply=%region_10.11 | all-reduce | flops 24576 | bytes 147456 | tf_op jit(solution)/shard_map/psum | solution.py:73
  937.8 31.5 %collective-permute-start.5 = (bf16[16,1536]{1,0:T(8,128)(2,1)S(1)}, bf16[16,1536]{1,0:T(8,128)(2,1)S(1)}, u32[]{:S(2)}, u32[]{:S(2)}) collective-permute-start(bf16[16,1536]{1,0:T(8,128)(2,1)S(1)} %psum.54), channel_id=1, source_target_pairs={{0,32},{32,64},{64,96},{96,128},{128,160},{160,192},{192,224},{1,3... | collective-permute-start | bytes 147464 | tf_op jit(solution)/shard_map/ppermute | solution.py:10
  969.3 1.2 collective-permute-done.5
  970.5 3.2 fusion.118
  973.7 3.1 fusion.16
  976.8 110.7 %psum.55 = bf16[16,1536]{1,0:T(8,128)(2,1)S(1)} all-reduce(f32[16,1536]{1,0:T(8,128)S(1)} %fusion.16), channel_id=1, replica_groups=mesh['sweep'=8,'layer'=32] {'layer'}, use_global_device_ids=true, to_apply=%region_11.12 | all-reduce | flops 24576 | bytes 147456 | tf_op jit(solution)/shard_map/psum | solution.py:73
  1087.4 31.3 %collective-permute-start.6 = (bf16[16,1536]{1,0:T(8,128)(2,1)S(1)}, bf16[16,1536]{1,0:T(8,128)(2,1)S(1)}, u32[]{:S(2)}, u32[]{:S(2)}) collective-permute-start(bf16[16,1536]{1,0:T(8,128)(2,1)S(1)} %psum.55), channel_id=1, source_target_pairs={{0,32},{32,64},{64,96},{96,128},{128,160},{160,192},{192,224},{1,3... | collective-permute-start | bytes 147464 | tf_op jit(solution)/shard_map/ppermute | solution.py:10
  1118.8 1.2 collective-permute-done.6
  1120.0 3.2 fusion.46
  1123.2 0.7 copy.19
  (10 shorter events, 0.1 us)
Async XLA Ops:
  0.0 69.2 %copy-start = (bf16[1,4,384,384]{3,2,1,0:T(8,128)(2,1)S(1)}, bf16[1,4,384,384]{3,2,1,0:T(8,128)(2,1)}, u32[]{:S(2)}) copy-start(bf16[1,4,384,384]{3,2,1,0:T(8,128)(2,1)} %param.11) | copy-start | bytes 3538948
  0.0 68.5 %copy-start.1 = (f32[1,16,4,384]{3,2,1,0:T(4,128)S(1)}, f32[1,16,4,384]{3,2,1,0:T(4,128)}, u32[]{:S(2)}) copy-start(f32[1,16,4,384]{3,2,1,0:T(4,128)} %param.7) | copy-start | bytes 294916
  7.0 20.4 %all-to-all-start = ((s32[32,1,32]{2,1,0:T(1,128)}), s32[32,1,32]{2,1,0:T(1,128)S(1)}, u32[]{:S(2)}, u32[]{:S(2)}) async-start(s32[32,1,32]{2,1,0:T(1,128)} %all_to_all.9), calls=%async_computation | async-start | bytes 32768 | tf_op jit(solution)/shard_map/all_to_all | solution.py:40
  27.4 41.1 %all-to-all-start.1 = ((f32[32,32,384]{2,1,0:T(8,128)}), f32[32,32,384]{2,1,0:T(8,128)S(1)}, u32[]{:S(2)}, u32[]{:S(2)}) async-start(f32[32,32,384]{2,1,0:T(8,128)} %bitcast.6), calls=%async_computation.1 | async-start | bytes 3145728 | tf_op jit(solution)/shard_map/all_to_all | solution.py:33
  187.8 35.4 %collective-permute-start = (bf16[16,1536]{1,0:T(8,128)(2,1)S(1)}, bf16[16,1536]{1,0:T(8,128)(2,1)S(1)}, u32[]{:S(2)}, u32[]{:S(2)}) collective-permute-start(bf16[16,1536]{1,0:T(8,128)(2,1)S(1)} %psum.49), channel_id=1, source_target_pairs={{0,32},{32,64},{64,96},{96,128},{128,160},{160,192},{192,224},{1,3... | collective-permute-start | bytes 147464 | tf_op jit(solution)/shard_map/ppermute | solution.py:10
  340.2 32.4 %collective-permute-start.1 = (bf16[16,1536]{1,0:T(8,128)(2,1)S(1)}, bf16[16,1536]{1,0:T(8,128)(2,1)S(1)}, u32[]{:S(2)}, u32[]{:S(2)}) collective-permute-start(bf16[16,1536]{1,0:T(8,128)(2,1)S(1)} %psum.50), channel_id=1, source_target_pairs={{0,32},{32,64},{64,96},{96,128},{128,160},{160,192},{192,224},{1,3... | collective-permute-start | bytes 147464 | tf_op jit(solution)/shard_map/ppermute | solution.py:10
  489.0 33.1 %collective-permute-start.2 = (bf16[16,1536]{1,0:T(8,128)(2,1)S(1)}, bf16[16,1536]{1,0:T(8,128)(2,1)S(1)}, u32[]{:S(2)}, u32[]{:S(2)}) collective-permute-start(bf16[16,1536]{1,0:T(8,128)(2,1)S(1)} %psum.51), channel_id=1, source_target_pairs={{0,32},{32,64},{64,96},{96,128},{128,160},{160,192},{192,224},{1,3... | collective-permute-start | bytes 147464 | tf_op jit(solution)/shard_map/ppermute | solution.py:10
  638.6 33.0 %collective-permute-start.3 = (bf16[16,1536]{1,0:T(8,128)(2,1)S(1)}, bf16[16,1536]{1,0:T(8,128)(2,1)S(1)}, u32[]{:S(2)}, u32[]{:S(2)}) collective-permute-start(bf16[16,1536]{1,0:T(8,128)(2,1)S(1)} %psum.52), channel_id=1, source_target_pairs={{0,32},{32,64},{64,96},{96,128},{128,160},{160,192},{192,224},{1,3... | collective-permute-start | bytes 147464 | tf_op jit(solution)/shard_map/ppermute | solution.py:10
  788.2 32.8 %collective-permute-start.4 = (bf16[16,1536]{1,0:T(8,128)(2,1)S(1)}, bf16[16,1536]{1,0:T(8,128)(2,1)S(1)}, u32[]{:S(2)}, u32[]{:S(2)}) collective-permute-start(bf16[16,1536]{1,0:T(8,128)(2,1)S(1)} %psum.53), channel_id=1, source_target_pairs={{0,32},{32,64},{64,96},{96,128},{128,160},{160,192},{192,224},{1,3... | collective-permute-start | bytes 147464 | tf_op jit(solution)/shard_map/ppermute | solution.py:10
  937.8 32.7 %collective-permute-start.5 = (bf16[16,1536]{1,0:T(8,128)(2,1)S(1)}, bf16[16,1536]{1,0:T(8,128)(2,1)S(1)}, u32[]{:S(2)}, u32[]{:S(2)}) collective-permute-start(bf16[16,1536]{1,0:T(8,128)(2,1)S(1)} %psum.54), channel_id=1, source_target_pairs={{0,32},{32,64},{64,96},{96,128},{128,160},{160,192},{192,224},{1,3... | collective-permute-start | bytes 147464 | tf_op jit(solution)/shard_map/ppermute | solution.py:10
  1087.4 32.5 %collective-permute-start.6 = (bf16[16,1536]{1,0:T(8,128)(2,1)S(1)}, bf16[16,1536]{1,0:T(8,128)(2,1)S(1)}, u32[]{:S(2)}, u32[]{:S(2)}) collective-permute-start(bf16[16,1536]{1,0:T(8,128)(2,1)S(1)} %psum.55), channel_id=1, source_target_pairs={{0,32},{32,64},{64,96},{96,128},{128,160},{160,192},{192,224},{1,3... | collective-permute-start | bytes 147464 | tf_op jit(solution)/shard_map/ppermute | solution.py:10
where the time goes:
time: 1130 us; the launch traced here: 1120 us
  blocking collectives  775 us (69%)
  starting transfers between devices  241 us (21%)
  matrix products  47.8 us (4%)
  waiting for transfers between devices  47.5 us (4%)
    psum x7, blocking collectives, on_device(): summed = lax.psum(panel_part, 'layer').astype(jnp.bfloat16)  775 us
    ppermute x7, starting transfers between devices, shifted(): return lax.ppermute(block, axis, route)  224 us
    all_to_all x1, waiting for transfers between devices, on_device(): lax.all_to_all(send_rows.reshape(group_size, capacity, face_width), 'laye...  35.1 us
    dot_general x8, matrix products, on_device(): jnp.einsum('rfw,fwv->rfv', local_part, inverse, preferred_element_type=jn...  25.7 us
  transfers between devices with their start and end apart: 9, of which 9 were waited for; matrix products, arithmetic and copies ran while one was open for 0% of the time, Pallas kernels for 0%

commit v1 on v0

v1 whole, which is shorter than its diff:
```python
import jax
import jax.numpy as jnp
from jax import lax
from jax.experimental import pallas as pl
from jax.experimental.pallas import tpu as pltpu
from jax.sharding import Mesh
from jax.sharding import PartitionSpec as P

BF = jnp.bfloat16
F32 = jnp.float32
LANES = 128


def pack_kernel(owner_count, owner_ref, slot_ref, rows_ref, out_ref):
    row_total, width = rows_ref.shape
    capacity = row_total // owner_count * 2
    owner = owner_ref[...]
    match = (lax.broadcasted_iota(jnp.int32, (owner_count, row_total), 0) == owner).astype(F32)
    earlier_mask = (
        lax.broadcasted_iota(jnp.int32, (row_total, row_total), 0)
        < lax.broadcasted_iota(jnp.int32, (row_total, row_total), 1)
    )
    earlier = jnp.dot(
        match.astype(BF), earlier_mask.astype(F32).astype(BF), preferred_element_type=F32
    )
    position = jnp.sum(earlier * match, axis=0, keepdims=True).astype(jnp.int32)
    target = owner * capacity + position
    slots = (slot_ref[...] + 1).astype(F32)
    rows = rows_ref[...].astype(BF)
    block = 256
    for start in range(0, owner_count * capacity, block):
        place = lax.broadcasted_iota(jnp.int32, (block, row_total), 0) + start
        chosen = place == target
        picked = jnp.where(chosen, 1.0, 0.0).astype(BF)
        out_ref[pl.ds(start, block), pl.ds(0, width)] = jnp.dot(
            picked, rows, preferred_element_type=F32
        ).astype(BF)
        slot = jnp.sum(jnp.where(chosen, slots, 0.0), axis=1, keepdims=True)
        out_ref[pl.ds(start, block), pl.ds(width, LANES)] = jnp.broadcast_to(
            slot, (block, LANES)
        ).astype(BF)


def unpack_kernel(face_dev, got_ref, face_ref, out_ref):
    rhs_count = out_ref.shape[0]
    width = out_ref.shape[1] // face_dev
    slot = got_ref[:, pl.ds(width, LANES)].astype(F32)
    lane = lax.broadcasted_iota(jnp.int32, slot.shape, 1)
    wanted = (lane % rhs_count) * face_dev + lane // rhs_count + 1
    wanted = jnp.where(lane < rhs_count * face_dev, wanted, -1).astype(F32)
    picked = jnp.where(slot == wanted, 1.0, 0.0).astype(BF)
    summed = lax.dot_general(
        picked,
        got_ref[:, pl.ds(0, width)],
        (((0,), (0,)), ((), ())),
        preferred_element_type=F32,
    )
    for face in range(face_dev):
        out_ref[:, pl.ds(face * width, width)] = (
            face_ref[:, face, :] + summed[face * rhs_count : (face + 1) * rhs_count, :]
        )


def on_device(shape, face_rhs, res_rows, row_owner, row_slot, inv_blocks, couple_in, couple_out):
    sweep_count, z_count, x_count = shape
    group_size = z_count * x_count
    rhs_count, face_dev, width = face_rhs.shape[1:]
    row_total = res_rows.shape[0]
    capacity = 2 * row_total // group_size
    coupling_in, coupling_out, inverse = couple_in[0], couple_out[0], inv_blocks[0]

    with jax.named_scope("pack"):
        packed = pl.pallas_call(
            lambda *refs: pack_kernel(group_size, *refs),
            out_shape=jax.ShapeDtypeStruct((group_size * capacity, width + LANES), BF),
            name="pack",
        )(row_owner.reshape(1, row_total), row_slot.reshape(1, row_total), res_rows)
    with jax.named_scope("route"):
        got = lax.all_to_all(
            packed.reshape(group_size, capacity, width + LANES),
            ("z", "x"),
            split_axis=0,
            concat_axis=0,
            tiled=True,
        ).reshape(group_size * capacity, width + LANES)
    with jax.named_scope("fold"):
        outward = jnp.einsum(
            "fwv,fvp->fwp",
            inverse,
            coupling_out.reshape(face_dev, width, -1),
            preferred_element_type=F32,
        )
        outward = outward.astype(BF).reshape(face_dev * width, -1)
        through = jnp.dot(coupling_in, outward, preferred_element_type=F32).astype(BF)
    with jax.named_scope("unpack"):
        assembled = pl.pallas_call(
            lambda *refs: unpack_kernel(face_dev, *refs),
            out_shape=jax.ShapeDtypeStruct((rhs_count, face_dev * width), F32),
            name="unpack",
        )(got, face_rhs[0])
    with jax.named_scope("source"):
        high = assembled.astype(BF)
        low = (assembled - high.astype(F32)).astype(BF)
        both = jnp.dot(
            jnp.concatenate([high, low], axis=0), outward, preferred_element_type=F32
        )
        source = both[:rhs_count] + both[rhs_count:]

    def number(s, z, x):
        return (s * z_count + z) * x_count + x

    def exchange(value, layer, mask_x, mask_z, shift=0):
        pairs = [
            (number(layer, z, x), number(layer + shift, z ^ mask_z, x ^ mask_x))
            for z in range(z_count)
            for x in range(x_count)
        ]
        return lax.ppermute(value, ("sweep", "z", "x"), pairs)

    def total(values):
        result = values[0].astype(F32)
        for value in values[1:]:
            result = result + value.astype(F32)
        return result

    panel = None
    arrived = []
    for layer in range(sweep_count - 1):
        with jax.named_scope("stage%d" % layer):
            part = source
            if panel is not None:
                part = source - jnp.dot(panel, through, preferred_element_type=F32)
            part = part.astype(BF)
            part = total([part] + [exchange(part, layer, m, 0) for m in range(1, x_count)])
            part = part.astype(BF)
            part = total([part] + [exchange(part, layer, 0, m) for m in range(1, z_count // 2)])
            part = part.astype(BF)
            panel = total(
                [exchange(part, layer, 0, m, 1) for m in (0, z_count - 1)]
            ).astype(BF)
            arrived.append(panel)
    with jax.named_scope("solve"):
        panel = total(arrived).astype(BF)
        coupled = jnp.dot(panel, coupling_in, preferred_element_type=F32)
        local = (assembled - coupled).astype(BF).reshape(rhs_count, face_dev, width)
        solved = jnp.einsum("rfw,fwv->rfv", local, inverse, preferred_element_type=F32)
    return solved[None]


def solution(mesh):
    shape = (mesh.shape["sweep"], 8, mesh.shape["layer"] // 8)
    fine = Mesh(mesh.devices.reshape(shape), ("sweep", "z", "x"))
    layer = ("z", "x")
    everywhere = ("sweep", "z", "x")
    return jax.shard_map(
        lambda *args: on_device(shape, *args),
        mesh=fine,
        in_specs=(
            P("sweep", None, layer, None),
            P(everywhere, None),
            P(everywhere, None),
            P(everywhere),
            P("sweep", layer, None, None),
            P("sweep", None, layer),
            P("sweep", layer, None),
        ),
        out_specs=P("sweep", None, layer, None),
        check_vma=False,
    )
```

time: 1130 us -> 477 us (0.42)
  blocking collectives: 775 us -> 0 us
  starting transfers between devices: 241 us -> 396 us
  matrix products: 47.8 us -> 28.5 us
    psum x7 -> x0, blocking collectives: 775 us -> none  [on_device(): summed = lax.psum(panel_part, 'layer').astype(jnp.bfloat16)]
    ppermute x7 -> x56, starting transfers between devices: 224 us -> 385 us  [exchange(): return lax.ppermute(value, ('sweep', 'z', 'x'), pairs)]
    all_to_all x2 -> x1, waiting for transfers between devices: 39.5 us -> 19.6 us  [on_device(): lax.all_to_all(packed.reshape(group_size, capacity, width + LANES), ('z',...]
    dot_general x16 -> x11, matrix products: 47.8 us -> 28.5 us  [the longest x1 9.5 us: on_device(): jnp.dot(coupling_in, outward, preferred_element_type=F32).astype(BF)]
    ppermute x7 -> x56, waiting for transfers between devices: 7.91 us -> 21.7 us  [exchange(): return lax.ppermute(value, ('sweep', 'z', 'x'), pairs)]
  transfers between devices with their start and end apart: 9 -> 57, of which waited for: 9 -> 8; matrix products, arithmetic and copies ran while one was open for 0% -> 3% of each run, Pallas kernels for 0% -> 0%
where the time goes in v1:
time: 477 us; the launch traced here: 476 us
  starting transfers between devices  396 us (83%)
  waiting for transfers between devices  41.3 us (9%)
  matrix products  28.5 us (6%)
  Pallas kernels  5.46 us (1%)
    ppermute x56, starting transfers between devices, exchange(): return lax.ppermute(value, ('sweep', 'z', 'x'), pairs)  385 us
    ppermute x56, waiting for transfers between devices, exchange(): return lax.ppermute(value, ('sweep', 'z', 'x'), pairs)  21.7 us
    all_to_all x1, waiting for transfers between devices, on_device(): lax.all_to_all(packed.reshape(group_size, capacity, width + LANES), ('z',...  19.6 us
    all_to_all x1, starting transfers between devices, on_device(): lax.all_to_all(packed.reshape(group_size, capacity, width + LANES), ('z',...  11.9 us
  transfers between devices with their start and end apart: 57, of which 8 were waited for; matrix products, arithmetic and copies ran while one was open for 3% of the time, Pallas kernels for 0%

profile of v1, /device:TPU:1, one launch (start us, length us, event | category | flops | bytes accessed | tf_op | source)
XLA Modules:
  0.0 475.8 jit_solution(697500153091094224)
XLA Ops:
  0.0 3.3 pack.1
  3.3 11.9 %all-to-all-start = ((bf16[32,32,512]{2,1,0:T(8,128)(2,1)}), bf16[32,32,512]{2,1,0:T(8,128)(2,1)S(1)}, u32[]{:S(2)}, u32[]{:S(2)}) async-start(bf16[32,32,512]{2,1,0:T(8,128)(2,1)} %bitcast.45), calls=%async_computation | async-start | bytes 2097152 | tf_op jit(solution)/shard_map/route/all_to_all | solution.py:79
  15.2 6.6 %convolution_convert_fusion.1 = bf16[4,384,1536]{2,1,0:T(8,128)(2,1)} fusion(bf16[4,384,1536]{2,1,0:T(8,128)(2,1)} %bitcast.42, bf16[1,4,384,384]{3,2,1,0:T(8,128)(2,1)S(1)} %copy-done), kind=kOutput, calls=%fused_computation.4 | convolution fusion | flops 1814298624 | bytes 10616832 | tf_op jit(solution)/shard_map/fold/fwv,fvp->fwp/dot_general | solution.py:87
  21.7 19.6 %all-to-all-done = bf16[32,32,512]{2,1,0:T(8,128)(2,1)S(1)} async-done(((bf16[32,32,512]{2,1,0:T(8,128)(2,1)}), bf16[32,32,512]{2,1,0:T(8,128)(2,1)S(1)}, u32[]{:S(2)}, u32[]{:S(2)}) %all-to-all-start) | async-done | bytes 1048608 | tf_op jit(solution)/shard_map/route/all_to_all | solution.py:79
  41.3 1.0 copy-done.2
  42.3 2.2 unpack.1
  44.5 1.1 subtract_convert_fusion
  45.6 3.5 fusion.21
  49.2 0.7 collective-permute-start.2
  49.9 0.7 collective-permute-start.1
  50.5 0.7 collective-permute-start
  52.6 0.7 collective-permute-start.3
  53.3 1.3 collective-permute-start.7
  54.6 1.3 collective-permute-start.6
  56.0 9.5 %convolution_convert_fusion = bf16[1536,1536]{1,0:T(8,128)(2,1)S(1)} fusion(bf16[1536,1536]{1,0:T(8,128)(2,1)S(1)} %bitcast.41, bf16[1,1536,1536]{2,1,0:T(8,128)(2,1)} %param.12), kind=kOutput, calls=%fused_computation | convolution fusion | flops 7250116608 | bytes 14155776 | tf_op jit(solution)/shard_map/fold/dot_general | solution.py:94
  65.5 15.8 %collective-permute-done.7 = bf16[16,1536]{1,0:T(8,128)(2,1)S(1)} collective-permute-done((bf16[16,1536]{1,0:T(8,128)(2,1)S(1)}, bf16[16,1536]{1,0:T(8,128)(2,1)S(1)}, u32[]{:S(2)}, u32[]{:S(2)}) %collective-permute-start.7) | collective-permute-done | bytes 49184 | tf_op jit(solution)/shard_map/stage0/ppermute | solution.py:118
  81.3 1.3 fusion.6
  82.6 3.6 collective-permute-start.10
  86.2 2.6 collective-permute-start.9
  88.9 2.8 collective-permute-start.8
  91.7 0.9 collective-permute-done.9
  92.6 1.1 collective-permute-done.8
  93.7 4.2 collective-permute-start.13
  98.0 2.8 collective-permute-start.12
  100.7 2.3 collective-permute-start.11
  103.7 1.9 collective-permute-done.11
  105.6 1.3 collective-permute-start.15
  106.9 1.3 collective-permute-start.14
  108.4 0.9 collective-permute-done.14
  109.4 1.3 fusion.7
  110.7 0.7 collective-permute-start.18
  111.3 0.7 collective-permute-start.17
  112.0 0.7 collective-permute-start.16
  112.8 0.7 collective-permute-start.21
  116.2 1.3 fusion.8
  117.5 0.7 collective-permute-start.26
  123.1 1.3 fusion.9
  124.4 0.7 collective-permute-start.34
  125.7 0.8 collective-permute-start.32
  126.7 68.9 %collective-permute-start.37 = (bf16[16,1536]{1,0:T(8,128)(2,1)S(1)}, bf16[16,1536]{1,0:T(8,128)(2,1)S(1)}, u32[]{:S(2)}, u32[]{:S(2)}) collective-permute-start(bf16[16,1536]{1,0:T(8,128)(2,1)S(1)} %add_convert_fusion.9), channel_id=1, source_target_pairs={{128,140},{129,141},{130,142},{131,143},{132,136},{133,137},{134,1... | collective-permute-start | bytes 147464 | tf_op jit(solution)/shard_map/stage4/ppermute | solution.py:118
  195.5 13.1 %collective-permute-start.36 = (bf16[16,1536]{1,0:T(8,128)(2,1)S(1)}, bf16[16,1536]{1,0:T(8,128)(2,1)S(1)}, u32[]{:S(2)}, u32[]{:S(2)}) collective-permute-start(bf16[16,1536]{1,0:T(8,128)(2,1)S(1)} %add_convert_fusion.9), channel_id=1, source_target_pairs={{128,136},{129,137},{130,138},{131,139},{132,140},{133,141},{134,1... | collective-permute-start | bytes 147464 | tf_op jit(solution)/shard_map/stage4/ppermute | solution.py:118
  208.7 13.1 %collective-permute-start.35 = (bf16[16,1536]{1,0:T(8,128)(2,1)S(1)}, bf16[16,1536]{1,0:T(8,128)(2,1)S(1)}, u32[]{:S(2)}, u32[]{:S(2)}) collective-permute-start(bf16[16,1536]{1,0:T(8,128)(2,1)S(1)} %add_convert_fusion.9), channel_id=1, source_target_pairs={{128,132},{129,133},{130,134},{131,135},{132,128},{133,129},{134,1... | collective-permute-start | bytes 147464 | tf_op jit(solution)/shard_map/stage4/ppermute | solution.py:118
  221.9 16.1 %collective-permute-start.39 = (bf16[16,1536]{1,0:T(8,128)(2,1)S(1)}, bf16[16,1536]{1,0:T(8,128)(2,1)S(1)}, u32[]{:S(2)}, u32[]{:S(2)}) collective-permute-start(bf16[16,1536]{1,0:T(8,128)(2,1)S(1)} %add_convert_fusion.8), channel_id=1, source_target_pairs={{128,188},{129,189},{130,190},{131,191},{132,184},{133,185},{134,1... | collective-permute-start | bytes 147464 | tf_op jit(solution)/shard_map/stage4/ppermute | solution.py:118
  238.0 13.1 %collective-permute-start.38 = (bf16[16,1536]{1,0:T(8,128)(2,1)S(1)}, bf16[16,1536]{1,0:T(8,128)(2,1)S(1)}, u32[]{:S(2)}, u32[]{:S(2)}) collective-permute-start(bf16[16,1536]{1,0:T(8,128)(2,1)S(1)} %add_convert_fusion.8), channel_id=1, source_target_pairs={{128,160},{129,161},{130,162},{131,163},{132,164},{133,165},{134,1... | collective-permute-start | bytes 147464 | tf_op jit(solution)/shard_map/stage4/ppermute | solution.py:118
  251.1 1.3 fusion.10
  252.4 14.0 %collective-permute-start.42 = (bf16[16,1536]{1,0:T(8,128)(2,1)S(1)}, bf16[16,1536]{1,0:T(8,128)(2,1)S(1)}, u32[]{:S(2)}, u32[]{:S(2)}) collective-permute-start(bf16[16,1536]{1,0:T(8,128)(2,1)S(1)} %fusion.10), channel_id=1, source_target_pairs={{160,163},{161,162},{162,161},{163,160},{164,167},{165,166},{166,1... | collective-permute-start | bytes 147464 | tf_op jit(solution)/shard_map/stage5/ppermute | solution.py:118
  266.4 12.9 %collective-permute-start.41 = (bf16[16,1536]{1,0:T(8,128)(2,1)S(1)}, bf16[16,1536]{1,0:T(8,128)(2,1)S(1)}, u32[]{:S(2)}, u32[]{:S(2)}) collective-permute-start(bf16[16,1536]{1,0:T(8,128)(2,1)S(1)} %fusion.10), channel_id=1, source_target_pairs={{160,162},{161,163},{162,160},{163,161},{164,166},{165,167},{166,1... | collective-permute-start | bytes 147464 | tf_op jit(solution)/shard_map/stage5/ppermute | solution.py:118
  279.3 12.9 %collective-permute-start.40 = (bf16[16,1536]{1,0:T(8,128)(2,1)S(1)}, bf16[16,1536]{1,0:T(8,128)(2,1)S(1)}, u32[]{:S(2)}, u32[]{:S(2)}) collective-permute-start(bf16[16,1536]{1,0:T(8,128)(2,1)S(1)} %fusion.10), channel_id=1, source_target_pairs={{160,161},{161,160},{162,163},{163,162},{164,165},{165,164},{166,1... | collective-permute-start | bytes 147464 | tf_op jit(solution)/shard_map/stage5/ppermute | solution.py:118
  292.2 15.2 %collective-permute-start.45 = (bf16[16,1536]{1,0:T(8,128)(2,1)S(1)}, bf16[16,1536]{1,0:T(8,128)(2,1)S(1)}, u32[]{:S(2)}, u32[]{:S(2)}) collective-permute-start(bf16[16,1536]{1,0:T(8,128)(2,1)S(1)} %add_convert_fusion.6), channel_id=1, source_target_pairs={{160,172},{161,173},{162,174},{163,175},{164,168},{165,169},{166,1... | collective-permute-start | bytes 147464 | tf_op jit(solution)/shard_map/stage5/ppermute | solution.py:118
  307.5 12.9 %collective-permute-start.44 = (bf16[16,1536]{1,0:T(8,128)(2,1)S(1)}, bf16[16,1536]{1,0:T(8,128)(2,1)S(1)}, u32[]{:S(2)}, u32[]{:S(2)}) collective-permute-start(bf16[16,1536]{1,0:T(8,128)(2,1)S(1)} %add_convert_fusion.6), channel_id=1, source_target_pairs={{160,168},{161,169},{162,170},{163,171},{164,172},{165,173},{166,1... | collective-permute-start | bytes 147464 | tf_op jit(solution)/shard_map/stage5/ppermute | solution.py:118
  320.3 12.9 %collective-permute-start.43 = (bf16[16,1536]{1,0:T(8,128)(2,1)S(1)}, bf16[16,1536]{1,0:T(8,128)(2,1)S(1)}, u32[]{:S(2)}, u32[]{:S(2)}) collective-permute-start(bf16[16,1536]{1,0:T(8,128)(2,1)S(1)} %add_convert_fusion.6), channel_id=1, source_target_pairs={{160,164},{161,165},{162,166},{163,167},{164,160},{165,161},{166,1... | collective-permute-start | bytes 147464 | tf_op jit(solution)/shard_map/stage5/ppermute | solution.py:118
  333.3 14.9 %collective-permute-start.47 = (bf16[16,1536]{1,0:T(8,128)(2,1)S(1)}, bf16[16,1536]{1,0:T(8,128)(2,1)S(1)}, u32[]{:S(2)}, u32[]{:S(2)}) collective-permute-start(bf16[16,1536]{1,0:T(8,128)(2,1)S(1)} %add_convert_fusion.5), channel_id=1, source_target_pairs={{160,220},{161,221},{162,222},{163,223},{164,216},{165,217},{166,2... | collective-permute-start | bytes 147464 | tf_op jit(solution)/shard_map/stage5/ppermute | solution.py:118
  348.1 12.9 %collective-permute-start.46 = (bf16[16,1536]{1,0:T(8,128)(2,1)S(1)}, bf16[16,1536]{1,0:T(8,128)(2,1)S(1)}, u32[]{:S(2)}, u32[]{:S(2)}) collective-permute-start(bf16[16,1536]{1,0:T(8,128)(2,1)S(1)} %add_convert_fusion.5), channel_id=1, source_target_pairs={{160,192},{161,193},{162,194},{163,195},{164,196},{165,197},{166,1... | collective-permute-start | bytes 147464 | tf_op jit(solution)/shard_map/stage5/ppermute | solution.py:118
  361.0 1.3 fusion.11
  362.4 15.2 %collective-permute-start.50 = (bf16[16,1536]{1,0:T(8,128)(2,1)S(1)}, bf16[16,1536]{1,0:T(8,128)(2,1)S(1)}, u32[]{:S(2)}, u32[]{:S(2)}) collective-permute-start(bf16[16,1536]{1,0:T(8,128)(2,1)S(1)} %fusion.11), channel_id=1, source_target_pairs={{192,195},{193,194},{194,193},{195,192},{196,199},{197,198},{198,1... | collective-permute-start | bytes 147464 | tf_op jit(solution)/shard_map/stage6/ppermute | solution.py:118
  377.5 12.9 %collective-permute-start.49 = (bf16[16,1536]{1,0:T(8,128)(2,1)S(1)}, bf16[16,1536]{1,0:T(8,128)(2,1)S(1)}, u32[]{:S(2)}, u32[]{:S(2)}) collective-permute-start(bf16[16,1536]{1,0:T(8,128)(2,1)S(1)} %fusion.11), channel_id=1, source_target_pairs={{192,194},{193,195},{194,192},{195,193},{196,198},{197,199},{198,1... | collective-permute-start | bytes 147464 | tf_op jit(solution)/shard_map/stage6/ppermute | solution.py:118
  390.4 12.9 %collective-permute-start.48 = (bf16[16,1536]{1,0:T(8,128)(2,1)S(1)}, bf16[16,1536]{1,0:T(8,128)(2,1)S(1)}, u32[]{:S(2)}, u32[]{:S(2)}) collective-permute-start(bf16[16,1536]{1,0:T(8,128)(2,1)S(1)} %fusion.11), channel_id=1, source_target_pairs={{192,193},{193,192},{194,195},{195,194},{196,197},{197,196},{198,1... | collective-permute-start | bytes 147464 | tf_op jit(solution)/shard_map/stage6/ppermute | solution.py:118
  403.4 16.1 %collective-permute-start.53 = (bf16[16,1536]{1,0:T(8,128)(2,1)S(1)}, bf16[16,1536]{1,0:T(8,128)(2,1)S(1)}, u32[]{:S(2)}, u32[]{:S(2)}) collective-permute-start(bf16[16,1536]{1,0:T(8,128)(2,1)S(1)} %add_convert_fusion.3), channel_id=1, source_target_pairs={{192,204},{193,205},{194,206},{195,207},{196,200},{197,201},{198,2... | collective-permute-start | bytes 147464 | tf_op jit(solution)/shard_map/stage6/ppermute | solution.py:118
  419.5 12.9 %collective-permute-start.52 = (bf16[16,1536]{1,0:T(8,128)(2,1)S(1)}, bf16[16,1536]{1,0:T(8,128)(2,1)S(1)}, u32[]{:S(2)}, u32[]{:S(2)}) collective-permute-start(bf16[16,1536]{1,0:T(8,128)(2,1)S(1)} %add_convert_fusion.3), channel_id=1, source_target_pairs={{192,200},{193,201},{194,202},{195,203},{196,204},{197,205},{198,2... | collective-permute-start | bytes 147464 | tf_op jit(solution)/shard_map/stage6/ppermute | solution.py:118
  432.4 12.9 %collective-permute-start.51 = (bf16[16,1536]{1,0:T(8,128)(2,1)S(1)}, bf16[16,1536]{1,0:T(8,128)(2,1)S(1)}, u32[]{:S(2)}, u32[]{:S(2)}) collective-permute-start(bf16[16,1536]{1,0:T(8,128)(2,1)S(1)} %add_convert_fusion.3), channel_id=1, source_target_pairs={{192,196},{193,197},{194,198},{195,199},{196,192},{197,193},{198,1... | collective-permute-start | bytes 147464 | tf_op jit(solution)/shard_map/stage6/ppermute | solution.py:118
  445.4 15.8 %collective-permute-start.55 = (bf16[16,1536]{1,0:T(8,128)(2,1)S(1)}, bf16[16,1536]{1,0:T(8,128)(2,1)S(1)}, u32[]{:S(2)}, u32[]{:S(2)}) collective-permute-start(bf16[16,1536]{1,0:T(8,128)(2,1)S(1)} %add_convert_fusion.2), channel_id=1, source_target_pairs={{192,252},{193,253},{194,254},{195,255},{196,248},{197,249},{198,2... | collective-permute-start | bytes 147464 | tf_op jit(solution)/shard_map/stage6/ppermute | solution.py:118
  461.1 12.9 %collective-permute-start.54 = (bf16[16,1536]{1,0:T(8,128)(2,1)S(1)}, bf16[16,1536]{1,0:T(8,128)(2,1)S(1)}, u32[]{:S(2)}, u32[]{:S(2)}) collective-permute-start(bf16[16,1536]{1,0:T(8,128)(2,1)S(1)} %add_convert_fusion.2), channel_id=1, source_target_pairs={{192,224},{193,225},{194,226},{195,227},{196,228},{197,229},{198,2... | collective-permute-start | bytes 147464 | tf_op jit(solution)/shard_map/stage6/ppermute | solution.py:118
  474.1 0.7 fusion.12
  475.1 0.7 copy.9
  (93 shorter events, 11.1 us)
Async XLA Ops:
  0.0 15.1 %copy-start = (bf16[1,4,384,384]{3,2,1,0:T(8,128)(2,1)S(1)}, bf16[1,4,384,384]{3,2,1,0:T(8,128)(2,1)}, u32[]{:S(2)}) copy-start(bf16[1,4,384,384]{3,2,1,0:T(8,128)(2,1)} %param.11) | copy-start | bytes 3538948
  3.3 38.1 %all-to-all-start = ((bf16[32,32,512]{2,1,0:T(8,128)(2,1)}), bf16[32,32,512]{2,1,0:T(8,128)(2,1)S(1)}, u32[]{:S(2)}, u32[]{:S(2)}) async-start(bf16[32,32,512]{2,1,0:T(8,128)(2,1)} %bitcast.45), calls=%async_computation | async-start | bytes 2097152 | tf_op jit(solution)/shard_map/route/all_to_all | solution.py:79
  41.3 1.0 copy-start.2
  44.5 11.4 %copy-start.1 = (bf16[4,384,1536]{2,1,0:T(8,128)(2,1)S(1)}, bf16[4,384,1536]{2,1,0:T(8,128)(2,1)}, u32[]{:S(2)}) copy-start(bf16[4,384,1536]{2,1,0:T(8,128)(2,1)} %convolution_convert_fusion.1) | copy-start | bytes 14155780
  49.2 2.0 collective-permute-start.2
  49.9 1.4 collective-permute-start.1
  50.5 0.7 collective-permute-start
  51.3 2.0 collective-permute-start.5
  51.9 1.4 collective-permute-start.4
  52.6 0.7 collective-permute-start.3
  53.3 28.0 %collective-permute-start.7 = (bf16[16,1536]{1,0:T(8,128)(2,1)S(1)}, bf16[16,1536]{1,0:T(8,128)(2,1)S(1)}, u32[]{:S(2)}, u32[]{:S(2)}) collective-permute-start(bf16[16,1536]{1,0:T(8,128)(2,1)S(1)} %add_convert_fusion.20), channel_id=1, source_target_pairs={{0,60},{1,61},{2,62},{3,63},{4,56},{5,57},{6,58},{7,59},{8,52},{9,... | collective-permute-start | bytes 147464 | tf_op jit(solution)/shard_map/stage0/ppermute | solution.py:118
  54.6 26.7 %collective-permute-start.6 = (bf16[16,1536]{1,0:T(8,128)(2,1)S(1)}, bf16[16,1536]{1,0:T(8,128)(2,1)S(1)}, u32[]{:S(2)}, u32[]{:S(2)}) collective-permute-start(bf16[16,1536]{1,0:T(8,128)(2,1)S(1)} %add_convert_fusion.20), channel_id=1, source_target_pairs={{0,32},{1,33},{2,34},{3,35},{4,36},{5,37},{6,38},{7,39},{8,40},{9,... | collective-permute-start | bytes 147464 | tf_op jit(solution)/shard_map/stage0/ppermute | solution.py:118
  82.6 9.0 %collective-permute-start.10 = (bf16[16,1536]{1,0:T(8,128)(2,1)S(1)}, bf16[16,1536]{1,0:T(8,128)(2,1)S(1)}, u32[]{:S(2)}, u32[]{:S(2)}) collective-permute-start(bf16[16,1536]{1,0:T(8,128)(2,1)S(1)} %fusion.6), channel_id=1, source_target_pairs={{32,35},{33,34},{34,33},{35,32},{36,39},{37,38},{38,37},{39,36},{4... | collective-permute-start | bytes 147464 | tf_op jit(solution)/shard_map/stage1/ppermute | solution.py:118
  86.2 6.3 %collective-permute-start.9 = (bf16[16,1536]{1,0:T(8,128)(2,1)S(1)}, bf16[16,1536]{1,0:T(8,128)(2,1)S(1)}, u32[]{:S(2)}, u32[]{:S(2)}) collective-permute-start(bf16[16,1536]{1,0:T(8,128)(2,1)S(1)} %fusion.6), channel_id=1, source_target_pairs={{32,34},{33,35},{34,32},{35,33},{36,38},{37,39},{38,36},{39,37},{4... | collective-permute-start | bytes 147464 | tf_op jit(solution)/shard_map/stage1/ppermute | solution.py:118
  88.9 4.8 %collective-permute-start.8 = (bf16[16,1536]{1,0:T(8,128)(2,1)S(1)}, bf16[16,1536]{1,0:T(8,128)(2,1)S(1)}, u32[]{:S(2)}, u32[]{:S(2)}) collective-permute-start(bf16[16,1536]{1,0:T(8,128)(2,1)S(1)} %fusion.6), channel_id=1, source_target_pairs={{32,33},{33,32},{34,35},{35,34},{36,37},{37,36},{38,39},{39,38},{4... | collective-permute-start | bytes 147464 | tf_op jit(solution)/shard_map/stage1/ppermute | solution.py:118
  93.7 9.3 %collective-permute-start.13 = (bf16[16,1536]{1,0:T(8,128)(2,1)S(1)}, bf16[16,1536]{1,0:T(8,128)(2,1)S(1)}, u32[]{:S(2)}, u32[]{:S(2)}) collective-permute-start(bf16[16,1536]{1,0:T(8,128)(2,1)S(1)} %add_convert_fusion.18), channel_id=1, source_target_pairs={{32,44},{33,45},{34,46},{35,47},{36,40},{37,41},{38,42},{39,43},{4... | collective-permute-start | bytes 147464 | tf_op jit(solution)/shard_map/stage1/ppermute | solution.py:118
  98.0 5.7 %collective-permute-start.12 = (bf16[16,1536]{1,0:T(8,128)(2,1)S(1)}, bf16[16,1536]{1,0:T(8,128)(2,1)S(1)}, u32[]{:S(2)}, u32[]{:S(2)}) collective-permute-start(bf16[16,1536]{1,0:T(8,128)(2,1)S(1)} %add_convert_fusion.18), channel_id=1, source_target_pairs={{32,40},{33,41},{34,42},{35,43},{36,44},{37,45},{38,46},{39,47},{4... | collective-permute-start | bytes 147464 | tf_op jit(solution)/shard_map/stage1/ppermute | solution.py:118
  100.7 4.8 %collective-permute-start.11 = (bf16[16,1536]{1,0:T(8,128)(2,1)S(1)}, bf16[16,1536]{1,0:T(8,128)(2,1)S(1)}, u32[]{:S(2)}, u32[]{:S(2)}) collective-permute-start(bf16[16,1536]{1,0:T(8,128)(2,1)S(1)} %add_convert_fusion.18), channel_id=1, source_target_pairs={{32,36},{33,37},{34,38},{35,39},{36,32},{37,33},{38,34},{39,35},{4... | collective-permute-start | bytes 147464 | tf_op jit(solution)/shard_map/stage1/ppermute | solution.py:118
  105.6 2.8 collective-permute-start.15
  106.9 2.5 collective-permute-start.14
  110.7 2.0 collective-permute-start.18
  111.3 1.4 collective-permute-start.17
  112.0 0.7 collective-permute-start.16
  112.8 2.0 collective-permute-start.21
  113.4 1.4 collective-permute-start.20
  114.1 0.7 collective-permute-start.19
  114.8 1.3 collective-permute-start.23
  115.5 0.7 collective-permute-start.22
  117.5 2.0 collective-permute-start.26
  118.2 1.4 collective-permute-start.25
  118.9 0.7 collective-permute-start.24
  119.6 2.0 collective-permute-start.29
  120.3 1.4 collective-permute-start.28
  121.0 0.7 collective-permute-start.27
  121.7 1.3 collective-permute-start.31
  122.4 0.7 collective-permute-start.30
  123.1 351.0 %slice-start = ((s8[4718592]{0:T(1024)(128)(4,1)}), s8[4194304]{0:T(1024)(128)(4,1)S(1)}, s32[]{:S(2)}) async-start(s8[4718592]{0:T(1024)(128)(4,1)} %bitcast.43), calls=%async_computation.1 | async-start | bytes 8388608
  124.4 2.2 collective-permute-start.34
  125.1 1.5 collective-permute-start.33
  125.7 0.9 collective-permute-start.32
  126.7 95.1 %collective-permute-start.37 = (bf16[16,1536]{1,0:T(8,128)(2,1)S(1)}, bf16[16,1536]{1,0:T(8,128)(2,1)S(1)}, u32[]{:S(2)}, u32[]{:S(2)}) collective-permute-start(bf16[16,1536]{1,0:T(8,128)(2,1)S(1)} %add_convert_fusion.9), channel_id=1, source_target_pairs={{128,140},{129,141},{130,142},{131,143},{132,136},{133,137},{134,1... | collective-permute-start | bytes 147464 | tf_op jit(solution)/shard_map/stage4/ppermute | solution.py:118
  195.5 26.3 %collective-permute-start.36 = (bf16[16,1536]{1,0:T(8,128)(2,1)S(1)}, bf16[16,1536]{1,0:T(8,128)(2,1)S(1)}, u32[]{:S(2)}, u32[]{:S(2)}) collective-permute-start(bf16[16,1536]{1,0:T(8,128)(2,1)S(1)} %add_convert_fusion.9), channel_id=1, source_target_pairs={{128,136},{129,137},{130,138},{131,139},{132,140},{133,141},{134,1... | collective-permute-start | bytes 147464 | tf_op jit(solution)/shard_map/stage4/ppermute | solution.py:118
  208.7 13.1 %collective-permute-start.35 = (bf16[16,1536]{1,0:T(8,128)(2,1)S(1)}, bf16[16,1536]{1,0:T(8,128)(2,1)S(1)}, u32[]{:S(2)}, u32[]{:S(2)}) collective-permute-start(bf16[16,1536]{1,0:T(8,128)(2,1)S(1)} %add_convert_fusion.9), channel_id=1, source_target_pairs={{128,132},{129,133},{130,134},{131,135},{132,128},{133,129},{134,1... | collective-permute-start | bytes 147464 | tf_op jit(solution)/shard_map/stage4/ppermute | solution.py:118
  221.8 252.2 %slice-start.1 = ((s8[4718592]{0:T(1024)(128)(4,1)}), s8[524288]{0:T(1024)(128)(4,1)S(1)}, s32[]{:S(2)}) async-start(s8[4718592]{0:T(1024)(128)(4,1)} %bitcast.43), calls=%async_computation.2 | async-start | bytes 1048576
  221.9 252.2 %copy-start.3 = (f32[16,1536]{1,0:T(8,128)S(1)}, f32[16,1536]{1,0:T(8,128)}, u32[]{:S(2)}) copy-start(f32[16,1536]{1,0:T(8,128)} %unpack.1) | copy-start | bytes 294916
  221.9 29.2 %collective-permute-start.39 = (bf16[16,1536]{1,0:T(8,128)(2,1)S(1)}, bf16[16,1536]{1,0:T(8,128)(2,1)S(1)}, u32[]{:S(2)}, u32[]{:S(2)}) collective-permute-start(bf16[16,1536]{1,0:T(8,128)(2,1)S(1)} %add_convert_fusion.8), channel_id=1, source_target_pairs={{128,188},{129,189},{130,190},{131,191},{132,184},{133,185},{134,1... | collective-permute-start | bytes 147464 | tf_op jit(solution)/shard_map/stage4/ppermute | solution.py:118
  238.0 13.1 %collective-permute-start.38 = (bf16[16,1536]{1,0:T(8,128)(2,1)S(1)}, bf16[16,1536]{1,0:T(8,128)(2,1)S(1)}, u32[]{:S(2)}, u32[]{:S(2)}) collective-permute-start(bf16[16,1536]{1,0:T(8,128)(2,1)S(1)} %add_convert_fusion.8), channel_id=1, source_target_pairs={{128,160},{129,161},{130,162},{131,163},{132,164},{133,165},{134,1... | collective-permute-start | bytes 147464 | tf_op jit(solution)/shard_map/stage4/ppermute | solution.py:118
  252.4 39.8 %collective-permute-start.42 = (bf16[16,1536]{1,0:T(8,128)(2,1)S(1)}, bf16[16,1536]{1,0:T(8,128)(2,1)S(1)}, u32[]{:S(2)}, u32[]{:S(2)}) collective-permute-start(bf16[16,1536]{1,0:T(8,128)(2,1)S(1)} %fusion.10), channel_id=1, source_target_pairs={{160,163},{161,162},{162,161},{163,160},{164,167},{165,166},{166,1... | collective-permute-start | bytes 147464 | tf_op jit(solution)/shard_map/stage5/ppermute | solution.py:118
  266.4 25.8 %collective-permute-start.41 = (bf16[16,1536]{1,0:T(8,128)(2,1)S(1)}, bf16[16,1536]{1,0:T(8,128)(2,1)S(1)}, u32[]{:S(2)}, u32[]{:S(2)}) collective-permute-start(bf16[16,1536]{1,0:T(8,128)(2,1)S(1)} %fusion.10), channel_id=1, source_target_pairs={{160,162},{161,163},{162,160},{163,161},{164,166},{165,167},{166,1... | collective-permute-start | bytes 147464 | tf_op jit(solution)/shard_map/stage5/ppermute | solution.py:118
  279.3 12.9 %collective-permute-start.40 = (bf16[16,1536]{1,0:T(8,128)(2,1)S(1)}, bf16[16,1536]{1,0:T(8,128)(2,1)S(1)}, u32[]{:S(2)}, u32[]{:S(2)}) collective-permute-start(bf16[16,1536]{1,0:T(8,128)(2,1)S(1)} %fusion.10), channel_id=1, source_target_pairs={{160,161},{161,160},{162,163},{163,162},{164,165},{165,164},{166,1... | collective-permute-start | bytes 147464 | tf_op jit(solution)/shard_map/stage5/ppermute | solution.py:118
  292.2 41.0 %collective-permute-start.45 = (bf16[16,1536]{1,0:T(8,128)(2,1)S(1)}, bf16[16,1536]{1,0:T(8,128)(2,1)S(1)}, u32[]{:S(2)}, u32[]{:S(2)}) collective-permute-start(bf16[16,1536]{1,0:T(8,128)(2,1)S(1)} %add_convert_fusion.6), channel_id=1, source_target_pairs={{160,172},{161,173},{162,174},{163,175},{164,168},{165,169},{166,1... | collective-permute-start | bytes 147464 | tf_op jit(solution)/shard_map/stage5/ppermute | solution.py:118
  307.5 25.8 %collective-permute-start.44 = (bf16[16,1536]{1,0:T(8,128)(2,1)S(1)}, bf16[16,1536]{1,0:T(8,128)(2,1)S(1)}, u32[]{:S(2)}, u32[]{:S(2)}) collective-permute-start(bf16[16,1536]{1,0:T(8,128)(2,1)S(1)} %add_convert_fusion.6), channel_id=1, source_target_pairs={{160,168},{161,169},{162,170},{163,171},{164,172},{165,173},{166,1... | collective-permute-start | bytes 147464 | tf_op jit(solution)/shard_map/stage5/ppermute | solution.py:118
  320.3 12.9 %collective-permute-start.43 = (bf16[16,1536]{1,0:T(8,128)(2,1)S(1)}, bf16[16,1536]{1,0:T(8,128)(2,1)S(1)}, u32[]{:S(2)}, u32[]{:S(2)}) collective-permute-start(bf16[16,1536]{1,0:T(8,128)(2,1)S(1)} %add_convert_fusion.6), channel_id=1, source_target_pairs={{160,164},{161,165},{162,166},{163,167},{164,160},{165,161},{166,1... | collective-permute-start | bytes 147464 | tf_op jit(solution)/shard_map/stage5/ppermute | solution.py:118
  333.3 27.7 %collective-permute-start.47 = (bf16[16,1536]{1,0:T(8,128)(2,1)S(1)}, bf16[16,1536]{1,0:T(8,128)(2,1)S(1)}, u32[]{:S(2)}, u32[]{:S(2)}) collective-permute-start(bf16[16,1536]{1,0:T(8,128)(2,1)S(1)} %add_convert_fusion.5), channel_id=1, source_target_pairs={{160,220},{161,221},{162,222},{163,223},{164,216},{165,217},{166,2... | collective-permute-start | bytes 147464 | tf_op jit(solution)/shard_map/stage5/ppermute | solution.py:118
  348.1 12.9 %collective-permute-start.46 = (bf16[16,1536]{1,0:T(8,128)(2,1)S(1)}, bf16[16,1536]{1,0:T(8,128)(2,1)S(1)}, u32[]{:S(2)}, u32[]{:S(2)}) collective-permute-start(bf16[16,1536]{1,0:T(8,128)(2,1)S(1)} %add_convert_fusion.5), channel_id=1, source_target_pairs={{160,192},{161,193},{162,194},{163,195},{164,196},{165,197},{166,1... | collective-permute-start | bytes 147464 | tf_op jit(solution)/shard_map/stage5/ppermute | solution.py:118
  362.4 41.0 %collective-permute-start.50 = (bf16[16,1536]{1,0:T(8,128)(2,1)S(1)}, bf16[16,1536]{1,0:T(8,128)(2,1)S(1)}, u32[]{:S(2)}, u32[]{:S(2)}) collective-permute-start(bf16[16,1536]{1,0:T(8,128)(2,1)S(1)} %fusion.11), channel_id=1, source_target_pairs={{192,195},{193,194},{194,193},{195,192},{196,199},{197,198},{198,1... | collective-permute-start | bytes 147464 | tf_op jit(solution)/shard_map/stage6/ppermute | solution.py:118
  377.5 25.8 %collective-permute-start.49 = (bf16[16,1536]{1,0:T(8,128)(2,1)S(1)}, bf16[16,1536]{1,0:T(8,128)(2,1)S(1)}, u32[]{:S(2)}, u32[]{:S(2)}) collective-permute-start(bf16[16,1536]{1,0:T(8,128)(2,1)S(1)} %fusion.11), channel_id=1, source_target_pairs={{192,194},{193,195},{194,192},{195,193},{196,198},{197,199},{198,1... | collective-permute-start | bytes 147464 | tf_op jit(solution)/shard_map/stage6/ppermute | solution.py:118
  390.4 12.9 %collective-permute-start.48 = (bf16[16,1536]{1,0:T(8,128)(2,1)S(1)}, bf16[16,1536]{1,0:T(8,128)(2,1)S(1)}, u32[]{:S(2)}, u32[]{:S(2)}) collective-permute-start(bf16[16,1536]{1,0:T(8,128)(2,1)S(1)} %fusion.11), channel_id=1, source_target_pairs={{192,193},{193,192},{194,195},{195,194},{196,197},{197,196},{198,1... | collective-permute-start | bytes 147464 | tf_op jit(solution)/shard_map/stage6/ppermute | solution.py:118
  403.4 41.9 %collective-permute-start.53 = (bf16[16,1536]{1,0:T(8,128)(2,1)S(1)}, bf16[16,1536]{1,0:T(8,128)(2,1)S(1)}, u32[]{:S(2)}, u32[]{:S(2)}) collective-permute-start(bf16[16,1536]{1,0:T(8,128)(2,1)S(1)} %add_convert_fusion.3), channel_id=1, source_target_pairs={{192,204},{193,205},{194,206},{195,207},{196,200},{197,201},{198,2... | collective-permute-start | bytes 147464 | tf_op jit(solution)/shard_map/stage6/ppermute | solution.py:118
  419.5 25.8 %collective-permute-start.52 = (bf16[16,1536]{1,0:T(8,128)(2,1)S(1)}, bf16[16,1536]{1,0:T(8,128)(2,1)S(1)}, u32[]{:S(2)}, u32[]{:S(2)}) collective-permute-start(bf16[16,1536]{1,0:T(8,128)(2,1)S(1)} %add_convert_fusion.3), channel_id=1, source_target_pairs={{192,200},{193,201},{194,202},{195,203},{196,204},{197,205},{198,2... | collective-permute-start | bytes 147464 | tf_op jit(solution)/shard_map/stage6/ppermute | solution.py:118
  432.4 12.9 %collective-permute-start.51 = (bf16[16,1536]{1,0:T(8,128)(2,1)S(1)}, bf16[16,1536]{1,0:T(8,128)(2,1)S(1)}, u32[]{:S(2)}, u32[]{:S(2)}) collective-permute-start(bf16[16,1536]{1,0:T(8,128)(2,1)S(1)} %add_convert_fusion.3), channel_id=1, source_target_pairs={{192,196},{193,197},{194,198},{195,199},{196,192},{197,193},{198,1... | collective-permute-start | bytes 147464 | tf_op jit(solution)/shard_map/stage6/ppermute | solution.py:118
  445.4 28.7 %collective-permute-start.55 = (bf16[16,1536]{1,0:T(8,128)(2,1)S(1)}, bf16[16,1536]{1,0:T(8,128)(2,1)S(1)}, u32[]{:S(2)}, u32[]{:S(2)}) collective-permute-start(bf16[16,1536]{1,0:T(8,128)(2,1)S(1)} %add_convert_fusion.2), channel_id=1, source_target_pairs={{192,252},{193,253},{194,254},{195,255},{196,248},{197,249},{198,2... | collective-permute-start | bytes 147464 | tf_op jit(solution)/shard_map/stage6/ppermute | solution.py:118
  461.1 12.9 %collective-permute-start.54 = (bf16[16,1536]{1,0:T(8,128)(2,1)S(1)}, bf16[16,1536]{1,0:T(8,128)(2,1)S(1)}, u32[]{:S(2)}, u32[]{:S(2)}) collective-permute-start(bf16[16,1536]{1,0:T(8,128)(2,1)S(1)} %add_convert_fusion.2), channel_id=1, source_target_pairs={{192,224},{193,225},{194,226},{195,227},{196,228},{197,229},{198,2... | collective-permute-start | bytes 147464 | tf_op jit(solution)/shard_map/stage6/ppermute | solution.py:118

commit v2 on v1

--- a/solution.py
+++ b/solution.py
@@ -9,6 +9,7 @@
 BF = jnp.bfloat16
 F32 = jnp.float32
 LANES = 128
+SWITCH = 7
 
 
 def pack_kernel(owner_count, owner_ref, slot_ref, rows_ref, out_ref):
@@ -109,9 +110,10 @@
     def number(s, z, x):
         return (s * z_count + z) * x_count + x
 
-    def exchange(value, layer, mask_x, mask_z, shift=0):
+    def exchange(value, mask_x, mask_z, shift=0, first=0, step=1):
         pairs = [
-            (number(layer, z, x), number(layer + shift, z ^ mask_z, x ^ mask_x))
+            (number(s, z, x), number(s + shift, z ^ mask_z, x ^ mask_x))
+            for s in range(first, sweep_count - shift, step)
             for z in range(z_count)
             for x in range(x_count)
         ]
@@ -123,24 +125,33 @@
             result = result + value.astype(F32)
         return result
 
+    far = z_count - 1
+    own_layer = lax.axis_index("sweep")
+    if SWITCH < sweep_count - 1:
+        with jax.named_scope("whole"):
+            whole = lax.psum(through, ("z", "x"))
     panel = None
-    arrived = []
     for layer in range(sweep_count - 1):
         with jax.named_scope("stage%d" % layer):
-            part = source
-            if panel is not None:
-                part = source - jnp.dot(panel, through, preferred_element_type=F32)
-            part = part.astype(BF)
-            part = total([part] + [exchange(part, layer, m, 0) for m in range(1, x_count)])
-            part = part.astype(BF)
-            part = total([part] + [exchange(part, layer, 0, m) for m in range(1, z_count // 2)])
-            part = part.astype(BF)
-            panel = total(
-                [exchange(part, layer, 0, m, 1) for m in (0, z_count - 1)]
-            ).astype(BF)
-            arrived.append(panel)
+            if layer < SWITCH:
+                part = source
+                if panel is not None:
+                    part = source - jnp.dot(panel, through, preferred_element_type=F32)
+                part = part.astype(BF)
+                part = total([part] + [exchange(part, m, 0) for m in range(1, x_count)])
+                part = part.astype(BF)
+                part = total([part] + [exchange(part, 0, m) for m in range(1, z_count // 2)])
+                part = part.astype(BF)
+                panel = total([exchange(part, 0, m, 1) for m in (0, far)]).astype(BF)
+                if layer == 0:
+                    kept = part
+            else:
+                if layer == SWITCH:
+                    whole_source = total([kept, exchange(kept, 0, far)])
+                following = whole_source - jnp.dot(panel, whole, preferred_element_type=F32)
+                sent = exchange(following.astype(BF), 0, 0, 1, layer % 2, 2)
+                panel = jnp.where(own_layer == layer + 1, sent, panel)
     with jax.named_scope("solve"):
-        panel = total(arrived).astype(BF)
         coupled = jnp.dot(panel, coupling_in, preferred_element_type=F32)
         local = (assembled - coupled).astype(BF).reshape(rhs_count, face_dev, width)
         solved = jnp.einsum("rfw,fwv->rfv", local, inverse, preferred_element_type=F32)

time: 477 us -> 234 us (0.49)
  starting transfers between devices: 396 us -> 132 us
  waiting for transfers between devices: 41.3 us -> 64.1 us
    ppermute x56, starting transfers between devices: 385 us -> 120 us  [exchange(): return lax.ppermute(value, ('sweep', 'z', 'x'), pairs)]
    ppermute x56, waiting for transfers between devices: 21.7 us -> 44.5 us  [exchange(): return lax.ppermute(value, ('sweep', 'z', 'x'), pairs)]
  transfers between devices with their start and end apart: 57 -> 57, of which waited for: 8 -> 36; matrix products, arithmetic and copies ran while one was open for 3% -> 7% of each run, Pallas kernels for 0% -> 0%
where the time goes in v2:
time: 234 us; the launch traced here: 233 us
  starting transfers between devices  132 us (56%)
  waiting for transfers between devices  64.1 us (27%)
  matrix products  28.5 us (12%)
  Pallas kernels  5.46 us (2%)
    ppermute x56, starting transfers between devices, exchange(): return lax.ppermute(value, ('sweep', 'z', 'x'), pairs)  120 us
    ppermute x56, waiting for transfers between devices, exchange(): return lax.ppermute(value, ('sweep', 'z', 'x'), pairs)  44.5 us
    all_to_all x1, waiting for transfers between devices, on_device(): lax.all_to_all(packed.reshape(group_size, capacity, width + LANES), ('z',...  19.6 us
    all_to_all x1, starting transfers between devices, on_device(): lax.all_to_all(packed.reshape(group_size, capacity, width + LANES), ('z',...  11.9 us
    dot_general x1, matrix products, on_device(): jnp.dot(coupling_in, outward, preferred_element_type=F32).astype(BF)  9.5 us
    dot_general x6, matrix products, on_device(): part = source - jnp.dot(panel, through, preferred_element_type=F32)  7.89 us
    dot_general x1, matrix products, on_device(): jnp.einsum('fwv,fvp->fwp', inverse, coupling_out.reshape(face_dev, width,...  6.57 us
  transfers between devices with their start and end apart: 57, of which 36 were waited for; matrix products, arithmetic and copies ran while one was open for 7% of the time, Pallas kernels for 0%

profile of v2, /device:TPU:1, one launch (start us, length us, event | category | flops | bytes accessed | tf_op | source)
XLA Modules:
  0.0 233.2 jit_solution(5321954155344199535)
XLA Ops:
  0.0 3.3 %pack.1 = bf16[1024,512]{1,0:T(8,128)(2,1)} custom-call(s32[1,512]{1,0:T(1,128)} %bitcast.49, s32[1,512]{1,0:T(1,128)} %bitcast.50, f32[512,384]{1,0:T(8,128)} %refs_2_.1), custom_call_target="tpu_custom_call" | custom-call | tf_op jit(solution)/shard_map/pack/pack/pallas_call | solution.py:74
  3.3 11.9 %all-to-all-start = ((bf16[32,32,512]{2,1,0:T(8,128)(2,1)}), bf16[32,32,512]{2,1,0:T(8,128)(2,1)S(1)}, u32[]{:S(2)}, u32[]{:S(2)}) async-start(bf16[32,32,512]{2,1,0:T(8,128)(2,1)} %bitcast.45), calls=%async_computation | async-start | bytes 2097152 | tf_op jit(solution)/shard_map/route/all_to_all | solution.py:80
  15.2 6.6 %convolution_convert_fusion.1 = bf16[4,384,1536]{2,1,0:T(8,128)(2,1)} fusion(bf16[4,384,1536]{2,1,0:T(8,128)(2,1)} %bitcast.42, bf16[1,4,384,384]{3,2,1,0:T(8,128)(2,1)S(1)} %copy-done), kind=kOutput, calls=%fused_computation.4 | convolution fusion | flops 1814298624 | bytes 10616832 | tf_op jit(solution)/shard_map/fold/fwv,fvp->fwp/dot_general | solution.py:88
  21.7 19.6 %all-to-all-done = bf16[32,32,512]{2,1,0:T(8,128)(2,1)S(1)} async-done(((bf16[32,32,512]{2,1,0:T(8,128)(2,1)}), bf16[32,32,512]{2,1,0:T(8,128)(2,1)S(1)}, u32[]{:S(2)}, u32[]{:S(2)}) %all-to-all-start) | async-done | bytes 1048608 | tf_op jit(solution)/shard_map/route/all_to_all | solution.py:80
  42.3 2.2 unpack.1
  45.6 3.5 %fusion.21 = f32[32,1536]{1,0:T(8,128)S(1)} fusion(bf16[1536,1536]{1,0:T(8,128)(2,1)} %bitcast.40, bf16[16,1536]{1,0:T(8,128)(2,1)S(1)} %get-tuple-element.7, bf16[16,1536]{1,0:T(8,128)(2,1)S(1)} %get-tuple-element.8), kind=kOutput, calls=%fused_computation.24 | convolution fusion | flops 151191552 | bytes 5013504 | tf_op jit(solution)/shard_map/source/dot_general | solution.py:105
  49.2 3.3 %collective-permute-start.2 = (bf16[16,1536]{1,0:T(8,128)(2,1)S(1)}, bf16[16,1536]{1,0:T(8,128)(2,1)S(1)}, u32[]{:S(2)}, u32[]{:S(2)}) collective-permute-start(bf16[16,1536]{1,0:T(8,128)(2,1)S(1)} %get-tuple-element.5), channel_id=1, source_target_pairs={{0,3},{1,2},{2,1},{3,0},{4,7},{5,6},{6,5},{7,4},{8,11},{9,10},{10,... | collective-permute-start | bytes 147464 | tf_op jit(solution)/shard_map/stage0/ppermute | solution.py:120
  54.0 3.1 %collective-permute-done.1 = bf16[16,1536]{1,0:T(8,128)(2,1)S(1)} collective-permute-done((bf16[16,1536]{1,0:T(8,128)(2,1)S(1)}, bf16[16,1536]{1,0:T(8,128)(2,1)S(1)}, u32[]{:S(2)}, u32[]{:S(2)}) %collective-permute-start.1) | collective-permute-done | bytes 49184 | tf_op jit(solution)/shard_map/stage0/ppermute | solution.py:120
  57.7 1.5 collective-permute-start.4
  59.2 1.5 collective-permute-start.3
  60.7 1.3 collective-permute-done.5
  62.7 7.9 %collective-permute-start.7 = (bf16[16,1536]{1,0:T(8,128)(2,1)S(1)}, bf16[16,1536]{1,0:T(8,128)(2,1)S(1)}, u32[]{:S(2)}, u32[]{:S(2)}) collective-permute-start(bf16[16,1536]{1,0:T(8,128)(2,1)S(1)} %add_convert_fusion.19), channel_id=1, source_target_pairs={{0,60},{1,61},{2,62},{3,63},{4,56},{5,57},{6,58},{7,59},{8,52},{9,... | collective-permute-start | bytes 147464 | tf_op jit(solution)/shard_map/stage0/ppermute | solution.py:120
  70.5 1.9 collective-permute-start.6
  72.5 9.5 %convolution_convert_fusion = bf16[1536,1536]{1,0:T(8,128)(2,1)S(1)} fusion(bf16[1536,1536]{1,0:T(8,128)(2,1)S(1)} %bitcast.41, bf16[1,1536,1536]{2,1,0:T(8,128)(2,1)} %param.12), kind=kOutput, calls=%fused_computation | convolution fusion | flops 7250116608 | bytes 14155776 | tf_op jit(solution)/shard_map/fold/dot_general | solution.py:95
  82.0 1.3 fusion.6
  83.3 1.5 collective-permute-start.10
  87.5 1.8 collective-permute-done.9
  89.3 2.0 collective-permute-start.13
  92.9 1.2 collective-permute-done.13
  95.5 9.2 %collective-permute-start.15 = (bf16[16,1536]{1,0:T(8,128)(2,1)S(1)}, bf16[16,1536]{1,0:T(8,128)(2,1)S(1)}, u32[]{:S(2)}, u32[]{:S(2)}) collective-permute-start(bf16[16,1536]{1,0:T(8,128)(2,1)S(1)} %add_convert_fusion.16), channel_id=1, source_target_pairs={{0,60},{1,61},{2,62},{3,63},{4,56},{5,57},{6,58},{7,59},{8,52},{9,... | collective-permute-start | bytes 147464 | tf_op jit(solution)/shard_map/stage1/ppermute | solution.py:120
  104.7 1.9 collective-permute-start.14
  106.7 1.2 collective-permute-done.14
  107.9 1.3 fusion.7
  109.2 1.4 collective-permute-start.18
  113.4 1.6 collective-permute-done.17
  116.0 1.5 collective-permute-start.20
  117.4 1.2 collective-permute-start.19
  118.7 1.3 collective-permute-done.21
  120.0 1.2 collective-permute-done.20
  121.2 7.6 %collective-permute-start.23 = (bf16[16,1536]{1,0:T(8,128)(2,1)S(1)}, bf16[16,1536]{1,0:T(8,128)(2,1)S(1)}, u32[]{:S(2)}, u32[]{:S(2)}) collective-permute-start(bf16[16,1536]{1,0:T(8,128)(2,1)S(1)} %add_convert_fusion.13), channel_id=1, source_target_pairs={{0,60},{1,61},{2,62},{3,63},{4,56},{5,57},{6,58},{7,59},{8,52},{9,... | collective-permute-start | bytes 147464 | tf_op jit(solution)/shard_map/stage2/ppermute | solution.py:120
  128.8 1.9 collective-permute-start.22
  132.0 1.3 fusion.8
  133.3 1.3 collective-permute-start.26
  137.5 1.6 collective-permute-done.25
  139.1 2.2 collective-permute-start.29
  142.7 1.2 collective-permute-done.29
  144.0 2.3 %collective-permute-done.28 = bf16[16,1536]{1,0:T(8,128)(2,1)S(1)} collective-permute-done((bf16[16,1536]{1,0:T(8,128)(2,1)S(1)}, bf16[16,1536]{1,0:T(8,128)(2,1)S(1)}, u32[]{:S(2)}, u32[]{:S(2)}) %collective-permute-start.28) | collective-permute-done | bytes 49184 | tf_op jit(solution)/shard_map/stage3/ppermute | solution.py:120
  146.3 7.9 %collective-permute-start.31 = (bf16[16,1536]{1,0:T(8,128)(2,1)S(1)}, bf16[16,1536]{1,0:T(8,128)(2,1)S(1)}, u32[]{:S(2)}, u32[]{:S(2)}) collective-permute-start(bf16[16,1536]{1,0:T(8,128)(2,1)S(1)} %add_convert_fusion.10), channel_id=1, source_target_pairs={{0,60},{1,61},{2,62},{3,63},{4,56},{5,57},{6,58},{7,59},{8,52},{9,... | collective-permute-start | bytes 147464 | tf_op jit(solution)/shard_map/stage3/ppermute | solution.py:120
  154.3 1.9 collective-permute-start.30
  157.4 1.3 fusion.9
  158.7 1.4 collective-permute-start.34
  162.9 1.6 collective-permute-done.33
  165.5 1.5 collective-permute-start.36
  167.0 1.3 collective-permute-start.35
  168.2 1.3 collective-permute-done.37
  170.6 8.1 %collective-permute-start.39 = (bf16[16,1536]{1,0:T(8,128)(2,1)S(1)}, bf16[16,1536]{1,0:T(8,128)(2,1)S(1)}, u32[]{:S(2)}, u32[]{:S(2)}) collective-permute-start(bf16[16,1536]{1,0:T(8,128)(2,1)S(1)} %add_convert_fusion.7), channel_id=1, source_target_pairs={{0,60},{1,61},{2,62},{3,63},{4,56},{5,57},{6,58},{7,59},{8,52},{9,... | collective-permute-start | bytes 147464 | tf_op jit(solution)/shard_map/stage4/ppermute | solution.py:120
  178.6 1.9 collective-permute-start.38
  181.8 1.3 fusion.10
  183.1 1.4 collective-permute-start.42
  187.3 1.6 collective-permute-done.41
  188.9 2.0 collective-permute-start.45
  192.6 1.3 collective-permute-done.45
  193.9 1.5 collective-permute-done.44
  195.4 8.7 %collective-permute-start.47 = (bf16[16,1536]{1,0:T(8,128)(2,1)S(1)}, bf16[16,1536]{1,0:T(8,128)(2,1)S(1)}, u32[]{:S(2)}, u32[]{:S(2)}) collective-permute-start(bf16[16,1536]{1,0:T(8,128)(2,1)S(1)} %add_convert_fusion.4), channel_id=1, source_target_pairs={{0,60},{1,61},{2,62},{3,63},{4,56},{5,57},{6,58},{7,59},{8,52},{9,... | collective-permute-start | bytes 147464 | tf_op jit(solution)/shard_map/stage5/ppermute | solution.py:120
  204.1 1.9 collective-permute-start.46
  206.0 1.2 collective-permute-done.46
  207.2 1.3 fusion.11
  208.5 1.4 collective-permute-start.50
  212.7 1.6 collective-permute-done.49
  215.4 1.9 collective-permute-start.52
  218.0 1.3 collective-permute-done.53
  219.3 1.3 collective-permute-done.52
  220.6 7.8 %collective-permute-start.55 = (bf16[16,1536]{1,0:T(8,128)(2,1)S(1)}, bf16[16,1536]{1,0:T(8,128)(2,1)S(1)}, u32[]{:S(2)}, u32[]{:S(2)}) collective-permute-start(bf16[16,1536]{1,0:T(8,128)(2,1)S(1)} %add_convert_fusion.1), channel_id=1, source_target_pairs={{0,60},{1,61},{2,62},{3,63},{4,56},{5,57},{6,58},{7,59},{8,52},{9,... | collective-permute-start | bytes 147464 | tf_op jit(solution)/shard_map/stage6/ppermute | solution.py:120
  228.4 1.9 collective-permute-start.54
  (93 shorter events, 39.2 us)
Async XLA Ops:
  0.0 15.1 %copy-start = (bf16[1,4,384,384]{3,2,1,0:T(8,128)(2,1)S(1)}, bf16[1,4,384,384]{3,2,1,0:T(8,128)(2,1)}, u32[]{:S(2)}) copy-start(bf16[1,4,384,384]{3,2,1,0:T(8,128)(2,1)} %param.11) | copy-start | bytes 3538948
  3.3 38.1 %all-to-all-start = ((bf16[32,32,512]{2,1,0:T(8,128)(2,1)}), bf16[32,32,512]{2,1,0:T(8,128)(2,1)S(1)}, u32[]{:S(2)}, u32[]{:S(2)}) async-start(bf16[32,32,512]{2,1,0:T(8,128)(2,1)} %bitcast.45), calls=%async_computation | async-start | bytes 2097152 | tf_op jit(solution)/shard_map/route/all_to_all | solution.py:80
  41.3 1.0 copy-start.2
  44.5 27.9 %copy-start.1 = (bf16[4,384,1536]{2,1,0:T(8,128)(2,1)S(1)}, bf16[4,384,1536]{2,1,0:T(8,128)(2,1)}, u32[]{:S(2)}) copy-start(bf16[4,384,1536]{2,1,0:T(8,128)(2,1)} %convolution_convert_fusion.1) | copy-start | bytes 14155780
  49.2 4.8 %collective-permute-start.2 = (bf16[16,1536]{1,0:T(8,128)(2,1)S(1)}, bf16[16,1536]{1,0:T(8,128)(2,1)S(1)}, u32[]{:S(2)}, u32[]{:S(2)}) collective-permute-start(bf16[16,1536]{1,0:T(8,128)(2,1)S(1)} %get-tuple-element.5), channel_id=1, source_target_pairs={{0,3},{1,2},{2,1},{3,0},{4,7},{5,6},{6,5},{7,4},{8,11},{9,10},{10,... | collective-permute-start | bytes 147464 | tf_op jit(solution)/shard_map/stage0/ppermute | solution.py:120
  52.5 4.6 %collective-permute-start.1 = (bf16[16,1536]{1,0:T(8,128)(2,1)S(1)}, bf16[16,1536]{1,0:T(8,128)(2,1)S(1)}, u32[]{:S(2)}, u32[]{:S(2)}) collective-permute-start(bf16[16,1536]{1,0:T(8,128)(2,1)S(1)} %get-tuple-element.5), channel_id=1, source_target_pairs={{0,2},{1,3},{2,0},{3,1},{4,6},{5,7},{6,4},{7,5},{8,10},{9,11},{10,... | collective-permute-start | bytes 147464 | tf_op jit(solution)/shard_map/stage0/ppermute | solution.py:120
  52.8 4.2 %collective-permute-start = (bf16[16,1536]{1,0:T(8,128)(2,1)S(1)}, bf16[16,1536]{1,0:T(8,128)(2,1)S(1)}, u32[]{:S(2)}, u32[]{:S(2)}) collective-permute-start(bf16[16,1536]{1,0:T(8,128)(2,1)S(1)} %get-tuple-element.5), channel_id=1, source_target_pairs={{0,1},{1,0},{2,3},{3,2},{4,5},{5,4},{6,7},{7,6},{8,9},{9,8},{10,11... | collective-permute-start | bytes 147464 | tf_op jit(solution)/shard_map/stage0/ppermute | solution.py:120
  57.1 5.0 %collective-permute-start.5 = (bf16[16,1536]{1,0:T(8,128)(2,1)S(1)}, bf16[16,1536]{1,0:T(8,128)(2,1)S(1)}, u32[]{:S(2)}, u32[]{:S(2)}) collective-permute-start(bf16[16,1536]{1,0:T(8,128)(2,1)S(1)} %add_convert_fusion.20), channel_id=1, source_target_pairs={{0,12},{1,13},{2,14},{3,15},{4,8},{5,9},{6,10},{7,11},{8,4},{9,5},... | collective-permute-start | bytes 147464 | tf_op jit(solution)/shard_map/stage0/ppermute | solution.py:120
  57.7 4.9 %collective-permute-start.4 = (bf16[16,1536]{1,0:T(8,128)(2,1)S(1)}, bf16[16,1536]{1,0:T(8,128)(2,1)S(1)}, u32[]{:S(2)}, u32[]{:S(2)}) collective-permute-start(bf16[16,1536]{1,0:T(8,128)(2,1)S(1)} %add_convert_fusion.20), channel_id=1, source_target_pairs={{0,8},{1,9},{2,10},{3,11},{4,12},{5,13},{6,14},{7,15},{8,0},{9,1},... | collective-permute-start | bytes 147464 | tf_op jit(solution)/shard_map/stage0/ppermute | solution.py:120
  59.2 3.4 %collective-permute-start.3 = (bf16[16,1536]{1,0:T(8,128)(2,1)S(1)}, bf16[16,1536]{1,0:T(8,128)(2,1)S(1)}, u32[]{:S(2)}, u32[]{:S(2)}) collective-permute-start(bf16[16,1536]{1,0:T(8,128)(2,1)S(1)} %add_convert_fusion.20), channel_id=1, source_target_pairs={{0,4},{1,5},{2,6},{3,7},{4,0},{5,1},{6,2},{7,3},{8,12},{9,13},{10,... | collective-permute-start | bytes 147464 | tf_op jit(solution)/shard_map/stage0/ppermute | solution.py:120
  62.7 19.3 %collective-permute-start.7 = (bf16[16,1536]{1,0:T(8,128)(2,1)S(1)}, bf16[16,1536]{1,0:T(8,128)(2,1)S(1)}, u32[]{:S(2)}, u32[]{:S(2)}) collective-permute-start(bf16[16,1536]{1,0:T(8,128)(2,1)S(1)} %add_convert_fusion.19), channel_id=1, source_target_pairs={{0,60},{1,61},{2,62},{3,63},{4,56},{5,57},{6,58},{7,59},{8,52},{9,... | collective-permute-start | bytes 147464 | tf_op jit(solution)/shard_map/stage0/ppermute | solution.py:120
  70.5 11.5 %collective-permute-start.6 = (bf16[16,1536]{1,0:T(8,128)(2,1)S(1)}, bf16[16,1536]{1,0:T(8,128)(2,1)S(1)}, u32[]{:S(2)}, u32[]{:S(2)}) collective-permute-start(bf16[16,1536]{1,0:T(8,128)(2,1)S(1)} %add_convert_fusion.19), channel_id=1, source_target_pairs={{0,32},{1,33},{2,34},{3,35},{4,36},{5,37},{6,38},{7,39},{8,40},{9,... | collective-permute-start | bytes 147464 | tf_op jit(solution)/shard_map/stage0/ppermute | solution.py:120
  83.3 4.2 %collective-permute-start.10 = (bf16[16,1536]{1,0:T(8,128)(2,1)S(1)}, bf16[16,1536]{1,0:T(8,128)(2,1)S(1)}, u32[]{:S(2)}, u32[]{:S(2)}) collective-permute-start(bf16[16,1536]{1,0:T(8,128)(2,1)S(1)} %fusion.6), channel_id=1, source_target_pairs={{0,3},{1,2},{2,1},{3,0},{4,7},{5,6},{6,5},{7,4},{8,11},{9,10},{10,... | collective-permute-start | bytes 147464 | tf_op jit(solution)/shard_map/stage1/ppermute | solution.py:120
  84.8 4.4 %collective-permute-start.9 = (bf16[16,1536]{1,0:T(8,128)(2,1)S(1)}, bf16[16,1536]{1,0:T(8,128)(2,1)S(1)}, u32[]{:S(2)}, u32[]{:S(2)}) collective-permute-start(bf16[16,1536]{1,0:T(8,128)(2,1)S(1)} %fusion.6), channel_id=1, source_target_pairs={{0,2},{1,3},{2,0},{3,1},{4,6},{5,7},{6,4},{7,5},{8,10},{9,11},{10,... | collective-permute-start | bytes 147464 | tf_op jit(solution)/shard_map/stage1/ppermute | solution.py:120
  85.6 3.6 %collective-permute-start.8 = (bf16[16,1536]{1,0:T(8,128)(2,1)S(1)}, bf16[16,1536]{1,0:T(8,128)(2,1)S(1)}, u32[]{:S(2)}, u32[]{:S(2)}) collective-permute-start(bf16[16,1536]{1,0:T(8,128)(2,1)S(1)} %fusion.6), channel_id=1, source_target_pairs={{0,1},{1,0},{2,3},{3,2},{4,5},{5,4},{6,7},{7,6},{8,9},{9,8},{10,11... | collective-permute-start | bytes 147464 | tf_op jit(solution)/shard_map/stage1/ppermute | solution.py:120
  89.3 4.8 %collective-permute-start.13 = (bf16[16,1536]{1,0:T(8,128)(2,1)S(1)}, bf16[16,1536]{1,0:T(8,128)(2,1)S(1)}, u32[]{:S(2)}, u32[]{:S(2)}) collective-permute-start(bf16[16,1536]{1,0:T(8,128)(2,1)S(1)} %add_convert_fusion.17), channel_id=1, source_target_pairs={{0,12},{1,13},{2,14},{3,15},{4,8},{5,9},{6,10},{7,11},{8,4},{9,5},... | collective-permute-start | bytes 147464 | tf_op jit(solution)/shard_map/stage1/ppermute | solution.py:120
  91.3 3.9 %collective-permute-start.12 = (bf16[16,1536]{1,0:T(8,128)(2,1)S(1)}, bf16[16,1536]{1,0:T(8,128)(2,1)S(1)}, u32[]{:S(2)}, u32[]{:S(2)}) collective-permute-start(bf16[16,1536]{1,0:T(8,128)(2,1)S(1)} %add_convert_fusion.17), channel_id=1, source_target_pairs={{0,8},{1,9},{2,10},{3,11},{4,12},{5,13},{6,14},{7,15},{8,0},{9,1},... | collective-permute-start | bytes 147464 | tf_op jit(solution)/shard_map/stage1/ppermute | solution.py:120
  92.0 3.5 %collective-permute-start.11 = (bf16[16,1536]{1,0:T(8,128)(2,1)S(1)}, bf16[16,1536]{1,0:T(8,128)(2,1)S(1)}, u32[]{:S(2)}, u32[]{:S(2)}) collective-permute-start(bf16[16,1536]{1,0:T(8,128)(2,1)S(1)} %add_convert_fusion.17), channel_id=1, source_target_pairs={{0,4},{1,5},{2,6},{3,7},{4,0},{5,1},{6,2},{7,3},{8,12},{9,13},{10,... | collective-permute-start | bytes 147464 | tf_op jit(solution)/shard_map/stage1/ppermute | solution.py:120
  95.5 11.2 %collective-permute-start.15 = (bf16[16,1536]{1,0:T(8,128)(2,1)S(1)}, bf16[16,1536]{1,0:T(8,128)(2,1)S(1)}, u32[]{:S(2)}, u32[]{:S(2)}) collective-permute-start(bf16[16,1536]{1,0:T(8,128)(2,1)S(1)} %add_convert_fusion.16), channel_id=1, source_target_pairs={{0,60},{1,61},{2,62},{3,63},{4,56},{5,57},{6,58},{7,59},{8,52},{9,... | collective-permute-start | bytes 147464 | tf_op jit(solution)/shard_map/stage1/ppermute | solution.py:120
  104.7 3.1 %collective-permute-start.14 = (bf16[16,1536]{1,0:T(8,128)(2,1)S(1)}, bf16[16,1536]{1,0:T(8,128)(2,1)S(1)}, u32[]{:S(2)}, u32[]{:S(2)}) collective-permute-start(bf16[16,1536]{1,0:T(8,128)(2,1)S(1)} %add_convert_fusion.16), channel_id=1, source_target_pairs={{0,32},{1,33},{2,34},{3,35},{4,36},{5,37},{6,38},{7,39},{8,40},{9,... | collective-permute-start | bytes 147464 | tf_op jit(solution)/shard_map/stage1/ppermute | solution.py:120
  109.2 4.2 %collective-permute-start.18 = (bf16[16,1536]{1,0:T(8,128)(2,1)S(1)}, bf16[16,1536]{1,0:T(8,128)(2,1)S(1)}, u32[]{:S(2)}, u32[]{:S(2)}) collective-permute-start(bf16[16,1536]{1,0:T(8,128)(2,1)S(1)} %fusion.7), channel_id=1, source_target_pairs={{0,3},{1,2},{2,1},{3,0},{4,7},{5,6},{6,5},{7,4},{8,11},{9,10},{10,... | collective-permute-start | bytes 147464 | tf_op jit(solution)/shard_map/stage2/ppermute | solution.py:120
  110.5 4.4 %collective-permute-start.17 = (bf16[16,1536]{1,0:T(8,128)(2,1)S(1)}, bf16[16,1536]{1,0:T(8,128)(2,1)S(1)}, u32[]{:S(2)}, u32[]{:S(2)}) collective-permute-start(bf16[16,1536]{1,0:T(8,128)(2,1)S(1)} %fusion.7), channel_id=1, source_target_pairs={{0,2},{1,3},{2,0},{3,1},{4,6},{5,7},{6,4},{7,5},{8,10},{9,11},{10,... | collective-permute-start | bytes 147464 | tf_op jit(solution)/shard_map/stage2/ppermute | solution.py:120
  111.7 3.3 %collective-permute-start.16 = (bf16[16,1536]{1,0:T(8,128)(2,1)S(1)}, bf16[16,1536]{1,0:T(8,128)(2,1)S(1)}, u32[]{:S(2)}, u32[]{:S(2)}) collective-permute-start(bf16[16,1536]{1,0:T(8,128)(2,1)S(1)} %fusion.7), channel_id=1, source_target_pairs={{0,1},{1,0},{2,3},{3,2},{4,5},{5,4},{6,7},{7,6},{8,9},{9,8},{10,11... | collective-permute-start | bytes 147464 | tf_op jit(solution)/shard_map/stage2/ppermute | solution.py:120
  115.0 4.9 %collective-permute-start.21 = (bf16[16,1536]{1,0:T(8,128)(2,1)S(1)}, bf16[16,1536]{1,0:T(8,128)(2,1)S(1)}, u32[]{:S(2)}, u32[]{:S(2)}) collective-permute-start(bf16[16,1536]{1,0:T(8,128)(2,1)S(1)} %add_convert_fusion.14), channel_id=1, source_target_pairs={{0,12},{1,13},{2,14},{3,15},{4,8},{5,9},{6,10},{7,11},{8,4},{9,5},... | collective-permute-start | bytes 147464 | tf_op jit(solution)/shard_map/stage2/ppermute | solution.py:120
  116.0 5.2 %collective-permute-start.20 = (bf16[16,1536]{1,0:T(8,128)(2,1)S(1)}, bf16[16,1536]{1,0:T(8,128)(2,1)S(1)}, u32[]{:S(2)}, u32[]{:S(2)}) collective-permute-start(bf16[16,1536]{1,0:T(8,128)(2,1)S(1)} %add_convert_fusion.14), channel_id=1, source_target_pairs={{0,8},{1,9},{2,10},{3,11},{4,12},{5,13},{6,14},{7,15},{8,0},{9,1},... | collective-permute-start | bytes 147464 | tf_op jit(solution)/shard_map/stage2/ppermute | solution.py:120
  117.4 3.7 %collective-permute-start.19 = (bf16[16,1536]{1,0:T(8,128)(2,1)S(1)}, bf16[16,1536]{1,0:T(8,128)(2,1)S(1)}, u32[]{:S(2)}, u32[]{:S(2)}) collective-permute-start(bf16[16,1536]{1,0:T(8,128)(2,1)S(1)} %add_convert_fusion.14), channel_id=1, source_target_pairs={{0,4},{1,5},{2,6},{3,7},{4,0},{5,1},{6,2},{7,3},{8,12},{9,13},{10,... | collective-permute-start | bytes 147464 | tf_op jit(solution)/shard_map/stage2/ppermute | solution.py:120
  121.2 9.6 %collective-permute-start.23 = (bf16[16,1536]{1,0:T(8,128)(2,1)S(1)}, bf16[16,1536]{1,0:T(8,128)(2,1)S(1)}, u32[]{:S(2)}, u32[]{:S(2)}) collective-permute-start(bf16[16,1536]{1,0:T(8,128)(2,1)S(1)} %add_convert_fusion.13), channel_id=1, source_target_pairs={{0,60},{1,61},{2,62},{3,63},{4,56},{5,57},{6,58},{7,59},{8,52},{9,... | collective-permute-start | bytes 147464 | tf_op jit(solution)/shard_map/stage2/ppermute | solution.py:120
  128.8 3.1 %collective-permute-start.22 = (bf16[16,1536]{1,0:T(8,128)(2,1)S(1)}, bf16[16,1536]{1,0:T(8,128)(2,1)S(1)}, u32[]{:S(2)}, u32[]{:S(2)}) collective-permute-start(bf16[16,1536]{1,0:T(8,128)(2,1)S(1)} %add_convert_fusion.13), channel_id=1, source_target_pairs={{0,32},{1,33},{2,34},{3,35},{4,36},{5,37},{6,38},{7,39},{8,40},{9,... | collective-permute-start | bytes 147464 | tf_op jit(solution)/shard_map/stage2/ppermute | solution.py:120
  133.3 4.2 %collective-permute-start.26 = (bf16[16,1536]{1,0:T(8,128)(2,1)S(1)}, bf16[16,1536]{1,0:T(8,128)(2,1)S(1)}, u32[]{:S(2)}, u32[]{:S(2)}) collective-permute-start(bf16[16,1536]{1,0:T(8,128)(2,1)S(1)} %fusion.8), channel_id=1, source_target_pairs={{0,3},{1,2},{2,1},{3,0},{4,7},{5,6},{6,5},{7,4},{8,11},{9,10},{10,... | collective-permute-start | bytes 147464 | tf_op jit(solution)/shard_map/stage3/ppermute | solution.py:120
  134.6 4.4 %collective-permute-start.25 = (bf16[16,1536]{1,0:T(8,128)(2,1)S(1)}, bf16[16,1536]{1,0:T(8,128)(2,1)S(1)}, u32[]{:S(2)}, u32[]{:S(2)}) collective-permute-start(bf16[16,1536]{1,0:T(8,128)(2,1)S(1)} %fusion.8), channel_id=1, source_target_pairs={{0,2},{1,3},{2,0},{3,1},{4,6},{5,7},{6,4},{7,5},{8,10},{9,11},{10,... | collective-permute-start | bytes 147464 | tf_op jit(solution)/shard_map/stage3/ppermute | solution.py:120
  135.8 3.3 %collective-permute-start.24 = (bf16[16,1536]{1,0:T(8,128)(2,1)S(1)}, bf16[16,1536]{1,0:T(8,128)(2,1)S(1)}, u32[]{:S(2)}, u32[]{:S(2)}) collective-permute-start(bf16[16,1536]{1,0:T(8,128)(2,1)S(1)} %fusion.8), channel_id=1, source_target_pairs={{0,1},{1,0},{2,3},{3,2},{4,5},{5,4},{6,7},{7,6},{8,9},{9,8},{10,11... | collective-permute-start | bytes 147464 | tf_op jit(solution)/shard_map/stage3/ppermute | solution.py:120
  139.1 4.9 %collective-permute-start.29 = (bf16[16,1536]{1,0:T(8,128)(2,1)S(1)}, bf16[16,1536]{1,0:T(8,128)(2,1)S(1)}, u32[]{:S(2)}, u32[]{:S(2)}) collective-permute-start(bf16[16,1536]{1,0:T(8,128)(2,1)S(1)} %add_convert_fusion.11), channel_id=1, source_target_pairs={{0,12},{1,13},{2,14},{3,15},{4,8},{5,9},{6,10},{7,11},{8,4},{9,5},... | collective-permute-start | bytes 147464 | tf_op jit(solution)/shard_map/stage3/ppermute | solution.py:120
  141.3 5.0 %collective-permute-start.28 = (bf16[16,1536]{1,0:T(8,128)(2,1)S(1)}, bf16[16,1536]{1,0:T(8,128)(2,1)S(1)}, u32[]{:S(2)}, u32[]{:S(2)}) collective-permute-start(bf16[16,1536]{1,0:T(8,128)(2,1)S(1)} %add_convert_fusion.11), channel_id=1, source_target_pairs={{0,8},{1,9},{2,10},{3,11},{4,12},{5,13},{6,14},{7,15},{8,0},{9,1},... | collective-permute-start | bytes 147464 | tf_op jit(solution)/shard_map/stage3/ppermute | solution.py:120
  142.0 4.3 %collective-permute-start.27 = (bf16[16,1536]{1,0:T(8,128)(2,1)S(1)}, bf16[16,1536]{1,0:T(8,128)(2,1)S(1)}, u32[]{:S(2)}, u32[]{:S(2)}) collective-permute-start(bf16[16,1536]{1,0:T(8,128)(2,1)S(1)} %add_convert_fusion.11), channel_id=1, source_target_pairs={{0,4},{1,5},{2,6},{3,7},{4,0},{5,1},{6,2},{7,3},{8,12},{9,13},{10,... | collective-permute-start | bytes 147464 | tf_op jit(solution)/shard_map/stage3/ppermute | solution.py:120
  146.3 9.9 %collective-permute-start.31 = (bf16[16,1536]{1,0:T(8,128)(2,1)S(1)}, bf16[16,1536]{1,0:T(8,128)(2,1)S(1)}, u32[]{:S(2)}, u32[]{:S(2)}) collective-permute-start(bf16[16,1536]{1,0:T(8,128)(2,1)S(1)} %add_convert_fusion.10), channel_id=1, source_target_pairs={{0,60},{1,61},{2,62},{3,63},{4,56},{5,57},{6,58},{7,59},{8,52},{9,... | collective-permute-start | bytes 147464 | tf_op jit(solution)/shard_map/stage3/ppermute | solution.py:120
  154.3 3.1 %collective-permute-start.30 = (bf16[16,1536]{1,0:T(8,128)(2,1)S(1)}, bf16[16,1536]{1,0:T(8,128)(2,1)S(1)}, u32[]{:S(2)}, u32[]{:S(2)}) collective-permute-start(bf16[16,1536]{1,0:T(8,128)(2,1)S(1)} %add_convert_fusion.10), channel_id=1, source_target_pairs={{0,32},{1,33},{2,34},{3,35},{4,36},{5,37},{6,38},{7,39},{8,40},{9,... | collective-permute-start | bytes 147464 | tf_op jit(solution)/shard_map/stage3/ppermute | solution.py:120
  157.4 74.1 %slice-start = ((s8[4718592]{0:T(1024)(128)(4,1)}), s8[4194304]{0:T(1024)(128)(4,1)S(1)}, s32[]{:S(2)}) async-start(s8[4718592]{0:T(1024)(128)(4,1)} %bitcast.43), calls=%async_computation.1 | async-start | bytes 8388608
  158.7 4.2 %collective-permute-start.34 = (bf16[16,1536]{1,0:T(8,128)(2,1)S(1)}, bf16[16,1536]{1,0:T(8,128)(2,1)S(1)}, u32[]{:S(2)}, u32[]{:S(2)}) collective-permute-start(bf16[16,1536]{1,0:T(8,128)(2,1)S(1)} %fusion.9), channel_id=1, source_target_pairs={{0,3},{1,2},{2,1},{3,0},{4,7},{5,6},{6,5},{7,4},{8,11},{9,10},{10,... | collective-permute-start | bytes 147464 | tf_op jit(solution)/shard_map/stage4/ppermute | solution.py:120
  160.1 4.4 %collective-permute-start.33 = (bf16[16,1536]{1,0:T(8,128)(2,1)S(1)}, bf16[16,1536]{1,0:T(8,128)(2,1)S(1)}, u32[]{:S(2)}, u32[]{:S(2)}) collective-permute-start(bf16[16,1536]{1,0:T(8,128)(2,1)S(1)} %fusion.9), channel_id=1, source_target_pairs={{0,2},{1,3},{2,0},{3,1},{4,6},{5,7},{6,4},{7,5},{8,10},{9,11},{10,... | collective-permute-start | bytes 147464 | tf_op jit(solution)/shard_map/stage4/ppermute | solution.py:120
  161.2 3.3 %collective-permute-start.32 = (bf16[16,1536]{1,0:T(8,128)(2,1)S(1)}, bf16[16,1536]{1,0:T(8,128)(2,1)S(1)}, u32[]{:S(2)}, u32[]{:S(2)}) collective-permute-start(bf16[16,1536]{1,0:T(8,128)(2,1)S(1)} %fusion.9), channel_id=1, source_target_pairs={{0,1},{1,0},{2,3},{3,2},{4,5},{5,4},{6,7},{7,6},{8,9},{9,8},{10,11... | collective-permute-start | bytes 147464 | tf_op jit(solution)/shard_map/stage4/ppermute | solution.py:120
  164.6 4.9 %collective-permute-start.37 = (bf16[16,1536]{1,0:T(8,128)(2,1)S(1)}, bf16[16,1536]{1,0:T(8,128)(2,1)S(1)}, u32[]{:S(2)}, u32[]{:S(2)}) collective-permute-start(bf16[16,1536]{1,0:T(8,128)(2,1)S(1)} %add_convert_fusion.8), channel_id=1, source_target_pairs={{0,12},{1,13},{2,14},{3,15},{4,8},{5,9},{6,10},{7,11},{8,4},{9,5},... | collective-permute-start | bytes 147464 | tf_op jit(solution)/shard_map/stage4/ppermute | solution.py:120
  165.5 5.0 %collective-permute-start.36 = (bf16[16,1536]{1,0:T(8,128)(2,1)S(1)}, bf16[16,1536]{1,0:T(8,128)(2,1)S(1)}, u32[]{:S(2)}, u32[]{:S(2)}) collective-permute-start(bf16[16,1536]{1,0:T(8,128)(2,1)S(1)} %add_convert_fusion.8), channel_id=1, source_target_pairs={{0,8},{1,9},{2,10},{3,11},{4,12},{5,13},{6,14},{7,15},{8,0},{9,1},... | collective-permute-start | bytes 147464 | tf_op jit(solution)/shard_map/stage4/ppermute | solution.py:120
  167.0 3.5 %collective-permute-start.35 = (bf16[16,1536]{1,0:T(8,128)(2,1)S(1)}, bf16[16,1536]{1,0:T(8,128)(2,1)S(1)}, u32[]{:S(2)}, u32[]{:S(2)}) collective-permute-start(bf16[16,1536]{1,0:T(8,128)(2,1)S(1)} %add_convert_fusion.8), channel_id=1, source_target_pairs={{0,4},{1,5},{2,6},{3,7},{4,0},{5,1},{6,2},{7,3},{8,12},{9,13},{10,... | collective-permute-start | bytes 147464 | tf_op jit(solution)/shard_map/stage4/ppermute | solution.py:120
  170.5 61.0 %slice-start.1 = ((s8[4718592]{0:T(1024)(128)(4,1)}), s8[524288]{0:T(1024)(128)(4,1)S(1)}, s32[]{:S(2)}) async-start(s8[4718592]{0:T(1024)(128)(4,1)} %bitcast.43), calls=%async_computation.2 | async-start | bytes 1048576
  170.5 61.0 %copy-start.3 = (f32[16,1536]{1,0:T(8,128)S(1)}, f32[16,1536]{1,0:T(8,128)}, u32[]{:S(2)}) copy-start(f32[16,1536]{1,0:T(8,128)} %unpack.1) | copy-start | bytes 294916
  170.6 10.0 %collective-permute-start.39 = (bf16[16,1536]{1,0:T(8,128)(2,1)S(1)}, bf16[16,1536]{1,0:T(8,128)(2,1)S(1)}, u32[]{:S(2)}, u32[]{:S(2)}) collective-permute-start(bf16[16,1536]{1,0:T(8,128)(2,1)S(1)} %add_convert_fusion.7), channel_id=1, source_target_pairs={{0,60},{1,61},{2,62},{3,63},{4,56},{5,57},{6,58},{7,59},{8,52},{9,... | collective-permute-start | bytes 147464 | tf_op jit(solution)/shard_map/stage4/ppermute | solution.py:120
  178.6 3.1 %collective-permute-start.38 = (bf16[16,1536]{1,0:T(8,128)(2,1)S(1)}, bf16[16,1536]{1,0:T(8,128)(2,1)S(1)}, u32[]{:S(2)}, u32[]{:S(2)}) collective-permute-start(bf16[16,1536]{1,0:T(8,128)(2,1)S(1)} %add_convert_fusion.7), channel_id=1, source_target_pairs={{0,32},{1,33},{2,34},{3,35},{4,36},{5,37},{6,38},{7,39},{8,40},{9,... | collective-permute-start | bytes 147464 | tf_op jit(solution)/shard_map/stage4/ppermute | solution.py:120
  183.1 4.2 %collective-permute-start.42 = (bf16[16,1536]{1,0:T(8,128)(2,1)S(1)}, bf16[16,1536]{1,0:T(8,128)(2,1)S(1)}, u32[]{:S(2)}, u32[]{:S(2)}) collective-permute-start(bf16[16,1536]{1,0:T(8,128)(2,1)S(1)} %fusion.10), channel_id=1, source_target_pairs={{0,3},{1,2},{2,1},{3,0},{4,7},{5,6},{6,5},{7,4},{8,11},{9,10},{10,... | collective-permute-start | bytes 147464 | tf_op jit(solution)/shard_map/stage5/ppermute | solution.py:120
  184.4 4.4 %collective-permute-start.41 = (bf16[16,1536]{1,0:T(8,128)(2,1)S(1)}, bf16[16,1536]{1,0:T(8,128)(2,1)S(1)}, u32[]{:S(2)}, u32[]{:S(2)}) collective-permute-start(bf16[16,1536]{1,0:T(8,128)(2,1)S(1)} %fusion.10), channel_id=1, source_target_pairs={{0,2},{1,3},{2,0},{3,1},{4,6},{5,7},{6,4},{7,5},{8,10},{9,11},{10,... | collective-permute-start | bytes 147464 | tf_op jit(solution)/shard_map/stage5/ppermute | solution.py:120
  185.6 3.3 %collective-permute-start.40 = (bf16[16,1536]{1,0:T(8,128)(2,1)S(1)}, bf16[16,1536]{1,0:T(8,128)(2,1)S(1)}, u32[]{:S(2)}, u32[]{:S(2)}) collective-permute-start(bf16[16,1536]{1,0:T(8,128)(2,1)S(1)} %fusion.10), channel_id=1, source_target_pairs={{0,1},{1,0},{2,3},{3,2},{4,5},{5,4},{6,7},{7,6},{8,9},{9,8},{10,11... | collective-permute-start | bytes 147464 | tf_op jit(solution)/shard_map/stage5/ppermute | solution.py:120
  188.9 4.9 %collective-permute-start.45 = (bf16[16,1536]{1,0:T(8,128)(2,1)S(1)}, bf16[16,1536]{1,0:T(8,128)(2,1)S(1)}, u32[]{:S(2)}, u32[]{:S(2)}) collective-permute-start(bf16[16,1536]{1,0:T(8,128)(2,1)S(1)} %add_convert_fusion.5), channel_id=1, source_target_pairs={{0,12},{1,13},{2,14},{3,15},{4,8},{5,9},{6,10},{7,11},{8,4},{9,5},... | collective-permute-start | bytes 147464 | tf_op jit(solution)/shard_map/stage5/ppermute | solution.py:120
  190.9 4.4 %collective-permute-start.44 = (bf16[16,1536]{1,0:T(8,128)(2,1)S(1)}, bf16[16,1536]{1,0:T(8,128)(2,1)S(1)}, u32[]{:S(2)}, u32[]{:S(2)}) collective-permute-start(bf16[16,1536]{1,0:T(8,128)(2,1)S(1)} %add_convert_fusion.5), channel_id=1, source_target_pairs={{0,8},{1,9},{2,10},{3,11},{4,12},{5,13},{6,14},{7,15},{8,0},{9,1},... | collective-permute-start | bytes 147464 | tf_op jit(solution)/shard_map/stage5/ppermute | solution.py:120
  191.9 3.5 %collective-permute-start.43 = (bf16[16,1536]{1,0:T(8,128)(2,1)S(1)}, bf16[16,1536]{1,0:T(8,128)(2,1)S(1)}, u32[]{:S(2)}, u32[]{:S(2)}) collective-permute-start(bf16[16,1536]{1,0:T(8,128)(2,1)S(1)} %add_convert_fusion.5), channel_id=1, source_target_pairs={{0,4},{1,5},{2,6},{3,7},{4,0},{5,1},{6,2},{7,3},{8,12},{9,13},{10,... | collective-permute-start | bytes 147464 | tf_op jit(solution)/shard_map/stage5/ppermute | solution.py:120
  195.4 10.6 %collective-permute-start.47 = (bf16[16,1536]{1,0:T(8,128)(2,1)S(1)}, bf16[16,1536]{1,0:T(8,128)(2,1)S(1)}, u32[]{:S(2)}, u32[]{:S(2)}) collective-permute-start(bf16[16,1536]{1,0:T(8,128)(2,1)S(1)} %add_convert_fusion.4), channel_id=1, source_target_pairs={{0,60},{1,61},{2,62},{3,63},{4,56},{5,57},{6,58},{7,59},{8,52},{9,... | collective-permute-start | bytes 147464 | tf_op jit(solution)/shard_map/stage5/ppermute | solution.py:120
  204.1 3.1 %collective-permute-start.46 = (bf16[16,1536]{1,0:T(8,128)(2,1)S(1)}, bf16[16,1536]{1,0:T(8,128)(2,1)S(1)}, u32[]{:S(2)}, u32[]{:S(2)}) collective-permute-start(bf16[16,1536]{1,0:T(8,128)(2,1)S(1)} %add_convert_fusion.4), channel_id=1, source_target_pairs={{0,32},{1,33},{2,34},{3,35},{4,36},{5,37},{6,38},{7,39},{8,40},{9,... | collective-permute-start | bytes 147464 | tf_op jit(solution)/shard_map/stage5/ppermute | solution.py:120
  208.5 4.2 %collective-permute-start.50 = (bf16[16,1536]{1,0:T(8,128)(2,1)S(1)}, bf16[16,1536]{1,0:T(8,128)(2,1)S(1)}, u32[]{:S(2)}, u32[]{:S(2)}) collective-permute-start(bf16[16,1536]{1,0:T(8,128)(2,1)S(1)} %fusion.11), channel_id=1, source_target_pairs={{0,3},{1,2},{2,1},{3,0},{4,7},{5,6},{6,5},{7,4},{8,11},{9,10},{10,... | collective-permute-start | bytes 147464 | tf_op jit(solution)/shard_map/stage6/ppermute | solution.py:120
  209.9 4.4 %collective-permute-start.49 = (bf16[16,1536]{1,0:T(8,128)(2,1)S(1)}, bf16[16,1536]{1,0:T(8,128)(2,1)S(1)}, u32[]{:S(2)}, u32[]{:S(2)}) collective-permute-start(bf16[16,1536]{1,0:T(8,128)(2,1)S(1)} %fusion.11), channel_id=1, source_target_pairs={{0,2},{1,3},{2,0},{3,1},{4,6},{5,7},{6,4},{7,5},{8,10},{9,11},{10,... | collective-permute-start | bytes 147464 | tf_op jit(solution)/shard_map/stage6/ppermute | solution.py:120
  211.0 3.3 %collective-permute-start.48 = (bf16[16,1536]{1,0:T(8,128)(2,1)S(1)}, bf16[16,1536]{1,0:T(8,128)(2,1)S(1)}, u32[]{:S(2)}, u32[]{:S(2)}) collective-permute-start(bf16[16,1536]{1,0:T(8,128)(2,1)S(1)} %fusion.11), channel_id=1, source_target_pairs={{0,1},{1,0},{2,3},{3,2},{4,5},{5,4},{6,7},{7,6},{8,9},{9,8},{10,11... | collective-permute-start | bytes 147464 | tf_op jit(solution)/shard_map/stage6/ppermute | solution.py:120
  214.3 4.9 %collective-permute-start.53 = (bf16[16,1536]{1,0:T(8,128)(2,1)S(1)}, bf16[16,1536]{1,0:T(8,128)(2,1)S(1)}, u32[]{:S(2)}, u32[]{:S(2)}) collective-permute-start(bf16[16,1536]{1,0:T(8,128)(2,1)S(1)} %add_convert_fusion.2), channel_id=1, source_target_pairs={{0,12},{1,13},{2,14},{3,15},{4,8},{5,9},{6,10},{7,11},{8,4},{9,5},... | collective-permute-start | bytes 147464 | tf_op jit(solution)/shard_map/stage6/ppermute | solution.py:120
  215.4 5.2 %collective-permute-start.52 = (bf16[16,1536]{1,0:T(8,128)(2,1)S(1)}, bf16[16,1536]{1,0:T(8,128)(2,1)S(1)}, u32[]{:S(2)}, u32[]{:S(2)}) collective-permute-start(bf16[16,1536]{1,0:T(8,128)(2,1)S(1)} %add_convert_fusion.2), channel_id=1, source_target_pairs={{0,8},{1,9},{2,10},{3,11},{4,12},{5,13},{6,14},{7,15},{8,0},{9,1},... | collective-permute-start | bytes 147464 | tf_op jit(solution)/shard_map/stage6/ppermute | solution.py:120
  217.3 3.3 %collective-permute-start.51 = (bf16[16,1536]{1,0:T(8,128)(2,1)S(1)}, bf16[16,1536]{1,0:T(8,128)(2,1)S(1)}, u32[]{:S(2)}, u32[]{:S(2)}) collective-permute-start(bf16[16,1536]{1,0:T(8,128)(2,1)S(1)} %add_convert_fusion.2), channel_id=1, source_target_pairs={{0,4},{1,5},{2,6},{3,7},{4,0},{5,1},{6,2},{7,3},{8,12},{9,13},{10,... | collective-permute-start | bytes 147464 | tf_op jit(solution)/shard_map/stage6/ppermute | solution.py:120
  220.6 9.7 %collective-permute-start.55 = (bf16[16,1536]{1,0:T(8,128)(2,1)S(1)}, bf16[16,1536]{1,0:T(8,128)(2,1)S(1)}, u32[]{:S(2)}, u32[]{:S(2)}) collective-permute-start(bf16[16,1536]{1,0:T(8,128)(2,1)S(1)} %add_convert_fusion.1), channel_id=1, source_target_pairs={{0,60},{1,61},{2,62},{3,63},{4,56},{5,57},{6,58},{7,59},{8,52},{9,... | collective-permute-start | bytes 147464 | tf_op jit(solution)/shard_map/stage6/ppermute | solution.py:120
  228.4 3.1 %collective-permute-start.54 = (bf16[16,1536]{1,0:T(8,128)(2,1)S(1)}, bf16[16,1536]{1,0:T(8,128)(2,1)S(1)}, u32[]{:S(2)}, u32[]{:S(2)}) collective-permute-start(bf16[16,1536]{1,0:T(8,128)(2,1)S(1)} %add_convert_fusion.1), channel_id=1, source_target_pairs={{0,32},{1,33},{2,34},{3,35},{4,36},{5,37},{6,38},{7,39},{8,40},{9,... | collective-permute-start | bytes 147464 | tf_op jit(solution)/shard_map/stage6/ppermute | solution.py:120

commit v3 on v1

--- a/solution.py
+++ b/solution.py
@@ -83,6 +83,30 @@
             concat_axis=0,
             tiled=True,
         ).reshape(group_size * capacity, width + LANES)
+    def number(s, z, x):
+        return (s * z_count + z) * x_count + x
+
+    def exchange(value, mask_x, mask_z, shift=0, first=0, step=1):
+        pairs = [
+            (number(s, z, x), number(s + shift, z ^ mask_z, x ^ mask_x))
+            for s in range(first, sweep_count - shift, step)
+            for z in range(z_count)
+            for x in range(x_count)
+        ]
+        return lax.ppermute(value, ("sweep", "z", "x"), pairs)
+
+    def total(values):
+        result = values[0].astype(F32)
+        for value in values[1:]:
+            result = result + value.astype(F32)
+        return result
+
+    far = z_count - 1
+    here_x, here_z = lax.axis_index("x"), lax.axis_index("z")
+    odd = lax.axis_index("sweep") % 2 == 1
+    panel_size = coupling_in.shape[0]
+    slab = panel_size // x_count
+
     with jax.named_scope("fold"):
         outward = jnp.einsum(
             "fwv,fvp->fwp",
@@ -91,7 +115,55 @@
             preferred_element_type=F32,
         )
         outward = outward.astype(BF).reshape(face_dev * width, -1)
-        through = jnp.dot(coupling_in, outward, preferred_element_type=F32).astype(BF)
+
+        def by_rows(masks):
+            return [
+                jnp.dot(
+                    lax.dynamic_slice_in_dim(coupling_in, (here_x ^ m) * slab, slab, 0),
+                    outward,
+                    preferred_element_type=F32,
+                ).astype(BF)
+                for m in masks
+            ]
+
+        def by_columns(masks):
+            return [
+                lax.dot_general(
+                    lax.dynamic_slice_in_dim(outward, (here_x ^ m) * slab, slab, 1),
+                    coupling_in,
+                    (((0,), (1,)), ((), ())),
+                    preferred_element_type=F32,
+                ).astype(BF)
+                for m in masks
+            ]
+
+        def folded(*masks):
+            return lax.cond(odd, lambda: by_rows(masks), lambda: by_columns(masks))
+
+        (piece2,) = folded(2)
+        piece1, piece3, piece0 = folded(1, 3, 0)
+    with jax.named_scope("sum_x"):
+        half = slab // 2
+        upper = exchange(piece2[:half], 1, 0)
+        lower = exchange(piece2[half:], 3, 0)
+        to3 = jnp.concatenate([total([piece3[:half], upper]).astype(BF), piece3[half:]], axis=0)
+        to1 = jnp.concatenate([piece1[:half], total([piece1[half:], lower]).astype(BF)], axis=0)
+        summed_x = total([piece0, exchange(to3, 3, 0), exchange(to1, 1, 0)]).astype(BF)
+    with jax.named_scope("sum_z"):
+        four = z_count // 2
+        spot = (here_z % four) ^ jnp.where(here_z >= four, four - 1, 0)
+        quarter = slab // four
+        quarters = [
+            lax.dynamic_slice_in_dim(summed_x, (spot ^ m) * quarter, quarter, 0)
+            for m in range(four)
+        ]
+        own = total([quarters[0]] + [exchange(quarters[m], 0, m) for m in range(1, four)])
+        own = own.astype(BF)
+        own = total([own, exchange(own, 0, far)]).astype(BF)
+        through = jnp.zeros((slab, panel_size), BF)
+        for m in range(four):
+            part = own if m == 0 else exchange(own, 0, m)
+            through = lax.dynamic_update_slice_in_dim(through, part, (spot ^ m) * quarter, 0)
     with jax.named_scope("unpack"):
         assembled = pl.pallas_call(
             lambda *refs: unpack_kernel(face_dev, *refs),
@@ -106,41 +178,36 @@
         )
         source = both[:rhs_count] + both[rhs_count:]
 
-    def number(s, z, x):
-        return (s * z_count + z) * x_count + x
-
-    def exchange(value, layer, mask_x, mask_z, shift=0):
-        pairs = [
-            (number(layer, z, x), number(layer + shift, z ^ mask_z, x ^ mask_x))
-            for z in range(z_count)
-            for x in range(x_count)
-        ]
-        return lax.ppermute(value, ("sweep", "z", "x"), pairs)
-
-    def total(values):
-        result = values[0].astype(F32)
-        for value in values[1:]:
-            result = result + value.astype(F32)
-        return result
-
+    with jax.named_scope("sum_source"):
+        part = source.astype(BF)
+        part = total([part] + [exchange(part, m, 0) for m in range(1, x_count)]).astype(BF)
+        part = total([part] + [exchange(part, 0, m) for m in range(1, four)]).astype(BF)
+        source = total([part, exchange(part, 0, far)])
+        source_slab = lax.dynamic_slice_in_dim(source, here_x * slab, slab, 1)
+        source_once = jnp.where(here_x == 0, source, 0.0)
     panel = None
-    arrived = []
     for layer in range(sweep_count - 1):
         with jax.named_scope("stage%d" % layer):
-            part = source
-            if panel is not None:
-                part = source - jnp.dot(panel, through, preferred_element_type=F32)
-            part = part.astype(BF)
-            part = total([part] + [exchange(part, layer, m, 0) for m in range(1, x_count)])
-            part = part.astype(BF)
-            part = total([part] + [exchange(part, layer, 0, m) for m in range(1, z_count // 2)])
-            part = part.astype(BF)
-            panel = total(
-                [exchange(part, layer, 0, m, 1) for m in (0, z_count - 1)]
-            ).astype(BF)
-            arrived.append(panel)
+            if layer % 2 == 0:
+                following = source_slab
+                if panel is not None:
+                    following = source_slab - lax.dot_general(
+                        panel, through, (((1,), (1,)), ((), ())), preferred_element_type=F32
+                    )
+                panel_slab = exchange(following.astype(BF), 0, 0, 1, 0, 2)
+            else:
+                part = source_once - jnp.dot(panel_slab, through, preferred_element_type=F32)
+                part = part.astype(BF)
+                panel = total(
+                    [exchange(part, m, 0, 1, 1, 2) for m in range(x_count)]
+                ).astype(BF)
+    with jax.named_scope("spread"):
+        spread = jnp.zeros((rhs_count, panel_size), BF)
+        for m in range(x_count):
+            part = panel_slab if m == 0 else exchange(panel_slab, m, 0)
+            spread = lax.dynamic_update_slice_in_dim(spread, part, (here_x ^ m) * slab, 1)
+        panel = jnp.where(odd, spread, panel)
     with jax.named_scope("solve"):
-        panel = total(arrived).astype(BF)
         coupled = jnp.dot(panel, coupling_in, preferred_element_type=F32)
         local = (assembled - coupled).astype(BF).reshape(rhs_count, face_dev, width)
         solved = jnp.einsum("rfw,fwv->rfv", local, inverse, preferred_element_type=F32)

time: 477 us -> 224 us (0.47)
  the two profiles are of different devices: /device:TPU:1 before, /device:TPU:72 now
where the time goes in v3:
time: 224 us
  waiting for transfers between devices  108 us (48%)
  starting transfers between devices  61.8 us (28%)
  matrix products  35.7 us (16%)
  other arithmetic  7.7 us (3%)
  Pallas kernels  5.34 us (2%)
  local copies, waits for them, and re-layouts  4.46 us (2%)
    ppermute x37, waiting for transfers between devices, exchange(): return lax.ppermute(value, ('sweep', 'z', 'x'), pairs)  108 us
    ppermute x37, starting transfers between devices, exchange(): return lax.ppermute(value, ('sweep', 'z', 'x'), pairs)  51.4 us
    dot_general x4, matrix products, by_columns(): lax.dot_general(lax.dynamic_slice_in_dim(outward, (here_x ^ m) * slab, sl...  20.4 us
    all_to_all x1, starting transfers between devices, on_device(): lax.all_to_all(packed.reshape(group_size, capacity, width + LANES), ('z',...  10.5 us
    dot_general x1, matrix products, on_device(): jnp.einsum('fwv,fvp->fwp', inverse, coupling_out.reshape(face_dev, width,...  6.58 us
  transfers between devices with their start and end apart: 38, of which 29 were waited for; matrix products, arithmetic and copies ran while one was open for 10% of the time, Pallas kernels for 1%

profile of v3, /device:TPU:72, one launch (start us, length us, event | category | flops | bytes accessed | tf_op | source)
XLA Modules:
  0.0 223.5 jit_solution(12635295052000209695)
XLA Ops:
  0.0 1.3 copy-done
  1.3 6.6 %convolution_convert_fusion.2 = bf16[4,384,1536]{2,1,0:T(8,128)(2,1)} fusion(bf16[4,384,1536]{2,1,0:T(8,128)(2,1)} %bitcast.50, bf16[1,4,384,384]{3,2,1,0:T(8,128)(2,1)S(1)} %copy-done), kind=kOutput, calls=%fused_computation.26 | convolution fusion | flops 1814298624 | bytes 10616832 | tf_op jit(solution)/shard_map/fold/fwv,fvp->fwp/dot_general | solution.py:111
  7.8 4.8 %conditional.5 = (bf16[384,1536]{1,0:T(8,128)(2,1)S(1)}) conditional(s32[]{:T(128)} %convert_element_type.221, (s32[]{:T(128)}, bf16[1536,1536]{1,0:T(8,128)(2,1)}, bf16[1536,1536]{1,0:T(8,128)(2,1)}) %tuple.42, (s32[]{:T(128)}, bf16[1536,1536]{1,0:T(8,128)(2,1)}, bf16[1536,1536]{1,0:T(8,128)(2,1)}) %tuple.43), branch_computations={%region_2.3_spmd, %region_3.4_spmd} | conditional | flops 1811939328 | bytes 7077958
  7.8 4.8 %fusion.18 = bf16[384,1536]{1,0:T(8,128)(2,1)S(1)} fusion(bf16[1536,1536]{1,0:T(8,128)(2,1)} %get-tuple-element.48, bf16[1536,1536]{1,0:T(8,128)(2,1)} %get-tuple-element.46, s32[]{:T(128)S(6)} %select_n.67), kind=kOutput, calls=%fused_computation.20 | convolution fusion | flops 1811939328 | bytes 7077892 | tf_op jit(solution)/shard_map/fold/cond/branch_0_fun/dot_general | solution.py:131
  12.6 1.1 fusion.48
  13.8 1.5 collective-permute-start.8
  15.3 3.2 %pack.1 = bf16[1024,512]{1,0:T(8,128)(2,1)} custom-call(s32[1,512]{1,0:T(1,128)} %bitcast.59, s32[1,512]{1,0:T(1,128)} %bitcast.60, f32[512,384]{1,0:T(8,128)} %refs_2_.1), custom_call_target="tpu_custom_call" | custom-call | tf_op jit(solution)/shard_map/pack/pack/pallas_call | solution.py:73
  18.4 10.5 %all-to-all-start = ((bf16[32,32,512]{2,1,0:T(8,128)(2,1)}), bf16[32,32,512]{2,1,0:T(8,128)(2,1)S(1)}, u32[]{:S(2)}, u32[]{:S(2)}) async-start(bf16[32,32,512]{2,1,0:T(8,128)(2,1)} %bitcast.55), calls=%async_computation | async-start | bytes 2097152 | tf_op jit(solution)/shard_map/route/all_to_all | solution.py:79
  28.9 2.8 %collective-permute-start.10 = (bf16[192,1536]{1,0:T(8,128)(2,1)}, bf16[192,1536]{1,0:T(8,128)(2,1)}, u32[]{:S(2)}, u32[]{:S(2)}) collective-permute-start(bf16[192,1536]{1,0:T(8,128)(2,1)} %get-tuple-element.66), channel_id=1, source_target_pairs={{0,3},{1,2},{2,1},{3,0},{4,7},{5,6},{6,5},{7,4},{8,11},{9,10},{10,... | collective-permute-start | bytes 1769480 | tf_op jit(solution)/shard_map/sum_x/ppermute | solution.py:96
  31.6 15.7 %conditional.4 = (bf16[384,1536]{1,0:T(8,128)(2,1)S(1)}, bf16[384,1536]{1,0:T(8,128)(2,1)S(1)}, f32[384,1536]{1,0:T(8,128)}) conditional(s32[]{:T(128)} %convert_element_type.221, (s32[]{:T(128)}, bf16[1536,1536]{1,0:T(8,128)(2,1)}, bf16[1536,1536]{1,0:T(8,128)(2,1)}) %tuple.44, (s32[]{:T(128)}, bf16[1536,1536]{1,0:T(8,128)(2,1)}, ...), branch_computations={%region_0.1_spmd, %region_1.2_spmd} | conditional | flops 5436997632 | bytes 22413510
  31.6 6.2 %fusion = f32[384,1536]{1,0:T(8,128)} fusion(bf16[1536,1536]{1,0:T(8,128)(2,1)} %get-tuple-element.42, bf16[1536,1536]{1,0:T(8,128)(2,1)} %get-tuple-element.40, s32[]{:T(128)S(6)} %select_n.63), kind=kOutput, calls=%fused_computation.1 | convolution fusion | flops 1813118976 | bytes 8257540 | tf_op jit(solution)/shard_map/fold/cond/branch_0_fun/dot_general | solution.py:131
  37.8 4.8 %fusion.2 = bf16[384,1536]{1,0:T(8,128)(2,1)S(1)} fusion(bf16[1536,1536]{1,0:T(8,128)(2,1)} %get-tuple-element.42, bf16[1536,1536]{1,0:T(8,128)(2,1)} %get-tuple-element.40, s32[]{:T(128)S(6)} %select_n.62), kind=kOutput, calls=%fused_computation.3 | convolution fusion | flops 1811939328 | bytes 7077892 | tf_op jit(solution)/shard_map/fold/cond/branch_0_fun/dot_general | solution.py:131
  42.6 4.8 %fusion.4 = bf16[384,1536]{1,0:T(8,128)(2,1)S(1)} fusion(bf16[1536,1536]{1,0:T(8,128)(2,1)} %get-tuple-element.42, bf16[1536,1536]{1,0:T(8,128)(2,1)} %get-tuple-element.40, s32[]{:T(128)S(6)} %select_n.61), kind=kOutput, calls=%fused_computation.5 | convolution fusion | flops 1811939328 | bytes 7077892 | tf_op jit(solution)/shard_map/fold/cond/branch_0_fun/dot_general | solution.py:131
  47.5 1.2 add_convert_fusion.2
  49.4 7.2 %collective-permute-done.10 = bf16[192,1536]{1,0:T(8,128)(2,1)} collective-permute-done((bf16[192,1536]{1,0:T(8,128)(2,1)}, bf16[192,1536]{1,0:T(8,128)(2,1)}, u32[]{:S(2)}, u32[]{:S(2)}) %collective-permute-start.10) | collective-permute-done | bytes 589856 | tf_op jit(solution)/shard_map/sum_x/ppermute | solution.py:96
  56.6 1.2 add_convert_fusion.1
  57.8 1.1 pad_maximum_fusion.1
  59.1 21.7 %collective-permute-done.9 = bf16[384,1536]{1,0:T(8,128)(2,1)} collective-permute-done((bf16[384,1536]{1,0:T(8,128)(2,1)S(1)}, bf16[384,1536]{1,0:T(8,128)(2,1)}, u32[]{:S(2)}, u32[]{:S(2)}) %collective-permute-start.9) | collective-permute-done | bytes 1179680 | tf_op jit(solution)/shard_map/sum_x/ppermute | solution.py:96
  80.8 3.1 %collective-permute-done.11 = bf16[384,1536]{1,0:T(8,128)(2,1)} collective-permute-done((bf16[384,1536]{1,0:T(8,128)(2,1)}, bf16[384,1536]{1,0:T(8,128)(2,1)}, u32[]{:S(2)}, u32[]{:S(2)}) %collective-permute-start.11) | collective-permute-done | bytes 1179680 | tf_op jit(solution)/shard_map/sum_x/ppermute | solution.py:96
  83.9 2.8 %add_convert_fusion = bf16[384,1536]{1,0:T(8,128)(2,1)S(1)} fusion(bf16[384,1536]{1,0:T(8,128)(2,1)} %collective-permute-done.11, f32[384,1536]{1,0:T(8,128)} %get-tuple-element.55, bf16[384,1536]{1,0:T(8,128)(2,1)} %collective-permute-done.9), kind=kLoop, calls=%fused_computation.27 | loop fusion | flops 2949120 | bytes 5898240 | tf_op jit(solution)/shard_map/sum_x/convert_element_type | solution.py:151
  86.7 1.0 copy-done.1
  87.7 2.2 unpack.1
  89.9 1.0 subtract_convert_fusion
  90.9 3.2 %fusion.38 = f32[32,1536]{1,0:T(8,128)S(1)} fusion(bf16[1536,1536]{1,0:T(8,128)(2,1)} %bitcast.49, bf16[16,1536]{1,0:T(8,128)(2,1)S(1)} %get-tuple-element.58, bf16[16,1536]{1,0:T(8,128)(2,1)S(1)} %get-tuple-element.59), kind=kOutput, calls=%fused_computation.54 | convolution fusion | flops 151191552 | bytes 5013504 | tf_op jit(solution)/shard_map/source/dot_general | solution.py:176
  94.1 1.5 collective-permute-start
  95.6 2.5 %collective-permute-start.1 = (bf16[16,1536]{1,0:T(8,128)(2,1)S(1)}, bf16[16,1536]{1,0:T(8,128)(2,1)S(1)}, u32[]{:S(2)}, u32[]{:S(2)}) collective-permute-start(bf16[16,1536]{1,0:T(8,128)(2,1)S(1)} %fusion.37), channel_id=1, source_target_pairs={{0,2},{1,3},{2,0},{3,1},{4,6},{5,7},{6,4},{7,5},{8,10},{9,11},{10,... | collective-permute-start | bytes 147464 | tf_op jit(solution)/shard_map/sum_source/ppermute | solution.py:96
  99.0 1.9 collective-permute-start.12
  103.5 1.9 collective-permute-start.3
  105.4 5.6 %collective-permute-done.12 = bf16[96,1536]{1,0:T(8,128)(2,1)S(1)} collective-permute-done((bf16[96,1536]{1,0:T(8,128)(2,1)S(1)}, bf16[96,1536]{1,0:T(8,128)(2,1)S(1)}, u32[]{:S(2)}, u32[]{:S(2)}) %collective-permute-start.12) | collective-permute-done | bytes 294944 | tf_op jit(solution)/shard_map/sum_z/ppermute | solution.py:96
  111.5 10.3 %collective-permute-done.13 = bf16[96,1536]{1,0:T(8,128)(2,1)S(1)} collective-permute-done((bf16[96,1536]{1,0:T(8,128)(2,1)S(1)}, bf16[96,1536]{1,0:T(8,128)(2,1)S(1)}, u32[]{:S(2)}, u32[]{:S(2)}) %collective-permute-start.13) | collective-permute-done | bytes 294944 | tf_op jit(solution)/shard_map/sum_z/ppermute | solution.py:96
  121.8 5.9 %collective-permute-done.14 = bf16[96,1536]{1,0:T(8,128)(2,1)S(1)} collective-permute-done((bf16[96,1536]{1,0:T(8,128)(2,1)S(1)}, bf16[96,1536]{1,0:T(8,128)(2,1)S(1)}, u32[]{:S(2)}, u32[]{:S(2)}) %collective-permute-start.14) | collective-permute-done | bytes 294944 | tf_op jit(solution)/shard_map/sum_z/ppermute | solution.py:96
  127.8 5.5 %collective-permute-start.15 = (bf16[96,1536]{1,0:T(8,128)(2,1)S(1)}, bf16[96,1536]{1,0:T(8,128)(2,1)S(1)}, u32[]{:S(2)}, u32[]{:S(2)}) collective-permute-start(bf16[96,1536]{1,0:T(8,128)(2,1)S(1)} %add_convert_fusion.4), channel_id=1, source_target_pairs={{0,28},{1,29},{2,30},{3,31},{4,24},{5,25},{6,26},{7,27},{8,20},{9,... | collective-permute-start | bytes 884744 | tf_op jit(solution)/shard_map/sum_z/ppermute | solution.py:96
  134.2 5.0 %collective-permute-done.15 = bf16[96,1536]{1,0:T(8,128)(2,1)S(1)} collective-permute-done((bf16[96,1536]{1,0:T(8,128)(2,1)S(1)}, bf16[96,1536]{1,0:T(8,128)(2,1)S(1)}, u32[]{:S(2)}, u32[]{:S(2)}) %collective-permute-start.15) | collective-permute-done | bytes 294944 | tf_op jit(solution)/shard_map/sum_z/ppermute | solution.py:96
  140.7 1.7 collective-permute-start.17
  142.3 1.3 collective-permute-start.7
  143.6 1.3 collective-permute-start.18
  144.9 5.0 %collective-permute-done.16 = bf16[96,1536]{1,0:T(8,128)(2,1)S(1)} collective-permute-done((bf16[96,1536]{1,0:T(8,128)(2,1)S(1)}, bf16[96,1536]{1,0:T(8,128)(2,1)S(1)}, u32[]{:S(2)}, u32[]{:S(2)}) %collective-permute-start.16) | collective-permute-done | bytes 294944 | tf_op jit(solution)/shard_map/sum_z/ppermute | solution.py:96
  150.0 11.4 %collective-permute-done.17 = bf16[96,1536]{1,0:T(8,128)(2,1)S(1)} collective-permute-done((bf16[96,1536]{1,0:T(8,128)(2,1)S(1)}, bf16[96,1536]{1,0:T(8,128)(2,1)S(1)}, u32[]{:S(2)}, u32[]{:S(2)}) %collective-permute-start.17) | collective-permute-done | bytes 294944 | tf_op jit(solution)/shard_map/sum_z/ppermute | solution.py:96
  161.4 5.8 %collective-permute-done.18 = bf16[96,1536]{1,0:T(8,128)(2,1)S(1)} collective-permute-done((bf16[96,1536]{1,0:T(8,128)(2,1)S(1)}, bf16[96,1536]{1,0:T(8,128)(2,1)S(1)}, u32[]{:S(2)}, u32[]{:S(2)}) %collective-permute-start.18) | collective-permute-done | bytes 294944 | tf_op jit(solution)/shard_map/sum_z/ppermute | solution.py:96
  167.6 1.3 collective-permute-start.19
  168.9 1.3 collective-permute-start.20
  170.2 1.3 collective-permute-start.21
  171.5 1.3 collective-permute-start.22
  173.0 2.2 collective-permute-done.20
  175.2 3.7 %collective-permute-done.21 = bf16[16,1536]{1,0:T(8,128)(2,1)S(1)} collective-permute-done((bf16[16,1536]{1,0:T(8,128)(2,1)S(1)}, bf16[16,1536]{1,0:T(8,128)(2,1)S(1)}, u32[]{:S(2)}, u32[]{:S(2)}) %collective-permute-start.21) | collective-permute-done | bytes 49184 | tf_op jit(solution)/shard_map/stage1/ppermute | solution.py:96
  179.8 1.3 collective-permute-start.23
  182.2 1.3 collective-permute-start.24
  183.5 1.3 collective-permute-start.25
  184.8 1.3 collective-permute-start.26
  186.1 1.3 collective-permute-start.27
  187.6 2.2 collective-permute-done.25
  189.8 3.3 %collective-permute-done.26 = bf16[16,1536]{1,0:T(8,128)(2,1)S(1)} collective-permute-done((bf16[16,1536]{1,0:T(8,128)(2,1)S(1)}, bf16[16,1536]{1,0:T(8,128)(2,1)S(1)}, u32[]{:S(2)}, u32[]{:S(2)}) %collective-permute-start.26) | collective-permute-done | bytes 49184 | tf_op jit(solution)/shard_map/stage3/ppermute | solution.py:96
  194.2 1.3 collective-permute-start.28
  196.6 1.4 collective-permute-start.29
  198.0 1.3 collective-permute-start.30
  199.3 1.3 collective-permute-start.31
  200.6 1.3 collective-permute-start.32
  202.1 2.2 collective-permute-done.30
  204.3 3.1 %collective-permute-done.31 = bf16[16,1536]{1,0:T(8,128)(2,1)S(1)} collective-permute-done((bf16[16,1536]{1,0:T(8,128)(2,1)S(1)}, bf16[16,1536]{1,0:T(8,128)(2,1)S(1)}, u32[]{:S(2)}, u32[]{:S(2)}) %collective-permute-start.31) | collective-permute-done | bytes 49184 | tf_op jit(solution)/shard_map/stage5/ppermute | solution.py:96
  208.6 1.3 collective-permute-start.33
  211.3 3.3 %collective-permute-start.35 = (bf16[16,384]{1,0:T(8,128)(2,1)S(1)}, bf16[16,384]{1,0:T(8,128)(2,1)S(1)}, u32[]{:S(2)}, u32[]{:S(2)}) collective-permute-start(bf16[16,384]{1,0:T(8,128)(2,1)S(1)} %collective-permute-done.33), channel_id=1, source_target_pairs={{0,2},{1,3},{2,0},{3,1},{4,6},{5,7},{6,4},{7,5},{8,10},{9,11},{10,... | collective-permute-start | bytes 36872 | tf_op jit(solution)/shard_map/spread/ppermute | solution.py:96
  215.5 1.0 collective-permute-done.35
  216.5 3.0 %collective-permute-done.36 = bf16[16,384]{1,0:T(8,128)(2,1)S(1)} collective-permute-done((bf16[16,384]{1,0:T(8,128)(2,1)S(1)}, bf16[16,384]{1,0:T(8,128)(2,1)S(1)}, u32[]{:S(2)}, u32[]{:S(2)}) %collective-permute-start.36) | collective-permute-done | bytes 12320 | tf_op jit(solution)/shard_map/spread/ppermute | solution.py:96
  219.5 3.1 %fusion.24 = bf16[16,1536]{1,0:T(8,128)(2,1)S(1)} fusion(f32[16,1536]{1,0:T(8,128)S(1)} %copy-done.2, bf16[16,1536]{1,0:T(8,128)(2,1)S(1)} %constant_dynamic-update-slice_fusion, bf16[16,1536]{1,0:T(8,128)(2,1)S(1)} %add_convert_fusion.5, pred[]{:T(512)S(6)} %eq.9, bf16[1,1536,1536]{2,1,0:T(8,128)(2,1)} %param.16), kind=kOutput, calls=%fused_computation.32 | convolution fusion | flops 75571200 | bytes 4964353 | tf_op jit(solution)/shard_map/solve/dot_general | solution.py:211
  (64 shorter events, 17.2 us)
Async XLA Ops:
  0.0 1.3 copy-start
  13.8 33.7 %collective-permute-start.8 = (bf16[192,1536]{1,0:T(8,128)(2,1)}, bf16[192,1536]{1,0:T(8,128)(2,1)}, u32[]{:S(2)}, u32[]{:S(2)}) collective-permute-start(bf16[192,1536]{1,0:T(8,128)(2,1)} %get-tuple-element.65), channel_id=1, source_target_pairs={{0,1},{1,0},{2,3},{3,2},{4,5},{5,4},{6,7},{7,6},{8,9},{9,8},{10,11... | collective-permute-start | bytes 1769480 | tf_op jit(solution)/shard_map/sum_x/ppermute | solution.py:96
  18.4 68.3 %all-to-all-start = ((bf16[32,32,512]{2,1,0:T(8,128)(2,1)}), bf16[32,32,512]{2,1,0:T(8,128)(2,1)S(1)}, u32[]{:S(2)}, u32[]{:S(2)}) async-start(bf16[32,32,512]{2,1,0:T(8,128)(2,1)} %bitcast.55), calls=%async_computation | async-start | bytes 2097152 | tf_op jit(solution)/shard_map/route/all_to_all | solution.py:79
  28.9 27.8 %collective-permute-start.10 = (bf16[192,1536]{1,0:T(8,128)(2,1)}, bf16[192,1536]{1,0:T(8,128)(2,1)}, u32[]{:S(2)}, u32[]{:S(2)}) collective-permute-start(bf16[192,1536]{1,0:T(8,128)(2,1)} %get-tuple-element.66), channel_id=1, source_target_pairs={{0,3},{1,2},{2,1},{3,0},{4,7},{5,6},{6,5},{7,4},{8,11},{9,10},{10,... | collective-permute-start | bytes 1769480 | tf_op jit(solution)/shard_map/sum_x/ppermute | solution.py:96
  48.8 32.0 %collective-permute-start.9 = (bf16[384,1536]{1,0:T(8,128)(2,1)S(1)}, bf16[384,1536]{1,0:T(8,128)(2,1)}, u32[]{:S(2)}, u32[]{:S(2)}) collective-permute-start(bf16[384,1536]{1,0:T(8,128)(2,1)S(1)} %pad_maximum_fusion), channel_id=1, source_target_pairs={{0,3},{1,2},{2,1},{3,0},{4,7},{5,6},{6,5},{7,4},{8,11},{9,10},{10,... | collective-permute-start | bytes 3538952 | tf_op jit(solution)/shard_map/sum_x/ppermute | solution.py:96
  58.9 25.0 %collective-permute-start.11 = (bf16[384,1536]{1,0:T(8,128)(2,1)}, bf16[384,1536]{1,0:T(8,128)(2,1)}, u32[]{:S(2)}, u32[]{:S(2)}) collective-permute-start(bf16[384,1536]{1,0:T(8,128)(2,1)} %pad_maximum_fusion.1), channel_id=1, source_target_pairs={{0,1},{1,0},{2,3},{3,2},{4,5},{5,4},{6,7},{7,6},{8,9},{9,8},{10,11... | collective-permute-start | bytes 3538952 | tf_op jit(solution)/shard_map/sum_x/ppermute | solution.py:96
  86.7 1.0 copy-start.1
  94.1 7.5 %collective-permute-start = (bf16[16,1536]{1,0:T(8,128)(2,1)S(1)}, bf16[16,1536]{1,0:T(8,128)(2,1)S(1)}, u32[]{:S(2)}, u32[]{:S(2)}) collective-permute-start(bf16[16,1536]{1,0:T(8,128)(2,1)S(1)} %fusion.37), channel_id=1, source_target_pairs={{0,1},{1,0},{2,3},{3,2},{4,5},{5,4},{6,7},{7,6},{8,9},{9,8},{10,11... | collective-permute-start | bytes 147464 | tf_op jit(solution)/shard_map/sum_source/ppermute | solution.py:96
  95.6 6.9 %collective-permute-start.1 = (bf16[16,1536]{1,0:T(8,128)(2,1)S(1)}, bf16[16,1536]{1,0:T(8,128)(2,1)S(1)}, u32[]{:S(2)}, u32[]{:S(2)}) collective-permute-start(bf16[16,1536]{1,0:T(8,128)(2,1)S(1)} %fusion.37), channel_id=1, source_target_pairs={{0,2},{1,3},{2,0},{3,1},{4,6},{5,7},{6,4},{7,5},{8,10},{9,11},{10,... | collective-permute-start | bytes 147464 | tf_op jit(solution)/shard_map/sum_source/ppermute | solution.py:96
  98.1 5.3 %collective-permute-start.2 = (bf16[16,1536]{1,0:T(8,128)(2,1)S(1)}, bf16[16,1536]{1,0:T(8,128)(2,1)S(1)}, u32[]{:S(2)}, u32[]{:S(2)}) collective-permute-start(bf16[16,1536]{1,0:T(8,128)(2,1)S(1)} %fusion.37), channel_id=1, source_target_pairs={{0,3},{1,2},{2,1},{3,0},{4,7},{5,6},{6,5},{7,4},{8,11},{9,10},{10,... | collective-permute-start | bytes 147464 | tf_op jit(solution)/shard_map/sum_source/ppermute | solution.py:96
  99.0 11.9 %collective-permute-start.12 = (bf16[96,1536]{1,0:T(8,128)(2,1)S(1)}, bf16[96,1536]{1,0:T(8,128)(2,1)S(1)}, u32[]{:S(2)}, u32[]{:S(2)}) collective-permute-start(bf16[96,1536]{1,0:T(8,128)(2,1)S(1)} %get-tuple-element.62), channel_id=1, source_target_pairs={{0,4},{1,5},{2,6},{3,7},{4,0},{5,1},{6,2},{7,3},{8,12},{9,13},{10,... | collective-permute-start | bytes 884744 | tf_op jit(solution)/shard_map/sum_z/ppermute | solution.py:96
  100.9 21.0 %collective-permute-start.13 = (bf16[96,1536]{1,0:T(8,128)(2,1)S(1)}, bf16[96,1536]{1,0:T(8,128)(2,1)S(1)}, u32[]{:S(2)}, u32[]{:S(2)}) collective-permute-start(bf16[96,1536]{1,0:T(8,128)(2,1)S(1)} %get-tuple-element.64), channel_id=1, source_target_pairs={{0,8},{1,9},{2,10},{3,11},{4,12},{5,13},{6,14},{7,15},{8,0},{9,1},... | collective-permute-start | bytes 884744 | tf_op jit(solution)/shard_map/sum_z/ppermute | solution.py:96
  101.6 26.0 %collective-permute-start.14 = (bf16[96,1536]{1,0:T(8,128)(2,1)S(1)}, bf16[96,1536]{1,0:T(8,128)(2,1)S(1)}, u32[]{:S(2)}, u32[]{:S(2)}) collective-permute-start(bf16[96,1536]{1,0:T(8,128)(2,1)S(1)} %get-tuple-element.63), channel_id=1, source_target_pairs={{0,12},{1,13},{2,14},{3,15},{4,8},{5,9},{6,10},{7,11},{8,4},{9,5},... | collective-permute-start | bytes 884744 | tf_op jit(solution)/shard_map/sum_z/ppermute | solution.py:96
  103.5 29.8 %collective-permute-start.3 = (bf16[16,1536]{1,0:T(8,128)(2,1)S(1)}, bf16[16,1536]{1,0:T(8,128)(2,1)S(1)}, u32[]{:S(2)}, u32[]{:S(2)}) collective-permute-start(bf16[16,1536]{1,0:T(8,128)(2,1)S(1)} %add_convert_fusion.9), channel_id=1, source_target_pairs={{0,4},{1,5},{2,6},{3,7},{4,0},{5,1},{6,2},{7,3},{8,12},{9,13},{10,... | collective-permute-start | bytes 147464 | tf_op jit(solution)/shard_map/sum_source/ppermute | solution.py:96
  105.4 27.9 %collective-permute-start.4 = (bf16[16,1536]{1,0:T(8,128)(2,1)S(1)}, bf16[16,1536]{1,0:T(8,128)(2,1)S(1)}, u32[]{:S(2)}, u32[]{:S(2)}) collective-permute-start(bf16[16,1536]{1,0:T(8,128)(2,1)S(1)} %add_convert_fusion.9), channel_id=1, source_target_pairs={{0,8},{1,9},{2,10},{3,11},{4,12},{5,13},{6,14},{7,15},{8,0},{9,1},... | collective-permute-start | bytes 147464 | tf_op jit(solution)/shard_map/sum_source/ppermute | solution.py:96
  110.9 22.4 %collective-permute-start.5 = (bf16[16,1536]{1,0:T(8,128)(2,1)S(1)}, bf16[16,1536]{1,0:T(8,128)(2,1)S(1)}, u32[]{:S(2)}, u32[]{:S(2)}) collective-permute-start(bf16[16,1536]{1,0:T(8,128)(2,1)S(1)} %add_convert_fusion.9), channel_id=1, source_target_pairs={{0,12},{1,13},{2,14},{3,15},{4,8},{5,9},{6,10},{7,11},{8,4},{9,5},... | collective-permute-start | bytes 147464 | tf_op jit(solution)/shard_map/sum_source/ppermute | solution.py:96
  127.8 11.3 %collective-permute-start.15 = (bf16[96,1536]{1,0:T(8,128)(2,1)S(1)}, bf16[96,1536]{1,0:T(8,128)(2,1)S(1)}, u32[]{:S(2)}, u32[]{:S(2)}) collective-permute-start(bf16[96,1536]{1,0:T(8,128)(2,1)S(1)} %add_convert_fusion.4), channel_id=1, source_target_pairs={{0,28},{1,29},{2,30},{3,31},{4,24},{5,25},{6,26},{7,27},{8,20},{9,... | collective-permute-start | bytes 884744 | tf_op jit(solution)/shard_map/sum_z/ppermute | solution.py:96
  133.3 7.3 %collective-permute-start.6 = (bf16[16,1536]{1,0:T(8,128)(2,1)S(1)}, bf16[16,1536]{1,0:T(8,128)(2,1)S(1)}, u32[]{:S(2)}, u32[]{:S(2)}) collective-permute-start(bf16[16,1536]{1,0:T(8,128)(2,1)S(1)} %add_convert_fusion.8), channel_id=1, source_target_pairs={{0,28},{1,29},{2,30},{3,31},{4,24},{5,25},{6,26},{7,27},{8,20},{9,... | collective-permute-start | bytes 147464 | tf_op jit(solution)/shard_map/sum_source/ppermute | solution.py:96
  139.3 10.6 %collective-permute-start.16 = (bf16[96,1536]{1,0:T(8,128)(2,1)S(1)}, bf16[96,1536]{1,0:T(8,128)(2,1)S(1)}, u32[]{:S(2)}, u32[]{:S(2)}) collective-permute-start(bf16[96,1536]{1,0:T(8,128)(2,1)S(1)} %get-tuple-element.61), channel_id=1, source_target_pairs={{0,4},{1,5},{2,6},{3,7},{4,0},{5,1},{6,2},{7,3},{8,12},{9,13},{10,... | collective-permute-start | bytes 884744 | tf_op jit(solution)/shard_map/sum_z/ppermute | solution.py:96
  140.7 20.7 %collective-permute-start.17 = (bf16[96,1536]{1,0:T(8,128)(2,1)S(1)}, bf16[96,1536]{1,0:T(8,128)(2,1)S(1)}, u32[]{:S(2)}, u32[]{:S(2)}) collective-permute-start(bf16[96,1536]{1,0:T(8,128)(2,1)S(1)} %get-tuple-element.61), channel_id=1, source_target_pairs={{0,8},{1,9},{2,10},{3,11},{4,12},{5,13},{6,14},{7,15},{8,0},{9,1},... | collective-permute-start | bytes 884744 | tf_op jit(solution)/shard_map/sum_z/ppermute | solution.py:96
  142.3 25.0 %collective-permute-start.7 = (bf16[16,384]{1,0:T(8,128)(2,1)S(1)}, bf16[16,384]{1,0:T(8,128)(2,1)S(1)}, u32[]{:S(2)}, u32[]{:S(2)}) collective-permute-start(bf16[16,384]{1,0:T(8,128)(2,1)S(1)} %dynamic-slice_convert_fusion), channel_id=1, source_target_pairs={{0,32},{1,33},{2,34},{3,35},{4,36},{5,37},{6,38},{7,39},{8,40},{9,... | collective-permute-start | bytes 36872 | tf_op jit(solution)/shard_map/stage0/ppermute | solution.py:96
  143.6 23.6 %collective-permute-start.18 = (bf16[96,1536]{1,0:T(8,128)(2,1)S(1)}, bf16[96,1536]{1,0:T(8,128)(2,1)S(1)}, u32[]{:S(2)}, u32[]{:S(2)}) collective-permute-start(bf16[96,1536]{1,0:T(8,128)(2,1)S(1)} %get-tuple-element.61), channel_id=1, source_target_pairs={{0,12},{1,13},{2,14},{3,15},{4,8},{5,9},{6,10},{7,11},{8,4},{9,5},... | collective-permute-start | bytes 884744 | tf_op jit(solution)/shard_map/sum_z/ppermute | solution.py:96
  167.6 5.4 %collective-permute-start.19 = (bf16[16,1536]{1,0:T(8,128)(2,1)S(1)}, bf16[16,1536]{1,0:T(8,128)(2,1)S(1)}, u32[]{:S(2)}, u32[]{:S(2)}) collective-permute-start(bf16[16,1536]{1,0:T(8,128)(2,1)S(1)} %fusion.25), channel_id=1, source_target_pairs={{32,64},{33,65},{34,66},{35,67},{36,68},{37,69},{38,70},{39,71},{4... | collective-permute-start | bytes 147464 | tf_op jit(solution)/shard_map/stage1/ppermute | solution.py:96
  168.9 6.3 %collective-permute-start.20 = (bf16[16,1536]{1,0:T(8,128)(2,1)S(1)}, bf16[16,1536]{1,0:T(8,128)(2,1)S(1)}, u32[]{:S(2)}, u32[]{:S(2)}) collective-permute-start(bf16[16,1536]{1,0:T(8,128)(2,1)S(1)} %fusion.25), channel_id=1, source_target_pairs={{32,65},{33,64},{34,67},{35,66},{36,69},{37,68},{38,71},{39,70},{4... | collective-permute-start | bytes 147464 | tf_op jit(solution)/shard_map/stage1/ppermute | solution.py:96
  170.2 8.7 %collective-permute-start.21 = (bf16[16,1536]{1,0:T(8,128)(2,1)S(1)}, bf16[16,1536]{1,0:T(8,128)(2,1)S(1)}, u32[]{:S(2)}, u32[]{:S(2)}) collective-permute-start(bf16[16,1536]{1,0:T(8,128)(2,1)S(1)} %fusion.25), channel_id=1, source_target_pairs={{32,66},{33,67},{34,64},{35,65},{36,70},{37,71},{38,68},{39,69},{4... | collective-permute-start | bytes 147464 | tf_op jit(solution)/shard_map/stage1/ppermute | solution.py:96
  171.5 7.9 %collective-permute-start.22 = (bf16[16,1536]{1,0:T(8,128)(2,1)S(1)}, bf16[16,1536]{1,0:T(8,128)(2,1)S(1)}, u32[]{:S(2)}, u32[]{:S(2)}) collective-permute-start(bf16[16,1536]{1,0:T(8,128)(2,1)S(1)} %fusion.25), channel_id=1, source_target_pairs={{32,67},{33,66},{34,65},{35,64},{36,71},{37,70},{38,69},{39,68},{4... | collective-permute-start | bytes 147464 | tf_op jit(solution)/shard_map/stage1/ppermute | solution.py:96
  179.8 2.1 collective-permute-start.23
  182.2 5.4 %collective-permute-start.24 = (bf16[16,1536]{1,0:T(8,128)(2,1)S(1)}, bf16[16,1536]{1,0:T(8,128)(2,1)S(1)}, u32[]{:S(2)}, u32[]{:S(2)}) collective-permute-start(bf16[16,1536]{1,0:T(8,128)(2,1)S(1)} %fusion.26), channel_id=1, source_target_pairs={{32,64},{33,65},{34,66},{35,67},{36,68},{37,69},{38,70},{39,71},{4... | collective-permute-start | bytes 147464 | tf_op jit(solution)/shard_map/stage3/ppermute | solution.py:96
  183.5 6.3 %collective-permute-start.25 = (bf16[16,1536]{1,0:T(8,128)(2,1)S(1)}, bf16[16,1536]{1,0:T(8,128)(2,1)S(1)}, u32[]{:S(2)}, u32[]{:S(2)}) collective-permute-start(bf16[16,1536]{1,0:T(8,128)(2,1)S(1)} %fusion.26), channel_id=1, source_target_pairs={{32,65},{33,64},{34,67},{35,66},{36,69},{37,68},{38,71},{39,70},{4... | collective-permute-start | bytes 147464 | tf_op jit(solution)/shard_map/stage3/ppermute | solution.py:96
  184.8 8.3 %collective-permute-start.26 = (bf16[16,1536]{1,0:T(8,128)(2,1)S(1)}, bf16[16,1536]{1,0:T(8,128)(2,1)S(1)}, u32[]{:S(2)}, u32[]{:S(2)}) collective-permute-start(bf16[16,1536]{1,0:T(8,128)(2,1)S(1)} %fusion.26), channel_id=1, source_target_pairs={{32,66},{33,67},{34,64},{35,65},{36,70},{37,71},{38,68},{39,69},{4... | collective-permute-start | bytes 147464 | tf_op jit(solution)/shard_map/stage3/ppermute | solution.py:96
  186.1 7.7 %collective-permute-start.27 = (bf16[16,1536]{1,0:T(8,128)(2,1)S(1)}, bf16[16,1536]{1,0:T(8,128)(2,1)S(1)}, u32[]{:S(2)}, u32[]{:S(2)}) collective-permute-start(bf16[16,1536]{1,0:T(8,128)(2,1)S(1)} %fusion.26), channel_id=1, source_target_pairs={{32,67},{33,66},{34,65},{35,64},{36,71},{37,70},{38,69},{39,68},{4... | collective-permute-start | bytes 147464 | tf_op jit(solution)/shard_map/stage3/ppermute | solution.py:96
  194.2 2.1 collective-permute-start.28
  196.6 22.9 %copy-start.2 = (f32[16,1536]{1,0:T(8,128)S(1)}, f32[16,1536]{1,0:T(8,128)}, u32[]{:S(2)}) copy-start(f32[16,1536]{1,0:T(8,128)} %unpack.1) | copy-start | bytes 294916
  196.6 5.5 %collective-permute-start.29 = (bf16[16,1536]{1,0:T(8,128)(2,1)S(1)}, bf16[16,1536]{1,0:T(8,128)(2,1)S(1)}, u32[]{:S(2)}, u32[]{:S(2)}) collective-permute-start(bf16[16,1536]{1,0:T(8,128)(2,1)S(1)} %fusion.27), channel_id=1, source_target_pairs={{32,64},{33,65},{34,66},{35,67},{36,68},{37,69},{38,70},{39,71},{4... | collective-permute-start | bytes 147464 | tf_op jit(solution)/shard_map/stage5/ppermute | solution.py:96
  198.0 6.3 %collective-permute-start.30 = (bf16[16,1536]{1,0:T(8,128)(2,1)S(1)}, bf16[16,1536]{1,0:T(8,128)(2,1)S(1)}, u32[]{:S(2)}, u32[]{:S(2)}) collective-permute-start(bf16[16,1536]{1,0:T(8,128)(2,1)S(1)} %fusion.27), channel_id=1, source_target_pairs={{32,65},{33,64},{34,67},{35,66},{36,69},{37,68},{38,71},{39,70},{4... | collective-permute-start | bytes 147464 | tf_op jit(solution)/shard_map/stage5/ppermute | solution.py:96
  199.3 8.1 %collective-permute-start.31 = (bf16[16,1536]{1,0:T(8,128)(2,1)S(1)}, bf16[16,1536]{1,0:T(8,128)(2,1)S(1)}, u32[]{:S(2)}, u32[]{:S(2)}) collective-permute-start(bf16[16,1536]{1,0:T(8,128)(2,1)S(1)} %fusion.27), channel_id=1, source_target_pairs={{32,66},{33,67},{34,64},{35,65},{36,70},{37,71},{38,68},{39,69},{4... | collective-permute-start | bytes 147464 | tf_op jit(solution)/shard_map/stage5/ppermute | solution.py:96
  200.6 7.5 %collective-permute-start.32 = (bf16[16,1536]{1,0:T(8,128)(2,1)S(1)}, bf16[16,1536]{1,0:T(8,128)(2,1)S(1)}, u32[]{:S(2)}, u32[]{:S(2)}) collective-permute-start(bf16[16,1536]{1,0:T(8,128)(2,1)S(1)} %fusion.27), channel_id=1, source_target_pairs={{32,67},{33,66},{34,65},{35,64},{36,71},{37,70},{38,69},{39,68},{4... | collective-permute-start | bytes 147464 | tf_op jit(solution)/shard_map/stage5/ppermute | solution.py:96
  208.6 2.1 collective-permute-start.33
  210.8 4.7 %collective-permute-start.34 = (bf16[16,384]{1,0:T(8,128)(2,1)S(1)}, bf16[16,384]{1,0:T(8,128)(2,1)S(1)}, u32[]{:S(2)}, u32[]{:S(2)}) collective-permute-start(bf16[16,384]{1,0:T(8,128)(2,1)S(1)} %collective-permute-done.33), channel_id=1, source_target_pairs={{0,1},{1,0},{2,3},{3,2},{4,5},{5,4},{6,7},{7,6},{8,9},{9,8},{10,11... | collective-permute-start | bytes 36872 | tf_op jit(solution)/shard_map/spread/ppermute | solution.py:96
  211.3 5.2 %collective-permute-start.35 = (bf16[16,384]{1,0:T(8,128)(2,1)S(1)}, bf16[16,384]{1,0:T(8,128)(2,1)S(1)}, u32[]{:S(2)}, u32[]{:S(2)}) collective-permute-start(bf16[16,384]{1,0:T(8,128)(2,1)S(1)} %collective-permute-done.33), channel_id=1, source_target_pairs={{0,2},{1,3},{2,0},{3,1},{4,6},{5,7},{6,4},{7,5},{8,10},{9,11},{10,... | collective-permute-start | bytes 36872 | tf_op jit(solution)/shard_map/spread/ppermute | solution.py:96
  214.6 4.9 %collective-permute-start.36 = (bf16[16,384]{1,0:T(8,128)(2,1)S(1)}, bf16[16,384]{1,0:T(8,128)(2,1)S(1)}, u32[]{:S(2)}, u32[]{:S(2)}) collective-permute-start(bf16[16,384]{1,0:T(8,128)(2,1)S(1)} %collective-permute-done.33), channel_id=1, source_target_pairs={{0,3},{1,2},{2,1},{3,0},{4,7},{5,6},{6,5},{7,4},{8,11},{9,10},{10,... | collective-permute-start | bytes 36872 | tf_op jit(solution)/shard_map/spread/ppermute | solution.py:96

commit v4 on v1

v4 whole, which is shorter than its diff:
```python
import jax
import jax.numpy as jnp
from jax import lax
from jax.experimental import pallas as pl
from jax.experimental.pallas import tpu as pltpu
from jax.sharding import Mesh
from jax.sharding import PartitionSpec as P

BF = jnp.bfloat16
F32 = jnp.float32
LANES = 128
FIRST = 2


def pack_kernel(owner_count, owner_ref, slot_ref, rows_ref, out_ref):
    row_total, width = rows_ref.shape
    capacity = row_total // owner_count * 2
    owner = owner_ref[...]
    match = (lax.broadcasted_iota(jnp.int32, (owner_count, row_total), 0) == owner).astype(F32)
    earlier_mask = (
        lax.broadcasted_iota(jnp.int32, (row_total, row_total), 0)
        < lax.broadcasted_iota(jnp.int32, (row_total, row_total), 1)
    )
    earlier = jnp.dot(
        match.astype(BF), earlier_mask.astype(F32).astype(BF), preferred_element_type=F32
    )
    position = jnp.sum(earlier * match, axis=0, keepdims=True).astype(jnp.int32)
    target = owner * capacity + position
    slots = (slot_ref[...] + 1).astype(F32)
    rows = rows_ref[...].astype(BF)
    block = 256
    for start in range(0, owner_count * capacity, block):
        place = lax.broadcasted_iota(jnp.int32, (block, row_total), 0) + start
        chosen = place == target
        picked = jnp.where(chosen, 1.0, 0.0).astype(BF)
        out_ref[pl.ds(start, block), pl.ds(0, width)] = jnp.dot(
            picked, rows, preferred_element_type=F32
        ).astype(BF)
        slot = jnp.sum(jnp.where(chosen, slots, 0.0), axis=1, keepdims=True)
        out_ref[pl.ds(start, block), pl.ds(width, LANES)] = jnp.broadcast_to(
            slot, (block, LANES)
        ).astype(BF)


def source_kernel(face_dev, got_ref, face_ref, outward_ref, assembled_ref, source_ref):
    rhs_count = assembled_ref.shape[0]
    width = assembled_ref.shape[1] // face_dev
    slot = got_ref[:, pl.ds(width, LANES)].astype(F32)
    lane = lax.broadcasted_iota(jnp.int32, slot.shape, 1)
    wanted = (lane % rhs_count) * face_dev + lane // rhs_count + 1
    wanted = jnp.where(lane < rhs_count * face_dev, wanted, -1).astype(F32)
    picked = jnp.where(slot == wanted, 1.0, 0.0).astype(BF)
    summed = lax.dot_general(
        picked,
        got_ref[:, pl.ds(0, width)],
        (((0,), (0,)), ((), ())),
        preferred_element_type=F32,
    )
    for face in range(face_dev):
        assembled_ref[:, pl.ds(face * width, width)] = (
            face_ref[:, face, :] + summed[face * rhs_count : (face + 1) * rhs_count, :]
        )
    assembled = assembled_ref[...]
    high = assembled.astype(BF)
    low = (assembled - high.astype(F32)).astype(BF)
    both = jnp.dot(
        jnp.concatenate([high, low], axis=0), outward_ref[...], preferred_element_type=F32
    )
    source_ref[...] = both[:rhs_count] + both[rhs_count:]


def outward_kernel(face_dev, side_ref, inv_ref, out_ref, in_ref, outward_ref, piece_ref, held):
    step = pl.program_id(0)
    width = inv_ref.shape[1]

    @pl.when(step < face_dev)
    def _():
        rows = jnp.dot(inv_ref[0], out_ref[...], preferred_element_type=F32).astype(BF)
        outward_ref[...] = rows
        held[pl.ds(pl.multiple_of(step * width, width), width), :] = rows

    @pl.when(step >= face_dev)
    def _():
        block = jnp.where(side_ref[1] == 1, step - face_dev, side_ref[0] ^ FIRST)
        slab = piece_ref.shape[1]
        columns = held[:, pl.ds(pl.multiple_of(block * slab, slab), slab)]
        piece_ref[...] = jnp.dot(in_ref[...], columns, preferred_element_type=F32).astype(BF)


def fold_kernel(side_ref, in_ref, outward_ref, piece_ref):
    piece_ref[0] = jnp.dot(
        in_ref[...], outward_ref[...], preferred_element_type=F32
    ).astype(BF)


def on_device(shape, face_rhs, res_rows, row_owner, row_slot, inv_blocks, couple_in, couple_out):
    sweep_count, z_count, x_count = shape
    group_size = z_count * x_count
    rhs_count, face_dev, width = face_rhs.shape[1:]
    row_total = res_rows.shape[0]
    capacity = 2 * row_total // group_size
    coupling_in, coupling_out, inverse = couple_in[0], couple_out[0], inv_blocks[0]

    def number(s, z, x):
        return (s * z_count + z) * x_count + x

    def exchange(value, mask_x, mask_z=0, partner=lambda s: s, along_z=None):
        pairs = [
            (
                number(s, z, x),
                number(partner(s), along_z[z] if along_z else z ^ mask_z, x ^ mask_x),
            )
            for s in range(sweep_count)
            for z in range(z_count)
            for x in range(x_count)
        ]
        return lax.ppermute(value, ("sweep", "z", "x"), pairs)

    def after_even(s):
        return s ^ 1

    def after_odd(s):
        return (s + 1 if s % 2 else s - 1) % sweep_count

    def total(values):
        result = values[0].astype(F32)
        for value in values[1:]:
            result = result + value.astype(F32)
        return result

    far, four = z_count - 1, z_count // 2
    here_x, here_z = lax.axis_index("x"), lax.axis_index("z")
    own_layer = lax.axis_index("sweep")
    odd = own_layer % 2 == 1
    panel_size = coupling_in.shape[0]
    slab = panel_size // x_count

    with jax.named_scope("pack"):
        packed = pl.pallas_call(
            lambda *refs: pack_kernel(group_size, *refs),
            out_shape=jax.ShapeDtypeStruct((group_size * capacity, width + LANES), BF),
            name="pack",
        )(row_owner.reshape(1, row_total), row_slot.reshape(1, row_total), res_rows)
    with jax.named_scope("route"):
        inverse_later, packed = lax.optimization_barrier((inverse, packed))
        got = lax.all_to_all(
            packed.reshape(group_size, capacity, width + LANES),
            ("z", "x"),
            split_axis=0,
            concat_axis=0,
            tiled=True,
        ).reshape(group_size * capacity, width + LANES)
    with jax.named_scope("fold"):
        side = jnp.stack([here_x, odd.astype(jnp.int32)])
        faces = panel_size // slab

        def mask_of(turn):
            return jnp.where(turn == 0, 1, jnp.where(turn == 1, 3, 0))

        outward, piece2 = pl.pallas_call(
            lambda *refs: outward_kernel(face_dev, *refs),
            grid_spec=pltpu.PrefetchScalarGridSpec(
                num_scalar_prefetch=1,
                grid=(face_dev + faces,),
                in_specs=[
                    pl.BlockSpec(
                        (1, width, width), lambda i, side: (jnp.minimum(i, face_dev - 1), 0, 0)
                    ),
                    pl.BlockSpec(
                        (width, panel_size), lambda i, side: (jnp.minimum(i, face_dev - 1), 0)
                    ),
                    pl.BlockSpec(
                        (slab, face_dev * width),
                        lambda i, side: (
                            jnp.where(
                                side[1] == 1, side[0] ^ FIRST, jnp.maximum(i - face_dev, 0)
                            ),
                            0,
                        ),
                    ),
                ],
                out_specs=[
                    pl.BlockSpec(
                        (width, panel_size), lambda i, side: (jnp.minimum(i, face_dev - 1), 0)
                    ),
                    pl.BlockSpec(
                        (slab, slab), lambda i, side: (0, jnp.maximum(i - face_dev, 0))
                    ),
                ],
                scratch_shapes=[pltpu.VMEM((face_dev * width, panel_size), BF)],
            ),
            out_shape=[
                jax.ShapeDtypeStruct((face_dev * width, panel_size), BF),
                jax.ShapeDtypeStruct((slab, panel_size), BF),
            ],
            compiler_params=pltpu.CompilerParams(vmem_limit_bytes=40 << 20),
            name="outward",
        )(side, inverse_later, coupling_out, coupling_in)
        pieces = pl.pallas_call(
            fold_kernel,
            grid_spec=pltpu.PrefetchScalarGridSpec(
                num_scalar_prefetch=1,
                grid=(x_count - 1, faces),
                in_specs=[
                    pl.BlockSpec(
                        (slab, face_dev * width),
                        lambda i, j, side: (
                            jnp.where(side[1] == 1, side[0] ^ mask_of(i), j),
                            0,
                        ),
                    ),
                    pl.BlockSpec(
                        (face_dev * width, slab),
                        lambda i, j, side: (
                            0,
                            jnp.where(side[1] == 1, j, side[0] ^ mask_of(i)),
                        ),
                    ),
                ],
                out_specs=pl.BlockSpec((1, slab, slab), lambda i, j, side: (i, 0, j)),
            ),
            out_shape=jax.ShapeDtypeStruct((x_count - 1, slab, panel_size), BF),
            compiler_params=pltpu.CompilerParams(vmem_limit_bytes=40 << 20),
            name="fold",
        )(side, coupling_in, outward)
        piece1, piece3, piece0 = pieces[0], pieces[1], pieces[2]
    with jax.named_scope("sum_x"):
        half = slab // 2
        upper = exchange(piece2[:half], 1)
        lower = exchange(piece2[half:], 3)
        to3 = jnp.concatenate([total([piece3[:half], upper]).astype(BF), piece3[half:]], axis=0)
        to1 = jnp.concatenate([piece1[:half], total([piece1[half:], lower]).astype(BF)], axis=0)
        got, to3, to1 = lax.optimization_barrier((got, to3, to1))
        summed_x = total(
            [piece0, exchange(to3, 3), exchange(to1, 1)]
        ).astype(BF)
    with jax.named_scope("source"):
        vmem = pl.BlockSpec(memory_space=pltpu.VMEM)
        assembled, source = pl.pallas_call(
            lambda *refs: source_kernel(face_dev, *refs),
            in_specs=[vmem, vmem, vmem],
            out_specs=[vmem, vmem],
            out_shape=[jax.ShapeDtypeStruct((rhs_count, face_dev * width), F32)] * 2,
            name="source",
        )(got, face_rhs[0], outward)
    with jax.named_scope("sum_source"):
        part = source.astype(BF)
        part = total([part] + [exchange(part, m) for m in range(1, x_count)]).astype(BF)
        source_x, summed_x = lax.optimization_barrier((part, summed_x))
    with jax.named_scope("sum_z"):
        turns = [z ^ 1 for z in range(z_count)], [3, 6, 5, 0, 7, 2, 1, 4]

        def shifted(places):
            return [(places[(z + 1) % z_count] - 1) % z_count for z in range(z_count)]

        near, across = turns
        paths = [(near, shifted(near), across), (shifted(near), near, shifted(across))]
        part_rows = slab // 2
        bits = [((102 >> z) & 1, (180 >> z) & 1) for z in (here_z, (here_z + 1) % z_count)]
        summed = [summed_x[:part_rows], summed_x[part_rows:]]

        def halved(rows, bit):
            size = rows.shape[0] // 2
            kept = lax.dynamic_slice_in_dim(rows, bit * size, size, 0)
            given = lax.dynamic_slice_in_dim(rows, (1 - bit) * size, size, 0)
            return kept, given

        def joined(own, other, bit):
            size = own.shape[0]
            both = jnp.concatenate([own, own], axis=0)
            return lax.dynamic_update_slice_in_dim(both, other, (1 - bit) * size, 0)

        def swap(values, turn):
            return [exchange(v, 0, 0, along_z=p[turn]) for v, p in zip(values, paths)]

        for turn in range(2):
            split = [halved(rows, bit[turn]) for rows, bit in zip(summed, bits)]
            got_rows = swap([given for _, given in split], turn)
            summed = [total([kept, new]).astype(BF) for (kept, _), new in zip(split, got_rows)]
            if turn == 0:
                source_x, summed[0] = lax.optimization_barrier((source_x, summed[0]))
                source_z = [source_x] + [exchange(source_x, 0, m) for m in range(1, four)]
            else:
                source_z = total(source_z).astype(BF)
                source_z, summed[0] = lax.optimization_barrier((source_z, summed[0]))
                source_far = exchange(source_z, 0, far)
        summed = [total([rows, new]).astype(BF) for rows, new in zip(summed, swap(summed, 2))]
        for turn in (1, 0):
            got_rows = swap(summed, turn)
            summed = [
                joined(rows, new, bit[turn]) for rows, new, bit in zip(summed, got_rows, bits)
            ]
        through = jnp.concatenate(summed, axis=0)
        source = total([source_z, source_far])
        source_slab = lax.dynamic_slice_in_dim(source, here_x * slab, slab, 1)
        source_once = jnp.where(here_x == 0, source, 0.0)
    through_columns = jnp.concatenate(
        [through[:, start : start + slab] for start in range(0, panel_size, slab)], axis=0
    )
    panel = None
    for layer in range(sweep_count - 1):
        with jax.named_scope("stage%d" % layer):
            if layer % 2 == 0:
                following = source_slab
                if panel is not None:
                    following = source_slab - jnp.dot(
                        panel, through_columns, preferred_element_type=F32
                    )
                following = following.astype(BF)
                if layer < sweep_count - 2:
                    panel_slab = exchange(following, 0, 0, after_even)
            else:
                part = source_once - jnp.dot(panel_slab, through, preferred_element_type=F32)
                part = part.astype(BF)
                part = total([exchange(part, m, 0, after_odd) for m in range(x_count)])
                panel = jnp.where(own_layer == 0, 0.0, part).astype(BF)
    with jax.named_scope("spread"):
        spread = jnp.zeros((rhs_count, panel_size), BF)
        for m in range(x_count):
            part = exchange(following, m, 0, after_even)
            spread = lax.dynamic_update_slice_in_dim(spread, part, (here_x ^ m) * slab, 1)
        panel = jnp.where(odd, spread, panel)
    with jax.named_scope("solve"):
        coupled = jnp.dot(panel, coupling_in, preferred_element_type=F32)
        local = (assembled - coupled).astype(BF).reshape(rhs_count, face_dev, width)
        solved = jnp.einsum("rfw,fwv->rfv", local, inverse, preferred_element_type=F32)
    return solved[None]


def solution(mesh):
    shape = (mesh.shape["sweep"], 8, mesh.shape["layer"] // 8)
    fine = Mesh(mesh.devices.reshape(shape), ("sweep", "z", "x"))
    layer = ("z", "x")
    everywhere = ("sweep", "z", "x")
    return jax.shard_map(
        lambda *args: on_device(shape, *args),
        mesh=fine,
        in_specs=(
            P("sweep", None, layer, None),
            P(everywhere, None),
            P(everywhere, None),
            P(everywhere),
            P("sweep", layer, None, None),
            P("sweep", None, layer),
            P("sweep", layer, None),
        ),
        out_specs=P("sweep", None, layer, None),
        check_vma=False,
    )
```

time: 477 us -> 184 us (0.39)
  starting transfers between devices: 396 us -> 82.2 us
  matrix products: 28.5 us -> 5.05 us
  Pallas kernels: 5.46 us -> 28.1 us
  waiting for transfers between devices: 41.3 us -> 54.7 us
  other arithmetic: 1.55 us -> 7.74 us
    ppermute x56 -> x40, starting transfers between devices: 385 us -> 70 us  [exchange(): return lax.ppermute(value, ('sweep', 'z', 'x'), pairs)]
    ppermute x56 -> x40, waiting for transfers between devices: 21.7 us -> 54.7 us  [exchange(): return lax.ppermute(value, ('sweep', 'z', 'x'), pairs)]
    dot_general x9 -> x6, matrix products: 27.5 us -> 1.62 us  [the longest x3 0.82 us: on_device(): jnp.dot(panel, through_columns, preferred_element_type=F32)]
    pallas_call x1 -> x3, Pallas kernels: 2.19 us -> 24.8 us  [the longest x1 11.9 us: on_device(): pl.pallas_call(fold_kernel, grid_spec=pltpu.PrefetchScalarGridSpec(num_sc...]
    all_to_all x1, waiting for transfers between devices: 19.6 us -> 0.01 us  [on_device(): lax.all_to_all(packed.reshape(group_size, capacity, width + LANES), ('z',...]
  transfers between devices with their start and end apart: 57 -> 41, of which waited for: 8 -> 21; matrix products, arithmetic and copies ran while one was open for 3% -> 3% of each run, Pallas kernels for 0% -> 14%
where the time goes in v4:
time: 184 us
  starting transfers between devices  82.2 us (45%)
  waiting for transfers between devices  54.7 us (30%)
  Pallas kernels  28.1 us (15%)
  other arithmetic  7.74 us (4%)
  local copies, waits for them, and re-layouts  5.84 us (3%)
  matrix products  5.05 us (3%)
    ppermute x40, starting transfers between devices, exchange(): return lax.ppermute(value, ('sweep', 'z', 'x'), pairs)  70 us
    ppermute x40, waiting for transfers between devices, exchange(): return lax.ppermute(value, ('sweep', 'z', 'x'), pairs)  54.7 us
    all_to_all x1, starting transfers between devices, on_device(): lax.all_to_all(packed.reshape(group_size, capacity, width + LANES), ('z',...  12.1 us
    pallas_call x1, Pallas kernels, on_device(): pl.pallas_call(fold_kernel, grid_spec=pltpu.PrefetchScalarGridSpec(num_sc...  11.9 us
    pallas_call x1, Pallas kernels, on_device(): pl.pallas_call(lambda *refs: outward_kernel(face_dev, *refs), grid_spec=p...  8.46 us
    unnamed x16, local copies, waits for them, and re-layouts  4.69 us
    pallas_call x1, Pallas kernels, on_device(): pl.pallas_call(lambda *refs: source_kernel(face_dev, *refs), in_specs=[vm...  4.5 us
  transfers between devices with their start and end apart: 41, of which 21 were waited for; matrix products, arithmetic and copies ran while one was open for 3% of the time, Pallas kernels for 14%

profile of v4, /device:TPU:1, one launch (start us, length us, event | category | flops | bytes accessed | tf_op | source)
XLA Modules:
  0.0 184.0 jit_solution(15027770543764366518)
XLA Ops:
  0.0 3.2 %pack.1 = bf16[1024,512]{1,0:T(8,128)(2,1)} custom-call(s32[1,512]{1,0:T(1,128)} %bitcast.54, s32[1,512]{1,0:T(1,128)} %bitcast.55, f32[512,384]{1,0:T(8,128)} %refs_2_.1), custom_call_target="tpu_custom_call" | custom-call | tf_op jit(solution)/shard_map/pack/pack/pallas_call | solution.py:139
  3.3 12.1 %all-to-all-start = ((bf16[32,32,512]{2,1,0:T(8,128)(2,1)}), bf16[32,32,512]{2,1,0:T(8,128)(2,1)}, u32[]{:S(2)}, u32[]{:S(2)}) async-start(bf16[32,32,512]{2,1,0:T(8,128)(2,1)} %bitcast.51), calls=%async_computation | async-start | bytes 2097152 | tf_op jit(solution)/shard_map/route/all_to_all | solution.py:146
  15.5 2.5 %copy-done.1 = bf16[1,1536,1536]{2,1,0:T(8,128)(2,1)S(1)} copy-done((bf16[1,1536,1536]{2,1,0:T(8,128)(2,1)S(1)}, bf16[1,1536,1536]{2,1,0:T(8,128)(2,1)}, u32[]{:S(2)}) %copy-start.1) | copy-done | bytes 4718616
  18.0 8.5 %outward.1 = (bf16[1536,1536]{1,0:T(8,128)(2,1)S(1)}, bf16[384,1536]{1,0:T(8,128)(2,1)S(1)}) custom-call(s32[2]{0:T(128)S(1)} %pad_add_fusion.refs_0_.side_ref, bf16[4,384,384]{2,1,0:T(8,128)(2,1)S(1)} %bitcast.50, bf16[1536,1536]{1,0:T(8,128)(2,1)S(1)} %bitcast.49, bf16[1536,1536]{1,0:T(8,128)(2,1)} %bitcast.45), custom_call_target="tpu_custom_call" | custom-call | tf_op jit(solution)/shard_map/fold/outward/pallas_call | solution.py:160
  26.5 2.5 %collective-permute-start.1 = (bf16[192,1536]{1,0:T(8,128)(2,1)S(1)}, bf16[192,1536]{1,0:T(8,128)(2,1)S(1)}, u32[]{:S(2)}, u32[]{:S(2)}) collective-permute-start(bf16[192,1536]{1,0:T(8,128)(2,1)S(1)} %get-tuple-element.45), channel_id=1, source_target_pairs={{0,3},{1,2},{2,1},{3,0},{4,7},{5,6},{6,5},{7,4},{8,11},{9,10},{10,... | collective-permute-start | bytes 1769480 | tf_op jit(solution)/shard_map/sum_x/ppermute | solution.py:117
  29.0 11.9 %fold.1 = bf16[3,384,1536]{2,1,0:T(8,128)(2,1)S(1)} custom-call(s32[2]{0:T(128)S(1)} %pad_add_fusion.refs_0_.side_ref, bf16[1536,1536]{1,0:T(8,128)(2,1)S(1)} %bitcast.48, bf16[1536,1536]{1,0:T(8,128)(2,1)S(1)} %get-tuple-element.22.outward_ref.refs_2_), custom_call_target="tpu_custom_call" | custom-call | tf_op jit(solution)/shard_map/fold/fold/pallas_call | solution.py:199
  40.9 2.2 %copy-done = bf16[1536,1536]{1,0:T(8,128)(2,1)} copy-done((bf16[1536,1536]{1,0:T(8,128)(2,1)}, bf16[1536,1536]{1,0:T(8,128)(2,1)S(1)}, u32[]{:S(2)}) %copy-start) | copy-done | bytes 4718616
  43.2 4.7 %collective-permute-done.1 = bf16[192,1536]{1,0:T(8,128)(2,1)S(1)} collective-permute-done((bf16[192,1536]{1,0:T(8,128)(2,1)S(1)}, bf16[192,1536]{1,0:T(8,128)(2,1)S(1)}, u32[]{:S(2)}, u32[]{:S(2)}) %collective-permute-start.1) | collective-permute-done | bytes 589856 | tf_op jit(solution)/shard_map/sum_x/ppermute | solution.py:117
  48.2 1.6 pad_maximum_fusion.1
  49.7 1.1 collective-permute-start.5
  50.8 4.5 %source.1 = (f32[16,1536]{1,0:T(8,128)}, f32[16,1536]{1,0:T(8,128)}) custom-call(bf16[1024,512]{1,0:T(8,128)(2,1)} %bitcast.4.refs_0_, f32[16,4,384]{2,1,0:T(4,128)} %bitcast.53, bf16[1536,1536]{1,0:T(8,128)(2,1)} %copy-done), custom_call_target="tpu_custom_call" | custom-call | tf_op jit(solution)/shard_map/source/source/pallas_call | solution.py:239
  55.3 1.5 convert_element_type.210
  56.8 1.6 collective-permute-start.4
  58.4 1.0 collective-permute-start.3
  59.4 0.6 collective-permute-start.2
  60.1 18.3 %collective-permute-done.4 = bf16[16,1536]{1,0:T(8,128)(2,1)} collective-permute-done((bf16[16,1536]{1,0:T(8,128)(2,1)}, bf16[16,1536]{1,0:T(8,128)(2,1)}, u32[]{:S(2)}, u32[]{:S(2)}) %collective-permute-start.4) | collective-permute-done | bytes 49184 | tf_op jit(solution)/shard_map/sum_source/ppermute | solution.py:117
  78.4 1.6 add_convert_fusion.7
  80.0 2.1 %fusion.1 = bf16[384,1536]{1,0:T(8,128)(2,1)S(1)} fusion(bf16[384,1536]{1,0:T(8,128)(2,1)} %collective-permute-done.6, bf16[384,1536]{1,0:T(8,128)(2,1)} %collective-permute-done.5, bf16[3,384,1536]{2,1,0:T(8,128)(2,1)S(1)} %fold.1), kind=kLoop, calls=%fused_computation.2 | loop fusion | flops 3538944 | bytes 4718592 | tf_op jit(solution)/shard_map/sum_x/convert_element_type | solution.py:236
  82.4 1.8 collective-permute-start.17
  84.1 3.7 %collective-permute-done.7 = bf16[96,1536]{1,0:T(8,128)(2,1)S(1)} collective-permute-done((bf16[96,1536]{1,0:T(8,128)(2,1)S(1)}, bf16[96,1536]{1,0:T(8,128)(2,1)S(1)}, u32[]{:S(2)}, u32[]{:S(2)}) %collective-permute-start.7) | collective-permute-done | bytes 294944 | tf_op jit(solution)/shard_map/sum_z/ppermute | solution.py:117
  87.9 2.7 %collective-permute-start.10 = (bf16[16,1536]{1,0:T(8,128)(2,1)S(1)}, bf16[16,1536]{1,0:T(8,128)(2,1)S(1)}, u32[]{:S(2)}, u32[]{:S(2)}) collective-permute-start(bf16[16,1536]{1,0:T(8,128)(2,1)S(1)} %copy-done.4), channel_id=1, source_target_pairs={{0,12},{1,13},{2,14},{3,15},{4,8},{5,9},{6,10},{7,11},{8,4},{9,5},... | collective-permute-start | bytes 147464 | tf_op jit(solution)/shard_map/sum_z/ppermute | solution.py:117
  90.7 0.4 collective-permute-start.9
  91.0 0.5 collective-permute-start.8
  91.6 1.5 collective-permute-start.11
  93.2 1.2 collective-permute-start.18
  94.3 1.0 collective-permute-done.9
  95.4 1.6 collective-permute-done.11
  97.1 1.3 collective-permute-start.12
  98.4 3.2 %collective-permute-start.19 = (bf16[48,1536]{1,0:T(8,128)(2,1)S(1)}, bf16[48,1536]{1,0:T(8,128)(2,1)S(1)}, u32[]{:S(2)}, u32[]{:S(2)}) collective-permute-start(bf16[48,1536]{1,0:T(8,128)(2,1)S(1)} %add_convert_fusion.3), channel_id=1, source_target_pairs={{0,20},{1,21},{2,22},{3,23},{4,16},{5,17},{6,18},{7,19},{8,28},{9,... | collective-permute-start | bytes 442376 | tf_op jit(solution)/shard_map/sum_z/ppermute | solution.py:117
  101.6 2.0 %collective-permute-start.14 = (bf16[48,1536]{1,0:T(8,128)(2,1)S(1)}, bf16[48,1536]{1,0:T(8,128)(2,1)S(1)}, u32[]{:S(2)}, u32[]{:S(2)}) collective-permute-start(bf16[48,1536]{1,0:T(8,128)(2,1)S(1)} %add_convert_fusion.5), channel_id=1, source_target_pairs={{0,12},{1,13},{2,14},{3,15},{4,24},{5,25},{6,26},{7,27},{8,20},{9,... | collective-permute-start | bytes 442376 | tf_op jit(solution)/shard_map/sum_z/ppermute | solution.py:117
  103.7 6.9 %collective-permute-start.13 = (bf16[16,384]{1,0:T(8,128)(2,1)S(1)}, bf16[16,384]{1,0:T(8,128)(2,1)S(1)}, u32[]{:S(2)}, u32[]{:S(2)}) collective-permute-start(bf16[16,384]{1,0:T(8,128)(2,1)S(1)} %dynamic-slice_convert_fusion), channel_id=1, source_target_pairs={{0,32},{1,33},{2,34},{3,35},{4,36},{5,37},{6,38},{7,39},{8,40},{9,... | collective-permute-start | bytes 36872 | tf_op jit(solution)/shard_map/stage0/ppermute | solution.py:117
  110.7 3.8 %collective-permute-start.20 = (bf16[48,1536]{1,0:T(8,128)(2,1)S(1)}, bf16[48,1536]{1,0:T(8,128)(2,1)S(1)}, u32[]{:S(2)}, u32[]{:S(2)}) collective-permute-start(bf16[48,1536]{1,0:T(8,128)(2,1)S(1)} %add_convert_fusion.2), channel_id=1, source_target_pairs={{0,4},{1,5},{2,6},{3,7},{4,0},{5,1},{6,2},{7,3},{8,12},{9,13},{10,... | collective-permute-start | bytes 442376 | tf_op jit(solution)/shard_map/sum_z/ppermute | solution.py:117
  114.8 4.0 %collective-permute-done.20 = bf16[48,1536]{1,0:T(8,128)(2,1)S(1)} collective-permute-done((bf16[48,1536]{1,0:T(8,128)(2,1)S(1)}, bf16[48,1536]{1,0:T(8,128)(2,1)S(1)}, u32[]{:S(2)}, u32[]{:S(2)}) %collective-permute-start.20) | collective-permute-done | bytes 147488 | tf_op jit(solution)/shard_map/sum_z/ppermute | solution.py:117
  118.8 1.2 collective-permute-start.21
  120.1 0.4 collective-permute-done.15
  120.7 5.5 %collective-permute-done.21 = bf16[96,1536]{1,0:T(8,128)(2,1)S(1)} collective-permute-done((bf16[96,1536]{1,0:T(8,128)(2,1)S(1)}, bf16[96,1536]{1,0:T(8,128)(2,1)S(1)}, u32[]{:S(2)}, u32[]{:S(2)}) %collective-permute-start.21) | collective-permute-done | bytes 294944 | tf_op jit(solution)/shard_map/sum_z/ppermute | solution.py:117
  126.8 10.1 %collective-permute-start.25 = (bf16[16,1536]{1,0:T(8,128)(2,1)S(1)}, bf16[16,1536]{1,0:T(8,128)(2,1)S(1)}, u32[]{:S(2)}, u32[]{:S(2)}) collective-permute-start(bf16[16,1536]{1,0:T(8,128)(2,1)S(1)} %fusion.3), channel_id=1, source_target_pairs={{0,227},{1,226},{2,225},{3,224},{4,231},{5,230},{6,229},{7,228},{8... | collective-permute-start | bytes 147464 | tf_op jit(solution)/shard_map/stage1/ppermute | solution.py:117
  137.0 1.4 collective-permute-start.23
  138.4 0.6 collective-permute-start.22
  139.2 0.8 collective-permute-done.25
  140.0 2.9 %collective-permute-done.24 = bf16[16,1536]{1,0:T(8,128)(2,1)S(1)} collective-permute-done((bf16[16,1536]{1,0:T(8,128)(2,1)S(1)}, bf16[16,1536]{1,0:T(8,128)(2,1)S(1)}, u32[]{:S(2)}, u32[]{:S(2)}) %collective-permute-start.24) | collective-permute-done | bytes 49184 | tf_op jit(solution)/shard_map/stage1/ppermute | solution.py:117
  143.1 1.1 collective-permute-start.26
  144.2 0.8 collective-permute-done.26
  145.3 2.5 %collective-permute-start.30 = (bf16[16,1536]{1,0:T(8,128)(2,1)S(1)}, bf16[16,1536]{1,0:T(8,128)(2,1)S(1)}, u32[]{:S(2)}, u32[]{:S(2)}) collective-permute-start(bf16[16,1536]{1,0:T(8,128)(2,1)S(1)} %fusion.4), channel_id=1, source_target_pairs={{0,227},{1,226},{2,225},{3,224},{4,231},{5,230},{6,229},{7,228},{8... | collective-permute-start | bytes 147464 | tf_op jit(solution)/shard_map/stage3/ppermute | solution.py:117
  147.8 1.7 collective-permute-start.29
  149.6 0.7 collective-permute-start.28
  150.2 1.0 collective-permute-start.27
  151.3 3.2 %collective-permute-done.29 = bf16[16,1536]{1,0:T(8,128)(2,1)S(1)} collective-permute-done((bf16[16,1536]{1,0:T(8,128)(2,1)S(1)}, bf16[16,1536]{1,0:T(8,128)(2,1)S(1)}, u32[]{:S(2)}, u32[]{:S(2)}) %collective-permute-start.29) | collective-permute-done | bytes 49184 | tf_op jit(solution)/shard_map/stage3/ppermute | solution.py:117
  155.1 4.0 %collective-permute-start.31 = (bf16[16,384]{1,0:T(8,128)(2,1)S(1)}, bf16[16,384]{1,0:T(8,128)(2,1)S(1)}, u32[]{:S(2)}, u32[]{:S(2)}) collective-permute-start(bf16[16,384]{1,0:T(8,128)(2,1)S(1)} %fusion.9), channel_id=1, source_target_pairs={{0,32},{1,33},{2,34},{3,35},{4,36},{5,37},{6,38},{7,39},{8,40},{9,... | collective-permute-start | bytes 36872 | tf_op jit(solution)/shard_map/stage4/ppermute | solution.py:117
  159.1 0.8 collective-permute-done.31
  160.2 2.8 %collective-permute-start.34 = (bf16[16,1536]{1,0:T(8,128)(2,1)S(1)}, bf16[16,1536]{1,0:T(8,128)(2,1)S(1)}, u32[]{:S(2)}, u32[]{:S(2)}) collective-permute-start(bf16[16,1536]{1,0:T(8,128)(2,1)S(1)} %fusion.5), channel_id=1, source_target_pairs={{0,226},{1,227},{2,224},{3,225},{4,230},{5,231},{6,228},{7,229},{8... | collective-permute-start | bytes 147464 | tf_op jit(solution)/shard_map/stage5/ppermute | solution.py:117
  163.0 1.5 collective-permute-start.33
  164.5 1.6 collective-permute-start.32
  166.1 0.4 collective-permute-done.35
  166.8 0.7 collective-permute-done.33
  167.4 0.9 collective-permute-done.32
  168.7 3.0 %collective-permute-start.36 = (bf16[16,384]{1,0:T(8,128)(2,1)S(1)}, bf16[16,384]{1,0:T(8,128)(2,1)S(1)}, u32[]{:S(2)}, u32[]{:S(2)}) collective-permute-start(bf16[16,384]{1,0:T(8,128)(2,1)S(1)} %fusion.10), channel_id=1, source_target_pairs={{0,32},{1,33},{2,34},{3,35},{4,36},{5,37},{6,38},{7,39},{8,40},{9,... | collective-permute-start | bytes 36872 | tf_op jit(solution)/shard_map/spread/ppermute | solution.py:117
  171.6 1.1 collective-permute-start.37
  172.8 2.7 %collective-permute-start.38 = (bf16[16,384]{1,0:T(8,128)(2,1)S(1)}, bf16[16,384]{1,0:T(8,128)(2,1)S(1)}, u32[]{:S(2)}, u32[]{:S(2)}) collective-permute-start(bf16[16,384]{1,0:T(8,128)(2,1)S(1)} %fusion.10), channel_id=1, source_target_pairs={{0,34},{1,35},{2,32},{3,33},{4,38},{5,39},{6,36},{7,37},{8,42},{9,... | collective-permute-start | bytes 36872 | tf_op jit(solution)/shard_map/spread/ppermute | solution.py:117
  175.5 0.4 collective-permute-start.39
  175.9 1.5 collective-permute-done.38
  177.4 2.4 %collective-permute-done.39 = bf16[16,384]{1,0:T(8,128)(2,1)S(1)} collective-permute-done((bf16[16,384]{1,0:T(8,128)(2,1)S(1)}, bf16[16,384]{1,0:T(8,128)(2,1)S(1)}, u32[]{:S(2)}, u32[]{:S(2)}) %collective-permute-start.39) | collective-permute-done | bytes 12320 | tf_op jit(solution)/shard_map/spread/ppermute | solution.py:117
  179.8 3.1 %fusion.2 = bf16[16,1536]{1,0:T(8,128)(2,1)S(1)} fusion(f32[16,1536]{1,0:T(8,128)S(1)} %copy-done.5, bf16[16,1536]{1,0:T(8,128)(2,1)S(1)} %constant_dynamic-update-slice_fusion, bf16[16,1536]{1,0:T(8,128)(2,1)S(1)} %select_convert_fusion, pred[]{:T(512)S(6)} %eq.14, bf16[1,1536,1536]{2,1,0:T(8,128)(2,1)} %param.12), kind=kOutput, calls=%fused_computation.7 | convolution fusion | flops 75571200 | bytes 4964353 | tf_op jit(solution)/shard_map/solve/dot_general | solution.py:324
  183.3 0.7 copy.9
  (85 shorter events, 4.7 us)
Async XLA Ops:
  3.2 12.2 %copy-start.2 = (bf16[1,4,384,384]{3,2,1,0:T(8,128)(2,1)S(1)}, bf16[1,4,384,384]{3,2,1,0:T(8,128)(2,1)}, u32[]{:S(2)}) copy-start(bf16[1,4,384,384]{3,2,1,0:T(8,128)(2,1)} %param.11) | copy-start | bytes 3538948
  3.3 46.5 %all-to-all-start = ((bf16[32,32,512]{2,1,0:T(8,128)(2,1)}), bf16[32,32,512]{2,1,0:T(8,128)(2,1)}, u32[]{:S(2)}, u32[]{:S(2)}) async-start(bf16[32,32,512]{2,1,0:T(8,128)(2,1)} %bitcast.51), calls=%async_computation | async-start | bytes 2097152 | tf_op jit(solution)/shard_map/route/all_to_all | solution.py:146
  15.5 13.5 %slice-start = ((s8[4718592]{0:T(1024)(128)(4,1)}), s8[4194304]{0:T(1024)(128)(4,1)S(1)}, s32[]{:S(2)}) async-start(s8[4718592]{0:T(1024)(128)(4,1)} %bitcast.46), calls=%async_computation.1 | async-start | bytes 8388608
  15.5 2.5 %copy-start.1 = (bf16[1,1536,1536]{2,1,0:T(8,128)(2,1)S(1)}, bf16[1,1536,1536]{2,1,0:T(8,128)(2,1)}, u32[]{:S(2)}) copy-start(bf16[1,1536,1536]{2,1,0:T(8,128)(2,1)} %param.13) | copy-start | bytes 14155780
  18.0 11.0 %slice-start.1 = ((s8[4718592]{0:T(1024)(128)(4,1)}), s8[524288]{0:T(1024)(128)(4,1)S(1)}, s32[]{:S(2)}) async-start(s8[4718592]{0:T(1024)(128)(4,1)} %bitcast.46), calls=%async_computation.2 | async-start | bytes 1048576
  26.5 21.3 %collective-permute-start.1 = (bf16[192,1536]{1,0:T(8,128)(2,1)S(1)}, bf16[192,1536]{1,0:T(8,128)(2,1)S(1)}, u32[]{:S(2)}, u32[]{:S(2)}) collective-permute-start(bf16[192,1536]{1,0:T(8,128)(2,1)S(1)} %get-tuple-element.45), channel_id=1, source_target_pairs={{0,3},{1,2},{2,1},{3,0},{4,7},{5,6},{6,5},{7,4},{8,11},{9,10},{10,... | collective-permute-start | bytes 1769480 | tf_op jit(solution)/shard_map/sum_x/ppermute | solution.py:117
  29.0 18.9 %collective-permute-start = (bf16[192,1536]{1,0:T(8,128)(2,1)S(1)}, bf16[192,1536]{1,0:T(8,128)(2,1)S(1)}, u32[]{:S(2)}, u32[]{:S(2)}) collective-permute-start(bf16[192,1536]{1,0:T(8,128)(2,1)S(1)} %get-tuple-element.46), channel_id=1, source_target_pairs={{0,1},{1,0},{2,3},{3,2},{4,5},{5,4},{6,7},{7,6},{8,9},{9,8},{10,11... | collective-permute-start | bytes 1769480 | tf_op jit(solution)/shard_map/sum_x/ppermute | solution.py:117
  40.9 2.2 %copy-start = (bf16[1536,1536]{1,0:T(8,128)(2,1)}, bf16[1536,1536]{1,0:T(8,128)(2,1)S(1)}, u32[]{:S(2)}) copy-start(bf16[1536,1536]{1,0:T(8,128)(2,1)S(1)} %get-tuple-element.22.outward_ref.refs_2_) | copy-start | bytes 14155780
  49.7 30.3 %collective-permute-start.6 = (bf16[384,1536]{1,0:T(8,128)(2,1)}, bf16[384,1536]{1,0:T(8,128)(2,1)}, u32[]{:S(2)}, u32[]{:S(2)}) collective-permute-start(bf16[384,1536]{1,0:T(8,128)(2,1)} %get-tuple-element.28), channel_id=1, source_target_pairs={{0,1},{1,0},{2,3},{3,2},{4,5},{5,4},{6,7},{7,6},{8,9},{9,8},{10,11... | collective-permute-start | bytes 3538952 | tf_op jit(solution)/shard_map/sum_x/ppermute | solution.py:117
  49.7 30.3 %collective-permute-start.5 = (bf16[384,1536]{1,0:T(8,128)(2,1)}, bf16[384,1536]{1,0:T(8,128)(2,1)}, u32[]{:S(2)}, u32[]{:S(2)}) collective-permute-start(bf16[384,1536]{1,0:T(8,128)(2,1)} %get-tuple-element.27), channel_id=1, source_target_pairs={{0,3},{1,2},{2,1},{3,0},{4,7},{5,6},{6,5},{7,4},{8,11},{9,10},{10,... | collective-permute-start | bytes 3538952 | tf_op jit(solution)/shard_map/sum_x/ppermute | solution.py:117
  56.8 21.6 %collective-permute-start.4 = (bf16[16,1536]{1,0:T(8,128)(2,1)}, bf16[16,1536]{1,0:T(8,128)(2,1)}, u32[]{:S(2)}, u32[]{:S(2)}) collective-permute-start(bf16[16,1536]{1,0:T(8,128)(2,1)} %convert_element_type.210), channel_id=1, source_target_pairs={{0,3},{1,2},{2,1},{3,0},{4,7},{5,6},{6,5},{7,4},{8,11},{9,10},{10,... | collective-permute-start | bytes 147464 | tf_op jit(solution)/shard_map/sum_source/ppermute | solution.py:117
  58.4 19.9 %collective-permute-start.3 = (bf16[16,1536]{1,0:T(8,128)(2,1)}, bf16[16,1536]{1,0:T(8,128)(2,1)}, u32[]{:S(2)}, u32[]{:S(2)}) collective-permute-start(bf16[16,1536]{1,0:T(8,128)(2,1)} %convert_element_type.210), channel_id=1, source_target_pairs={{0,2},{1,3},{2,0},{3,1},{4,6},{5,7},{6,4},{7,5},{8,10},{9,11},{10,... | collective-permute-start | bytes 147464 | tf_op jit(solution)/shard_map/sum_source/ppermute | solution.py:117
  59.4 18.9 %collective-permute-start.2 = (bf16[16,1536]{1,0:T(8,128)(2,1)}, bf16[16,1536]{1,0:T(8,128)(2,1)}, u32[]{:S(2)}, u32[]{:S(2)}) collective-permute-start(bf16[16,1536]{1,0:T(8,128)(2,1)} %convert_element_type.210), channel_id=1, source_target_pairs={{0,1},{1,0},{2,3},{3,2},{4,5},{5,4},{6,7},{7,6},{8,9},{9,8},{10,11... | collective-permute-start | bytes 147464 | tf_op jit(solution)/shard_map/sum_source/ppermute | solution.py:117
  82.1 5.8 %copy-start.4 = (bf16[16,1536]{1,0:T(8,128)(2,1)S(1)}, bf16[16,1536]{1,0:T(8,128)(2,1)}, u32[]{:S(2)}) copy-start(bf16[16,1536]{1,0:T(8,128)(2,1)} %add_convert_fusion.7) | copy-start | bytes 147460
  82.2 5.7 %collective-permute-start.7 = (bf16[96,1536]{1,0:T(8,128)(2,1)S(1)}, bf16[96,1536]{1,0:T(8,128)(2,1)S(1)}, u32[]{:S(2)}, u32[]{:S(2)}) collective-permute-start(bf16[96,1536]{1,0:T(8,128)(2,1)S(1)} %constant_dynamic-slice_fusion.3), channel_id=1, source_target_pairs={{0,4},{1,5},{2,6},{3,7},{4,0},{5,1},{6,2},{7,3},{8,12},{9,13},{10,... | collective-permute-start | bytes 884744 | tf_op jit(solution)/shard_map/sum_z/ppermute | solution.py:117
  82.4 10.7 %collective-permute-start.17 = (bf16[96,1536]{1,0:T(8,128)(2,1)S(1)}, bf16[96,1536]{1,0:T(8,128)(2,1)S(1)}, u32[]{:S(2)}, u32[]{:S(2)}) collective-permute-start(bf16[96,1536]{1,0:T(8,128)(2,1)S(1)} %constant_dynamic-slice_fusion.1), channel_id=1, source_target_pairs={{0,28},{1,29},{2,30},{3,31},{4,8},{5,9},{6,10},{7,11},{8,4},{9,5},... | collective-permute-start | bytes 884744 | tf_op jit(solution)/shard_map/sum_z/ppermute | solution.py:117
  87.9 6.4 %collective-permute-start.10 = (bf16[16,1536]{1,0:T(8,128)(2,1)S(1)}, bf16[16,1536]{1,0:T(8,128)(2,1)S(1)}, u32[]{:S(2)}, u32[]{:S(2)}) collective-permute-start(bf16[16,1536]{1,0:T(8,128)(2,1)S(1)} %copy-done.4), channel_id=1, source_target_pairs={{0,12},{1,13},{2,14},{3,15},{4,8},{5,9},{6,10},{7,11},{8,4},{9,5},... | collective-permute-start | bytes 147464 | tf_op jit(solution)/shard_map/sum_z/ppermute | solution.py:117
  90.7 4.7 %collective-permute-start.9 = (bf16[16,1536]{1,0:T(8,128)(2,1)S(1)}, bf16[16,1536]{1,0:T(8,128)(2,1)S(1)}, u32[]{:S(2)}, u32[]{:S(2)}) collective-permute-start(bf16[16,1536]{1,0:T(8,128)(2,1)S(1)} %copy-done.4), channel_id=1, source_target_pairs={{0,8},{1,9},{2,10},{3,11},{4,12},{5,13},{6,14},{7,15},{8,0},{9,1},... | collective-permute-start | bytes 147464 | tf_op jit(solution)/shard_map/sum_z/ppermute | solution.py:117
  91.0 4.3 %collective-permute-start.8 = (bf16[16,1536]{1,0:T(8,128)(2,1)S(1)}, bf16[16,1536]{1,0:T(8,128)(2,1)S(1)}, u32[]{:S(2)}, u32[]{:S(2)}) collective-permute-start(bf16[16,1536]{1,0:T(8,128)(2,1)S(1)} %copy-done.4), channel_id=1, source_target_pairs={{0,4},{1,5},{2,6},{3,7},{4,0},{5,1},{6,2},{7,3},{8,12},{9,13},{10,... | collective-permute-start | bytes 147464 | tf_op jit(solution)/shard_map/sum_z/ppermute | solution.py:117
  91.6 5.5 %collective-permute-start.11 = (bf16[48,1536]{1,0:T(8,128)(2,1)S(1)}, bf16[48,1536]{1,0:T(8,128)(2,1)S(1)}, u32[]{:S(2)}, u32[]{:S(2)}) collective-permute-start(bf16[48,1536]{1,0:T(8,128)(2,1)S(1)} %constant_dynamic-slice_fusion.2), channel_id=1, source_target_pairs={{0,28},{1,29},{2,30},{3,31},{4,8},{5,9},{6,10},{7,11},{8,4},{9,5},... | collective-permute-start | bytes 442376 | tf_op jit(solution)/shard_map/sum_z/ppermute | solution.py:117
  93.2 5.2 %collective-permute-start.18 = (bf16[48,1536]{1,0:T(8,128)(2,1)S(1)}, bf16[48,1536]{1,0:T(8,128)(2,1)S(1)}, u32[]{:S(2)}, u32[]{:S(2)}) collective-permute-start(bf16[48,1536]{1,0:T(8,128)(2,1)S(1)} %constant_dynamic-slice_fusion), channel_id=1, source_target_pairs={{0,4},{1,5},{2,6},{3,7},{4,0},{5,1},{6,2},{7,3},{8,12},{9,13},{10,... | collective-permute-start | bytes 442376 | tf_op jit(solution)/shard_map/sum_z/ppermute | solution.py:117
  97.1 6.6 %collective-permute-start.12 = (bf16[16,1536]{1,0:T(8,128)(2,1)S(1)}, bf16[16,1536]{1,0:T(8,128)(2,1)S(1)}, u32[]{:S(2)}, u32[]{:S(2)}) collective-permute-start(bf16[16,1536]{1,0:T(8,128)(2,1)S(1)} %add_convert_fusion.6), channel_id=1, source_target_pairs={{0,28},{1,29},{2,30},{3,31},{4,24},{5,25},{6,26},{7,27},{8,20},{9,... | collective-permute-start | bytes 147464 | tf_op jit(solution)/shard_map/sum_z/ppermute | solution.py:117
  98.4 12.2 %collective-permute-start.19 = (bf16[48,1536]{1,0:T(8,128)(2,1)S(1)}, bf16[48,1536]{1,0:T(8,128)(2,1)S(1)}, u32[]{:S(2)}, u32[]{:S(2)}) collective-permute-start(bf16[48,1536]{1,0:T(8,128)(2,1)S(1)} %add_convert_fusion.3), channel_id=1, source_target_pairs={{0,20},{1,21},{2,22},{3,23},{4,16},{5,17},{6,18},{7,19},{8,28},{9,... | collective-permute-start | bytes 442376 | tf_op jit(solution)/shard_map/sum_z/ppermute | solution.py:117
  101.6 12.9 %collective-permute-start.14 = (bf16[48,1536]{1,0:T(8,128)(2,1)S(1)}, bf16[48,1536]{1,0:T(8,128)(2,1)S(1)}, u32[]{:S(2)}, u32[]{:S(2)}) collective-permute-start(bf16[48,1536]{1,0:T(8,128)(2,1)S(1)} %add_convert_fusion.5), channel_id=1, source_target_pairs={{0,12},{1,13},{2,14},{3,15},{4,24},{5,25},{6,26},{7,27},{8,20},{9,... | collective-permute-start | bytes 442376 | tf_op jit(solution)/shard_map/sum_z/ppermute | solution.py:117
  103.7 22.8 %collective-permute-start.13 = (bf16[16,384]{1,0:T(8,128)(2,1)S(1)}, bf16[16,384]{1,0:T(8,128)(2,1)S(1)}, u32[]{:S(2)}, u32[]{:S(2)}) collective-permute-start(bf16[16,384]{1,0:T(8,128)(2,1)S(1)} %dynamic-slice_convert_fusion), channel_id=1, source_target_pairs={{0,32},{1,33},{2,34},{3,35},{4,36},{5,37},{6,38},{7,39},{8,40},{9,... | collective-permute-start | bytes 36872 | tf_op jit(solution)/shard_map/stage0/ppermute | solution.py:117
  110.7 8.1 %collective-permute-start.20 = (bf16[48,1536]{1,0:T(8,128)(2,1)S(1)}, bf16[48,1536]{1,0:T(8,128)(2,1)S(1)}, u32[]{:S(2)}, u32[]{:S(2)}) collective-permute-start(bf16[48,1536]{1,0:T(8,128)(2,1)S(1)} %add_convert_fusion.2), channel_id=1, source_target_pairs={{0,4},{1,5},{2,6},{3,7},{4,0},{5,1},{6,2},{7,3},{8,12},{9,13},{10,... | collective-permute-start | bytes 442376 | tf_op jit(solution)/shard_map/sum_z/ppermute | solution.py:117
  114.6 5.9 %collective-permute-start.15 = (bf16[48,1536]{1,0:T(8,128)(2,1)S(1)}, bf16[48,1536]{1,0:T(8,128)(2,1)S(1)}, u32[]{:S(2)}, u32[]{:S(2)}) collective-permute-start(bf16[48,1536]{1,0:T(8,128)(2,1)S(1)} %add_convert_fusion.4), channel_id=1, source_target_pairs={{0,28},{1,29},{2,30},{3,31},{4,8},{5,9},{6,10},{7,11},{8,4},{9,5},... | collective-permute-start | bytes 442376 | tf_op jit(solution)/shard_map/sum_z/ppermute | solution.py:117
  118.8 7.4 %collective-permute-start.21 = (bf16[96,1536]{1,0:T(8,128)(2,1)S(1)}, bf16[96,1536]{1,0:T(8,128)(2,1)S(1)}, u32[]{:S(2)}, u32[]{:S(2)}) collective-permute-start(bf16[96,1536]{1,0:T(8,128)(2,1)S(1)} %constant_dynamic-update-slice_fusion.5), channel_id=1, source_target_pairs={{0,28},{1,29},{2,30},{3,31},{4,8},{5,9},{6,10},{7,11},{8,4},{9,5},... | collective-permute-start | bytes 884744 | tf_op jit(solution)/shard_map/sum_z/ppermute | solution.py:117
  120.6 6.0 %collective-permute-start.16 = (bf16[96,1536]{1,0:T(8,128)(2,1)S(1)}, bf16[96,1536]{1,0:T(8,128)(2,1)S(1)}, u32[]{:S(2)}, u32[]{:S(2)}) collective-permute-start(bf16[96,1536]{1,0:T(8,128)(2,1)S(1)} %constant_dynamic-update-slice_fusion.7), channel_id=1, source_target_pairs={{0,4},{1,5},{2,6},{3,7},{4,0},{5,1},{6,2},{7,3},{8,12},{9,13},{10,... | collective-permute-start | bytes 884744 | tf_op jit(solution)/shard_map/sum_z/ppermute | solution.py:117
  126.8 13.1 %collective-permute-start.25 = (bf16[16,1536]{1,0:T(8,128)(2,1)S(1)}, bf16[16,1536]{1,0:T(8,128)(2,1)S(1)}, u32[]{:S(2)}, u32[]{:S(2)}) collective-permute-start(bf16[16,1536]{1,0:T(8,128)(2,1)S(1)} %fusion.3), channel_id=1, source_target_pairs={{0,227},{1,226},{2,225},{3,224},{4,231},{5,230},{6,229},{7,228},{8... | collective-permute-start | bytes 147464 | tf_op jit(solution)/shard_map/stage1/ppermute | solution.py:117
  136.9 5.9 %collective-permute-start.24 = (bf16[16,1536]{1,0:T(8,128)(2,1)S(1)}, bf16[16,1536]{1,0:T(8,128)(2,1)S(1)}, u32[]{:S(2)}, u32[]{:S(2)}) collective-permute-start(bf16[16,1536]{1,0:T(8,128)(2,1)S(1)} %fusion.3), channel_id=1, source_target_pairs={{0,226},{1,227},{2,224},{3,225},{4,230},{5,231},{6,228},{7,229},{8... | collective-permute-start | bytes 147464 | tf_op jit(solution)/shard_map/stage1/ppermute | solution.py:117
  137.0 5.8 %collective-permute-start.23 = (bf16[16,1536]{1,0:T(8,128)(2,1)S(1)}, bf16[16,1536]{1,0:T(8,128)(2,1)S(1)}, u32[]{:S(2)}, u32[]{:S(2)}) collective-permute-start(bf16[16,1536]{1,0:T(8,128)(2,1)S(1)} %fusion.3), channel_id=1, source_target_pairs={{0,225},{1,224},{2,227},{3,226},{4,229},{5,228},{6,231},{7,230},{8... | collective-permute-start | bytes 147464 | tf_op jit(solution)/shard_map/stage1/ppermute | solution.py:117
  138.4 4.4 %collective-permute-start.22 = (bf16[16,1536]{1,0:T(8,128)(2,1)S(1)}, bf16[16,1536]{1,0:T(8,128)(2,1)S(1)}, u32[]{:S(2)}, u32[]{:S(2)}) collective-permute-start(bf16[16,1536]{1,0:T(8,128)(2,1)S(1)} %fusion.3), channel_id=1, source_target_pairs={{0,224},{1,225},{2,226},{3,227},{4,228},{5,229},{6,230},{7,231},{8... | collective-permute-start | bytes 147464 | tf_op jit(solution)/shard_map/stage1/ppermute | solution.py:117
  143.1 1.9 %collective-permute-start.26 = (bf16[16,384]{1,0:T(8,128)(2,1)S(1)}, bf16[16,384]{1,0:T(8,128)(2,1)S(1)}, u32[]{:S(2)}, u32[]{:S(2)}) collective-permute-start(bf16[16,384]{1,0:T(8,128)(2,1)S(1)} %fusion.8), channel_id=1, source_target_pairs={{0,32},{1,33},{2,34},{3,35},{4,36},{5,37},{6,38},{7,39},{8,40},{9,... | collective-permute-start | bytes 36872 | tf_op jit(solution)/shard_map/stage2/ppermute | solution.py:117
  145.3 6.0 %collective-permute-start.30 = (bf16[16,1536]{1,0:T(8,128)(2,1)S(1)}, bf16[16,1536]{1,0:T(8,128)(2,1)S(1)}, u32[]{:S(2)}, u32[]{:S(2)}) collective-permute-start(bf16[16,1536]{1,0:T(8,128)(2,1)S(1)} %fusion.4), channel_id=1, source_target_pairs={{0,227},{1,226},{2,225},{3,224},{4,231},{5,230},{6,229},{7,228},{8... | collective-permute-start | bytes 147464 | tf_op jit(solution)/shard_map/stage3/ppermute | solution.py:117
  147.8 6.7 %collective-permute-start.29 = (bf16[16,1536]{1,0:T(8,128)(2,1)S(1)}, bf16[16,1536]{1,0:T(8,128)(2,1)S(1)}, u32[]{:S(2)}, u32[]{:S(2)}) collective-permute-start(bf16[16,1536]{1,0:T(8,128)(2,1)S(1)} %fusion.4), channel_id=1, source_target_pairs={{0,226},{1,227},{2,224},{3,225},{4,230},{5,231},{6,228},{7,229},{8... | collective-permute-start | bytes 147464 | tf_op jit(solution)/shard_map/stage3/ppermute | solution.py:117
  149.6 4.9 %collective-permute-start.28 = (bf16[16,1536]{1,0:T(8,128)(2,1)S(1)}, bf16[16,1536]{1,0:T(8,128)(2,1)S(1)}, u32[]{:S(2)}, u32[]{:S(2)}) collective-permute-start(bf16[16,1536]{1,0:T(8,128)(2,1)S(1)} %fusion.4), channel_id=1, source_target_pairs={{0,225},{1,224},{2,227},{3,226},{4,229},{5,228},{6,231},{7,230},{8... | collective-permute-start | bytes 147464 | tf_op jit(solution)/shard_map/stage3/ppermute | solution.py:117
  150.2 4.6 %collective-permute-start.27 = (bf16[16,1536]{1,0:T(8,128)(2,1)S(1)}, bf16[16,1536]{1,0:T(8,128)(2,1)S(1)}, u32[]{:S(2)}, u32[]{:S(2)}) collective-permute-start(bf16[16,1536]{1,0:T(8,128)(2,1)S(1)} %fusion.4), channel_id=1, source_target_pairs={{0,224},{1,225},{2,226},{3,227},{4,228},{5,229},{6,230},{7,231},{8... | collective-permute-start | bytes 147464 | tf_op jit(solution)/shard_map/stage3/ppermute | solution.py:117
  155.1 4.8 %collective-permute-start.31 = (bf16[16,384]{1,0:T(8,128)(2,1)S(1)}, bf16[16,384]{1,0:T(8,128)(2,1)S(1)}, u32[]{:S(2)}, u32[]{:S(2)}) collective-permute-start(bf16[16,384]{1,0:T(8,128)(2,1)S(1)} %fusion.9), channel_id=1, source_target_pairs={{0,32},{1,33},{2,34},{3,35},{4,36},{5,37},{6,38},{7,39},{8,40},{9,... | collective-permute-start | bytes 36872 | tf_op jit(solution)/shard_map/stage4/ppermute | solution.py:117
  160.2 6.4 %collective-permute-start.35 = (bf16[16,1536]{1,0:T(8,128)(2,1)S(1)}, bf16[16,1536]{1,0:T(8,128)(2,1)S(1)}, u32[]{:S(2)}, u32[]{:S(2)}) collective-permute-start(bf16[16,1536]{1,0:T(8,128)(2,1)S(1)} %fusion.5), channel_id=1, source_target_pairs={{0,227},{1,226},{2,225},{3,224},{4,231},{5,230},{6,229},{7,228},{8... | collective-permute-start | bytes 147464 | tf_op jit(solution)/shard_map/stage5/ppermute | solution.py:117
  160.2 6.6 %collective-permute-start.34 = (bf16[16,1536]{1,0:T(8,128)(2,1)S(1)}, bf16[16,1536]{1,0:T(8,128)(2,1)S(1)}, u32[]{:S(2)}, u32[]{:S(2)}) collective-permute-start(bf16[16,1536]{1,0:T(8,128)(2,1)S(1)} %fusion.5), channel_id=1, source_target_pairs={{0,226},{1,227},{2,224},{3,225},{4,230},{5,231},{6,228},{7,229},{8... | collective-permute-start | bytes 147464 | tf_op jit(solution)/shard_map/stage5/ppermute | solution.py:117
  163.0 4.4 %collective-permute-start.33 = (bf16[16,1536]{1,0:T(8,128)(2,1)S(1)}, bf16[16,1536]{1,0:T(8,128)(2,1)S(1)}, u32[]{:S(2)}, u32[]{:S(2)}) collective-permute-start(bf16[16,1536]{1,0:T(8,128)(2,1)S(1)} %fusion.5), channel_id=1, source_target_pairs={{0,225},{1,224},{2,227},{3,226},{4,229},{5,228},{6,231},{7,230},{8... | collective-permute-start | bytes 147464 | tf_op jit(solution)/shard_map/stage5/ppermute | solution.py:117
  164.5 3.8 %collective-permute-start.32 = (bf16[16,1536]{1,0:T(8,128)(2,1)S(1)}, bf16[16,1536]{1,0:T(8,128)(2,1)S(1)}, u32[]{:S(2)}, u32[]{:S(2)}) collective-permute-start(bf16[16,1536]{1,0:T(8,128)(2,1)S(1)} %fusion.5), channel_id=1, source_target_pairs={{0,224},{1,225},{2,226},{3,227},{4,228},{5,229},{6,230},{7,231},{8... | collective-permute-start | bytes 147464 | tf_op jit(solution)/shard_map/stage5/ppermute | solution.py:117
  168.4 11.4 %copy-start.5 = (f32[16,1536]{1,0:T(8,128)S(1)}, f32[16,1536]{1,0:T(8,128)}, u32[]{:S(2)}) copy-start(f32[16,1536]{1,0:T(8,128)} %get-tuple-element.25) | copy-start | bytes 294916
  168.7 7.2 %collective-permute-start.36 = (bf16[16,384]{1,0:T(8,128)(2,1)S(1)}, bf16[16,384]{1,0:T(8,128)(2,1)S(1)}, u32[]{:S(2)}, u32[]{:S(2)}) collective-permute-start(bf16[16,384]{1,0:T(8,128)(2,1)S(1)} %fusion.10), channel_id=1, source_target_pairs={{0,32},{1,33},{2,34},{3,35},{4,36},{5,37},{6,38},{7,39},{8,40},{9,... | collective-permute-start | bytes 36872 | tf_op jit(solution)/shard_map/spread/ppermute | solution.py:117
  171.6 4.2 %collective-permute-start.37 = (bf16[16,384]{1,0:T(8,128)(2,1)S(1)}, bf16[16,384]{1,0:T(8,128)(2,1)S(1)}, u32[]{:S(2)}, u32[]{:S(2)}) collective-permute-start(bf16[16,384]{1,0:T(8,128)(2,1)S(1)} %fusion.10), channel_id=1, source_target_pairs={{0,33},{1,32},{2,35},{3,34},{4,37},{5,36},{6,39},{7,38},{8,41},{9,... | collective-permute-start | bytes 36872 | tf_op jit(solution)/shard_map/spread/ppermute | solution.py:117
  172.8 4.6 %collective-permute-start.38 = (bf16[16,384]{1,0:T(8,128)(2,1)S(1)}, bf16[16,384]{1,0:T(8,128)(2,1)S(1)}, u32[]{:S(2)}, u32[]{:S(2)}) collective-permute-start(bf16[16,384]{1,0:T(8,128)(2,1)S(1)} %fusion.10), channel_id=1, source_target_pairs={{0,34},{1,35},{2,32},{3,33},{4,38},{5,39},{6,36},{7,37},{8,42},{9,... | collective-permute-start | bytes 36872 | tf_op jit(solution)/shard_map/spread/ppermute | solution.py:117
  175.5 4.3 %collective-permute-start.39 = (bf16[16,384]{1,0:T(8,128)(2,1)S(1)}, bf16[16,384]{1,0:T(8,128)(2,1)S(1)}, u32[]{:S(2)}, u32[]{:S(2)}) collective-permute-start(bf16[16,384]{1,0:T(8,128)(2,1)S(1)} %fusion.10), channel_id=1, source_target_pairs={{0,35},{1,34},{2,33},{3,32},{4,39},{5,38},{6,37},{7,36},{8,43},{9,... | collective-permute-start | bytes 36872 | tf_op jit(solution)/shard_map/spread/ppermute | solution.py:117
  179.8 3.2 %copy-start.3 = (bf16[1,4,384,384]{3,2,1,0:T(8,128)(2,1)S(1)}, bf16[1,4,384,384]{3,2,1,0:T(8,128)(2,1)}, u32[]{:S(2)}) copy-start(bf16[1,4,384,384]{3,2,1,0:T(8,128)(2,1)} %param.11) | copy-start | bytes 3538948

commit v5 on v4

--- a/solution.py
+++ b/solution.py
@@ -245,8 +245,9 @@
         )(got, face_rhs[0], outward)
     with jax.named_scope("sum_source"):
         part = source.astype(BF)
-        part = total([part] + [exchange(part, m) for m in range(1, x_count)]).astype(BF)
-        source_x, summed_x = lax.optimization_barrier((part, summed_x))
+        part = total([part] + [exchange(part, 0, m) for m in range(1, four)]).astype(BF)
+        part = total([part, exchange(part, 0, far)]).astype(BF)
+        source_parts = [part] + [exchange(part, m) for m in range(1, x_count)]
     with jax.named_scope("sum_z"):
         turns = [z ^ 1 for z in range(z_count)], [3, 6, 5, 0, 7, 2, 1, 4]
 
@@ -278,12 +279,7 @@
             got_rows = swap([given for _, given in split], turn)
             summed = [total([kept, new]).astype(BF) for (kept, _), new in zip(split, got_rows)]
             if turn == 0:
-                source_x, summed[0] = lax.optimization_barrier((source_x, summed[0]))
-                source_z = [source_x] + [exchange(source_x, 0, m) for m in range(1, four)]
-            else:
-                source_z = total(source_z).astype(BF)
-                source_z, summed[0] = lax.optimization_barrier((source_z, summed[0]))
-                source_far = exchange(source_z, 0, far)
+                source, summed[0] = lax.optimization_barrier((total(source_parts), summed[0]))
         summed = [total([rows, new]).astype(BF) for rows, new in zip(summed, swap(summed, 2))]
         for turn in (1, 0):
             got_rows = swap(summed, turn)
@@ -291,7 +287,6 @@
                 joined(rows, new, bit[turn]) for rows, new, bit in zip(summed, got_rows, bits)
             ]
         through = jnp.concatenate(summed, axis=0)
-        source = total([source_z, source_far])
         source_slab = lax.dynamic_slice_in_dim(source, here_x * slab, slab, 1)
         source_once = jnp.where(here_x == 0, source, 0.0)
     through_columns = jnp.concatenate(

time: 184 us -> 177 us (0.962)
  starting transfers between devices: 82.2 us -> 78.5 us
  waiting for transfers between devices: 54.7 us -> 51.2 us
    ppermute x40, starting transfers between devices: 70 us -> 66.3 us  [exchange(): return lax.ppermute(value, ('sweep', 'z', 'x'), pairs)]
    ppermute x40, waiting for transfers between devices: 54.7 us -> 51.2 us  [exchange(): return lax.ppermute(value, ('sweep', 'z', 'x'), pairs)]
    unnamed x16 -> x14, local copies, waits for them, and re-layouts: 4.69 us -> 4.69 us
  transfers between devices with their start and end apart: 41 -> 41, of which waited for: 21 -> 25; matrix products, arithmetic and copies ran while one was open for 3% -> 5% of each run, Pallas kernels for 14% -> 14%
where the time goes in v5:
time: 177 us
  starting transfers between devices  78.5 us (44%)
  waiting for transfers between devices  51.2 us (29%)
  Pallas kernels  28.1 us (16%)
  other arithmetic  7.87 us (4%)
  local copies, waits for them, and re-layouts  5.85 us (3%)
  matrix products  5.05 us (3%)
    ppermute x40, starting transfers between devices, exchange(): return lax.ppermute(value, ('sweep', 'z', 'x'), pairs)  66.3 us
    ppermute x40, waiting for transfers between devices, exchange(): return lax.ppermute(value, ('sweep', 'z', 'x'), pairs)  51.2 us
    all_to_all x1, starting transfers between devices, on_device(): lax.all_to_all(packed.reshape(group_size, capacity, width + LANES), ('z',...  12.1 us
    pallas_call x1, Pallas kernels, on_device(): pl.pallas_call(fold_kernel, grid_spec=pltpu.PrefetchScalarGridSpec(num_sc...  11.9 us
    pallas_call x1, Pallas kernels, on_device(): pl.pallas_call(lambda *refs: outward_kernel(face_dev, *refs), grid_spec=p...  8.46 us
    unnamed x14, local copies, waits for them, and re-layouts  4.69 us
    pallas_call x1, Pallas kernels, on_device(): pl.pallas_call(lambda *refs: source_kernel(face_dev, *refs), in_specs=[vm...  4.5 us
  transfers between devices with their start and end apart: 41, of which 25 were waited for; matrix products, arithmetic and copies ran while one was open for 5% of the time, Pallas kernels for 14%

profile of v5, /device:TPU:1, one launch (start us, length us, event | category | flops | bytes accessed | tf_op | source)
XLA Modules:
  0.0 176.8 jit_solution(11480799270147441204)
XLA Ops:
  0.0 3.3 %pack.1 = bf16[1024,512]{1,0:T(8,128)(2,1)} custom-call(s32[1,512]{1,0:T(1,128)} %bitcast.54, s32[1,512]{1,0:T(1,128)} %bitcast.55, f32[512,384]{1,0:T(8,128)} %refs_2_.1), custom_call_target="tpu_custom_call" | custom-call | tf_op jit(solution)/shard_map/pack/pack/pallas_call | solution.py:139
  3.3 12.1 %all-to-all-start = ((bf16[32,32,512]{2,1,0:T(8,128)(2,1)}), bf16[32,32,512]{2,1,0:T(8,128)(2,1)}, u32[]{:S(2)}, u32[]{:S(2)}) async-start(bf16[32,32,512]{2,1,0:T(8,128)(2,1)} %bitcast.51), calls=%async_computation | async-start | bytes 2097152 | tf_op jit(solution)/shard_map/route/all_to_all | solution.py:146
  15.5 2.5 %copy-done.1 = bf16[1,1536,1536]{2,1,0:T(8,128)(2,1)S(1)} copy-done((bf16[1,1536,1536]{2,1,0:T(8,128)(2,1)S(1)}, bf16[1,1536,1536]{2,1,0:T(8,128)(2,1)}, u32[]{:S(2)}) %copy-start.1) | copy-done | bytes 4718616
  18.0 8.5 %outward.1 = (bf16[1536,1536]{1,0:T(8,128)(2,1)S(1)}, bf16[384,1536]{1,0:T(8,128)(2,1)S(1)}) custom-call(s32[2]{0:T(128)S(1)} %pad_add_fusion.refs_0_.side_ref, bf16[4,384,384]{2,1,0:T(8,128)(2,1)S(1)} %bitcast.50, bf16[1536,1536]{1,0:T(8,128)(2,1)S(1)} %bitcast.49, bf16[1536,1536]{1,0:T(8,128)(2,1)} %bitcast.45), custom_call_target="tpu_custom_call" | custom-call | tf_op jit(solution)/shard_map/fold/outward/pallas_call | solution.py:160
  26.5 2.5 %collective-permute-start.1 = (bf16[192,1536]{1,0:T(8,128)(2,1)S(1)}, bf16[192,1536]{1,0:T(8,128)(2,1)S(1)}, u32[]{:S(2)}, u32[]{:S(2)}) collective-permute-start(bf16[192,1536]{1,0:T(8,128)(2,1)S(1)} %get-tuple-element.37), channel_id=1, source_target_pairs={{0,3},{1,2},{2,1},{3,0},{4,7},{5,6},{6,5},{7,4},{8,11},{9,10},{10,... | collective-permute-start | bytes 1769480 | tf_op jit(solution)/shard_map/sum_x/ppermute | solution.py:117
  29.0 11.9 %fold.1 = bf16[3,384,1536]{2,1,0:T(8,128)(2,1)S(1)} custom-call(s32[2]{0:T(128)S(1)} %pad_add_fusion.refs_0_.side_ref, bf16[1536,1536]{1,0:T(8,128)(2,1)S(1)} %bitcast.48, bf16[1536,1536]{1,0:T(8,128)(2,1)S(1)} %get-tuple-element.18.outward_ref.refs_2_), custom_call_target="tpu_custom_call" | custom-call | tf_op jit(solution)/shard_map/fold/fold/pallas_call | solution.py:199
  40.9 2.2 %copy-done = bf16[1536,1536]{1,0:T(8,128)(2,1)} copy-done((bf16[1536,1536]{1,0:T(8,128)(2,1)}, bf16[1536,1536]{1,0:T(8,128)(2,1)S(1)}, u32[]{:S(2)}) %copy-start) | copy-done | bytes 4718616
  43.2 4.7 %collective-permute-done.1 = bf16[192,1536]{1,0:T(8,128)(2,1)S(1)} collective-permute-done((bf16[192,1536]{1,0:T(8,128)(2,1)S(1)}, bf16[192,1536]{1,0:T(8,128)(2,1)S(1)}, u32[]{:S(2)}, u32[]{:S(2)}) %collective-permute-start.1) | collective-permute-done | bytes 589856 | tf_op jit(solution)/shard_map/sum_x/ppermute | solution.py:117
  48.2 1.6 pad_maximum_fusion.1
  49.8 1.1 collective-permute-start.9
  50.8 4.5 %source.1 = (f32[16,1536]{1,0:T(8,128)}, f32[16,1536]{1,0:T(8,128)}) custom-call(bf16[1024,512]{1,0:T(8,128)(2,1)} %bitcast.4.refs_0_, f32[16,4,384]{2,1,0:T(4,128)} %bitcast.53, bf16[1536,1536]{1,0:T(8,128)(2,1)} %copy-done), custom_call_target="tpu_custom_call" | custom-call | tf_op jit(solution)/shard_map/source/source/pallas_call | solution.py:239
  55.3 0.9 convert_element_type.210
  56.2 2.7 %collective-permute-start.4 = (bf16[16,1536]{1,0:T(8,128)(2,1)S(1)}, bf16[16,1536]{1,0:T(8,128)(2,1)S(1)}, u32[]{:S(2)}, u32[]{:S(2)}) collective-permute-start(bf16[16,1536]{1,0:T(8,128)(2,1)S(1)} %convert_element_type.210), channel_id=1, source_target_pairs={{0,12},{1,13},{2,14},{3,15},{4,8},{5,9},{6,10},{7,11},{8,4},{9,5},... | collective-permute-start | bytes 147464 | tf_op jit(solution)/shard_map/sum_source/ppermute | solution.py:117
  59.0 0.8 collective-permute-start.2
  59.8 1.3 collective-permute-done.4
  61.1 3.0 %collective-permute-done.3 = bf16[16,1536]{1,0:T(8,128)(2,1)S(1)} collective-permute-done((bf16[16,1536]{1,0:T(8,128)(2,1)S(1)}, bf16[16,1536]{1,0:T(8,128)(2,1)S(1)}, u32[]{:S(2)}, u32[]{:S(2)}) %collective-permute-start.3) | collective-permute-done | bytes 49184 | tf_op jit(solution)/shard_map/sum_source/ppermute | solution.py:117
  64.1 1.5 add_convert_fusion.7
  65.6 2.2 %collective-permute-start.5 = (bf16[16,1536]{1,0:T(8,128)(2,1)}, bf16[16,1536]{1,0:T(8,128)(2,1)}, u32[]{:S(2)}, u32[]{:S(2)}) collective-permute-start(bf16[16,1536]{1,0:T(8,128)(2,1)} %add_convert_fusion.7), channel_id=1, source_target_pairs={{0,28},{1,29},{2,30},{3,31},{4,24},{5,25},{6,26},{7,27},{8,20},{9,... | collective-permute-start | bytes 147464 | tf_op jit(solution)/shard_map/sum_source/ppermute | solution.py:117
  67.8 3.1 %collective-permute-done.5 = bf16[16,1536]{1,0:T(8,128)(2,1)} collective-permute-done((bf16[16,1536]{1,0:T(8,128)(2,1)}, bf16[16,1536]{1,0:T(8,128)(2,1)}, u32[]{:S(2)}, u32[]{:S(2)}) %collective-permute-start.5) | collective-permute-done | bytes 49184 | tf_op jit(solution)/shard_map/sum_source/ppermute | solution.py:117
  70.9 0.8 add_convert_fusion.6
  72.1 1.7 collective-permute-start.7
  73.8 1.3 collective-permute-start.6
  75.1 1.0 collective-permute-done.10
  76.0 0.9 collective-permute-done.9
  76.9 2.1 %fusion.1 = bf16[384,1536]{1,0:T(8,128)(2,1)S(1)} fusion(bf16[384,1536]{1,0:T(8,128)(2,1)} %collective-permute-done.10, bf16[384,1536]{1,0:T(8,128)(2,1)} %collective-permute-done.9, bf16[3,384,1536]{2,1,0:T(8,128)(2,1)S(1)} %fold.1), kind=kLoop, calls=%fused_computation.2 | loop fusion | flops 3538944 | bytes 4718592 | tf_op jit(solution)/shard_map/sum_x/convert_element_type | solution.py:236
  79.3 1.9 %collective-permute-start.17 = (bf16[96,1536]{1,0:T(8,128)(2,1)S(1)}, bf16[96,1536]{1,0:T(8,128)(2,1)S(1)}, u32[]{:S(2)}, u32[]{:S(2)}) collective-permute-start(bf16[96,1536]{1,0:T(8,128)(2,1)S(1)} %constant_dynamic-slice_fusion.1), channel_id=1, source_target_pairs={{0,28},{1,29},{2,30},{3,31},{4,8},{5,9},{6,10},{7,11},{8,4},{9,5},... | collective-permute-start | bytes 884744 | tf_op jit(solution)/shard_map/sum_z/ppermute | solution.py:117
  81.1 3.6 %collective-permute-done.11 = bf16[96,1536]{1,0:T(8,128)(2,1)S(1)} collective-permute-done((bf16[96,1536]{1,0:T(8,128)(2,1)S(1)}, bf16[96,1536]{1,0:T(8,128)(2,1)S(1)}, u32[]{:S(2)}, u32[]{:S(2)}) %collective-permute-start.11) | collective-permute-done | bytes 294944 | tf_op jit(solution)/shard_map/sum_z/ppermute | solution.py:117
  84.8 5.1 %collective-permute-start.12 = (bf16[16,384]{1,0:T(8,128)(2,1)S(1)}, bf16[16,384]{1,0:T(8,128)(2,1)S(1)}, u32[]{:S(2)}, u32[]{:S(2)}) collective-permute-start(bf16[16,384]{1,0:T(8,128)(2,1)S(1)} %dynamic-slice_convert_fusion), channel_id=1, source_target_pairs={{0,32},{1,33},{2,34},{3,35},{4,36},{5,37},{6,38},{7,39},{8,40},{9,... | collective-permute-start | bytes 36872 | tf_op jit(solution)/shard_map/stage0/ppermute | solution.py:117
  90.3 2.2 %collective-permute-start.13 = (bf16[48,1536]{1,0:T(8,128)(2,1)S(1)}, bf16[48,1536]{1,0:T(8,128)(2,1)S(1)}, u32[]{:S(2)}, u32[]{:S(2)}) collective-permute-start(bf16[48,1536]{1,0:T(8,128)(2,1)S(1)} %constant_dynamic-slice_fusion.2), channel_id=1, source_target_pairs={{0,28},{1,29},{2,30},{3,31},{4,8},{5,9},{6,10},{7,11},{8,4},{9,5},... | collective-permute-start | bytes 442376 | tf_op jit(solution)/shard_map/sum_z/ppermute | solution.py:117
  92.4 1.7 collective-permute-done.18
  94.1 3.5 %collective-permute-start.19 = (bf16[48,1536]{1,0:T(8,128)(2,1)S(1)}, bf16[48,1536]{1,0:T(8,128)(2,1)S(1)}, u32[]{:S(2)}, u32[]{:S(2)}) collective-permute-start(bf16[48,1536]{1,0:T(8,128)(2,1)S(1)} %add_convert_fusion.3), channel_id=1, source_target_pairs={{0,20},{1,21},{2,22},{3,23},{4,16},{5,17},{6,18},{7,19},{8,28},{9,... | collective-permute-start | bytes 442376 | tf_op jit(solution)/shard_map/sum_z/ppermute | solution.py:117
  97.7 1.3 collective-permute-start.14
  99.0 4.1 %collective-permute-done.19 = bf16[48,1536]{1,0:T(8,128)(2,1)S(1)} collective-permute-done((bf16[48,1536]{1,0:T(8,128)(2,1)S(1)}, bf16[48,1536]{1,0:T(8,128)(2,1)S(1)}, u32[]{:S(2)}, u32[]{:S(2)}) %collective-permute-start.19) | collective-permute-done | bytes 147488 | tf_op jit(solution)/shard_map/sum_z/ppermute | solution.py:117
  103.1 2.0 %collective-permute-start.20 = (bf16[48,1536]{1,0:T(8,128)(2,1)S(1)}, bf16[48,1536]{1,0:T(8,128)(2,1)S(1)}, u32[]{:S(2)}, u32[]{:S(2)}) collective-permute-start(bf16[48,1536]{1,0:T(8,128)(2,1)S(1)} %add_convert_fusion.2), channel_id=1, source_target_pairs={{0,4},{1,5},{2,6},{3,7},{4,0},{5,1},{6,2},{7,3},{8,12},{9,13},{10,... | collective-permute-start | bytes 442376 | tf_op jit(solution)/shard_map/sum_z/ppermute | solution.py:117
  105.1 1.4 collective-permute-done.14
  107.0 4.3 %collective-permute-done.20 = bf16[48,1536]{1,0:T(8,128)(2,1)S(1)} collective-permute-done((bf16[48,1536]{1,0:T(8,128)(2,1)S(1)}, bf16[48,1536]{1,0:T(8,128)(2,1)S(1)}, u32[]{:S(2)}, u32[]{:S(2)}) %collective-permute-start.20) | collective-permute-done | bytes 147488 | tf_op jit(solution)/shard_map/sum_z/ppermute | solution.py:117
  111.4 1.0 collective-permute-start.21
  112.9 7.9 %collective-permute-done.21 = bf16[96,1536]{1,0:T(8,128)(2,1)S(1)} collective-permute-done((bf16[96,1536]{1,0:T(8,128)(2,1)S(1)}, bf16[96,1536]{1,0:T(8,128)(2,1)S(1)}, u32[]{:S(2)}, u32[]{:S(2)}) %collective-permute-start.21) | collective-permute-done | bytes 294944 | tf_op jit(solution)/shard_map/sum_z/ppermute | solution.py:117
  121.2 8.3 %collective-permute-start.25 = (bf16[16,1536]{1,0:T(8,128)(2,1)S(1)}, bf16[16,1536]{1,0:T(8,128)(2,1)S(1)}, u32[]{:S(2)}, u32[]{:S(2)}) collective-permute-start(bf16[16,1536]{1,0:T(8,128)(2,1)S(1)} %fusion.3), channel_id=1, source_target_pairs={{0,227},{1,226},{2,225},{3,224},{4,231},{5,230},{6,229},{7,228},{8... | collective-permute-start | bytes 147464 | tf_op jit(solution)/shard_map/stage1/ppermute | solution.py:117
  129.9 2.4 %collective-permute-start.23 = (bf16[16,1536]{1,0:T(8,128)(2,1)S(1)}, bf16[16,1536]{1,0:T(8,128)(2,1)S(1)}, u32[]{:S(2)}, u32[]{:S(2)}) collective-permute-start(bf16[16,1536]{1,0:T(8,128)(2,1)S(1)} %fusion.3), channel_id=1, source_target_pairs={{0,225},{1,224},{2,227},{3,226},{4,229},{5,228},{6,231},{7,230},{8... | collective-permute-start | bytes 147464 | tf_op jit(solution)/shard_map/stage1/ppermute | solution.py:117
  132.4 2.9 %collective-permute-done.24 = bf16[16,1536]{1,0:T(8,128)(2,1)S(1)} collective-permute-done((bf16[16,1536]{1,0:T(8,128)(2,1)S(1)}, bf16[16,1536]{1,0:T(8,128)(2,1)S(1)}, u32[]{:S(2)}, u32[]{:S(2)}) %collective-permute-start.24) | collective-permute-done | bytes 49184 | tf_op jit(solution)/shard_map/stage1/ppermute | solution.py:117
  135.4 0.8 collective-permute-done.22
  136.5 1.4 collective-permute-start.26
  137.9 0.8 collective-permute-done.26
  139.0 1.3 collective-permute-start.30
  140.3 2.3 %collective-permute-start.29 = (bf16[16,1536]{1,0:T(8,128)(2,1)S(1)}, bf16[16,1536]{1,0:T(8,128)(2,1)S(1)}, u32[]{:S(2)}, u32[]{:S(2)}) collective-permute-start(bf16[16,1536]{1,0:T(8,128)(2,1)S(1)} %fusion.4), channel_id=1, source_target_pairs={{0,226},{1,227},{2,224},{3,225},{4,230},{5,231},{6,228},{7,229},{8... | collective-permute-start | bytes 147464 | tf_op jit(solution)/shard_map/stage3/ppermute | solution.py:117
  142.7 0.6 collective-permute-start.28
  143.3 1.6 collective-permute-start.27
  145.0 1.5 collective-permute-done.29
  146.4 0.7 collective-permute-done.28
  147.8 4.7 %collective-permute-start.31 = (bf16[16,384]{1,0:T(8,128)(2,1)S(1)}, bf16[16,384]{1,0:T(8,128)(2,1)S(1)}, u32[]{:S(2)}, u32[]{:S(2)}) collective-permute-start(bf16[16,384]{1,0:T(8,128)(2,1)S(1)} %fusion.9), channel_id=1, source_target_pairs={{0,32},{1,33},{2,34},{3,35},{4,36},{5,37},{6,38},{7,39},{8,40},{9,... | collective-permute-start | bytes 36872 | tf_op jit(solution)/shard_map/stage4/ppermute | solution.py:117
  152.5 0.8 collective-permute-done.31
  153.6 3.3 %collective-permute-start.34 = (bf16[16,1536]{1,0:T(8,128)(2,1)S(1)}, bf16[16,1536]{1,0:T(8,128)(2,1)S(1)}, u32[]{:S(2)}, u32[]{:S(2)}) collective-permute-start(bf16[16,1536]{1,0:T(8,128)(2,1)S(1)} %fusion.5), channel_id=1, source_target_pairs={{0,226},{1,227},{2,224},{3,225},{4,230},{5,231},{6,228},{7,229},{8... | collective-permute-start | bytes 147464 | tf_op jit(solution)/shard_map/stage5/ppermute | solution.py:117
  157.1 2.4 %collective-permute-start.32 = (bf16[16,1536]{1,0:T(8,128)(2,1)S(1)}, bf16[16,1536]{1,0:T(8,128)(2,1)S(1)}, u32[]{:S(2)}, u32[]{:S(2)}) collective-permute-start(bf16[16,1536]{1,0:T(8,128)(2,1)S(1)} %fusion.5), channel_id=1, source_target_pairs={{0,224},{1,225},{2,226},{3,227},{4,228},{5,229},{6,230},{7,231},{8... | collective-permute-start | bytes 147464 | tf_op jit(solution)/shard_map/stage5/ppermute | solution.py:117
  159.5 0.7 collective-permute-done.34
  160.2 1.5 collective-permute-done.33
  162.4 2.6 %collective-permute-start.36 = (bf16[16,384]{1,0:T(8,128)(2,1)S(1)}, bf16[16,384]{1,0:T(8,128)(2,1)S(1)}, u32[]{:S(2)}, u32[]{:S(2)}) collective-permute-start(bf16[16,384]{1,0:T(8,128)(2,1)S(1)} %fusion.10), channel_id=1, source_target_pairs={{0,32},{1,33},{2,34},{3,35},{4,36},{5,37},{6,38},{7,39},{8,40},{9,... | collective-permute-start | bytes 36872 | tf_op jit(solution)/shard_map/spread/ppermute | solution.py:117
  165.1 1.1 collective-permute-start.37
  166.2 2.2 %collective-permute-start.38 = (bf16[16,384]{1,0:T(8,128)(2,1)S(1)}, bf16[16,384]{1,0:T(8,128)(2,1)S(1)}, u32[]{:S(2)}, u32[]{:S(2)}) collective-permute-start(bf16[16,384]{1,0:T(8,128)(2,1)S(1)} %fusion.10), channel_id=1, source_target_pairs={{0,34},{1,35},{2,32},{3,33},{4,38},{5,39},{6,36},{7,37},{8,42},{9,... | collective-permute-start | bytes 36872 | tf_op jit(solution)/shard_map/spread/ppermute | solution.py:117
  168.4 0.9 collective-permute-start.39
  169.3 1.5 collective-permute-done.38
  170.8 1.9 %collective-permute-done.39 = bf16[16,384]{1,0:T(8,128)(2,1)S(1)} collective-permute-done((bf16[16,384]{1,0:T(8,128)(2,1)S(1)}, bf16[16,384]{1,0:T(8,128)(2,1)S(1)}, u32[]{:S(2)}, u32[]{:S(2)}) %collective-permute-start.39) | collective-permute-done | bytes 12320 | tf_op jit(solution)/shard_map/spread/ppermute | solution.py:117
  172.7 3.1 %fusion.2 = bf16[16,1536]{1,0:T(8,128)(2,1)S(1)} fusion(f32[16,1536]{1,0:T(8,128)S(1)} %copy-done.4, bf16[16,1536]{1,0:T(8,128)(2,1)S(1)} %constant_dynamic-update-slice_fusion, bf16[16,1536]{1,0:T(8,128)(2,1)S(1)} %select_convert_fusion, pred[]{:T(512)S(6)} %eq.14, bf16[1,1536,1536]{2,1,0:T(8,128)(2,1)} %param.12), kind=kOutput, calls=%fused_computation.7 | convolution fusion | flops 75571200 | bytes 4964353 | tf_op jit(solution)/shard_map/solve/dot_general | solution.py:319
  176.2 0.7 copy.9
  (83 shorter events, 6.5 us)
Async XLA Ops:
  3.3 12.2 %copy-start.2 = (bf16[1,4,384,384]{3,2,1,0:T(8,128)(2,1)S(1)}, bf16[1,4,384,384]{3,2,1,0:T(8,128)(2,1)}, u32[]{:S(2)}) copy-start(bf16[1,4,384,384]{3,2,1,0:T(8,128)(2,1)} %param.11) | copy-start | bytes 3538948
  3.3 46.5 %all-to-all-start = ((bf16[32,32,512]{2,1,0:T(8,128)(2,1)}), bf16[32,32,512]{2,1,0:T(8,128)(2,1)}, u32[]{:S(2)}, u32[]{:S(2)}) async-start(bf16[32,32,512]{2,1,0:T(8,128)(2,1)} %bitcast.51), calls=%async_computation | async-start | bytes 2097152 | tf_op jit(solution)/shard_map/route/all_to_all | solution.py:146
  15.5 13.5 %slice-start = ((s8[4718592]{0:T(1024)(128)(4,1)}), s8[4194304]{0:T(1024)(128)(4,1)S(1)}, s32[]{:S(2)}) async-start(s8[4718592]{0:T(1024)(128)(4,1)} %bitcast.46), calls=%async_computation.1 | async-start | bytes 8388608
  15.5 2.5 %copy-start.1 = (bf16[1,1536,1536]{2,1,0:T(8,128)(2,1)S(1)}, bf16[1,1536,1536]{2,1,0:T(8,128)(2,1)}, u32[]{:S(2)}) copy-start(bf16[1,1536,1536]{2,1,0:T(8,128)(2,1)} %param.13) | copy-start | bytes 14155780
  18.0 11.0 %slice-start.1 = ((s8[4718592]{0:T(1024)(128)(4,1)}), s8[524288]{0:T(1024)(128)(4,1)S(1)}, s32[]{:S(2)}) async-start(s8[4718592]{0:T(1024)(128)(4,1)} %bitcast.46), calls=%async_computation.2 | async-start | bytes 1048576
  26.5 21.3 %collective-permute-start.1 = (bf16[192,1536]{1,0:T(8,128)(2,1)S(1)}, bf16[192,1536]{1,0:T(8,128)(2,1)S(1)}, u32[]{:S(2)}, u32[]{:S(2)}) collective-permute-start(bf16[192,1536]{1,0:T(8,128)(2,1)S(1)} %get-tuple-element.37), channel_id=1, source_target_pairs={{0,3},{1,2},{2,1},{3,0},{4,7},{5,6},{6,5},{7,4},{8,11},{9,10},{10,... | collective-permute-start | bytes 1769480 | tf_op jit(solution)/shard_map/sum_x/ppermute | solution.py:117
  29.0 18.9 %collective-permute-start = (bf16[192,1536]{1,0:T(8,128)(2,1)S(1)}, bf16[192,1536]{1,0:T(8,128)(2,1)S(1)}, u32[]{:S(2)}, u32[]{:S(2)}) collective-permute-start(bf16[192,1536]{1,0:T(8,128)(2,1)S(1)} %get-tuple-element.38), channel_id=1, source_target_pairs={{0,1},{1,0},{2,3},{3,2},{4,5},{5,4},{6,7},{7,6},{8,9},{9,8},{10,11... | collective-permute-start | bytes 1769480 | tf_op jit(solution)/shard_map/sum_x/ppermute | solution.py:117
  40.9 2.2 %copy-start = (bf16[1536,1536]{1,0:T(8,128)(2,1)}, bf16[1536,1536]{1,0:T(8,128)(2,1)S(1)}, u32[]{:S(2)}) copy-start(bf16[1536,1536]{1,0:T(8,128)(2,1)S(1)} %get-tuple-element.18.outward_ref.refs_2_) | copy-start | bytes 14155780
  49.8 26.3 %collective-permute-start.10 = (bf16[384,1536]{1,0:T(8,128)(2,1)}, bf16[384,1536]{1,0:T(8,128)(2,1)}, u32[]{:S(2)}, u32[]{:S(2)}) collective-permute-start(bf16[384,1536]{1,0:T(8,128)(2,1)} %get-tuple-element.24), channel_id=1, source_target_pairs={{0,1},{1,0},{2,3},{3,2},{4,5},{5,4},{6,7},{7,6},{8,9},{9,8},{10,11... | collective-permute-start | bytes 3538952 | tf_op jit(solution)/shard_map/sum_x/ppermute | solution.py:117
  49.8 27.1 %collective-permute-start.9 = (bf16[384,1536]{1,0:T(8,128)(2,1)}, bf16[384,1536]{1,0:T(8,128)(2,1)}, u32[]{:S(2)}, u32[]{:S(2)}) collective-permute-start(bf16[384,1536]{1,0:T(8,128)(2,1)} %get-tuple-element.23), channel_id=1, source_target_pairs={{0,3},{1,2},{2,1},{3,0},{4,7},{5,6},{6,5},{7,4},{8,11},{9,10},{10,... | collective-permute-start | bytes 3538952 | tf_op jit(solution)/shard_map/sum_x/ppermute | solution.py:117
  56.2 4.8 %collective-permute-start.4 = (bf16[16,1536]{1,0:T(8,128)(2,1)S(1)}, bf16[16,1536]{1,0:T(8,128)(2,1)S(1)}, u32[]{:S(2)}, u32[]{:S(2)}) collective-permute-start(bf16[16,1536]{1,0:T(8,128)(2,1)S(1)} %convert_element_type.210), channel_id=1, source_target_pairs={{0,12},{1,13},{2,14},{3,15},{4,8},{5,9},{6,10},{7,11},{8,4},{9,5},... | collective-permute-start | bytes 147464 | tf_op jit(solution)/shard_map/sum_source/ppermute | solution.py:117
  58.9 5.2 %collective-permute-start.3 = (bf16[16,1536]{1,0:T(8,128)(2,1)S(1)}, bf16[16,1536]{1,0:T(8,128)(2,1)S(1)}, u32[]{:S(2)}, u32[]{:S(2)}) collective-permute-start(bf16[16,1536]{1,0:T(8,128)(2,1)S(1)} %convert_element_type.210), channel_id=1, source_target_pairs={{0,8},{1,9},{2,10},{3,11},{4,12},{5,13},{6,14},{7,15},{8,0},{9,1},... | collective-permute-start | bytes 147464 | tf_op jit(solution)/shard_map/sum_source/ppermute | solution.py:117
  59.0 5.1 %collective-permute-start.2 = (bf16[16,1536]{1,0:T(8,128)(2,1)S(1)}, bf16[16,1536]{1,0:T(8,128)(2,1)S(1)}, u32[]{:S(2)}, u32[]{:S(2)}) collective-permute-start(bf16[16,1536]{1,0:T(8,128)(2,1)S(1)} %convert_element_type.210), channel_id=1, source_target_pairs={{0,4},{1,5},{2,6},{3,7},{4,0},{5,1},{6,2},{7,3},{8,12},{9,13},{10,... | collective-permute-start | bytes 147464 | tf_op jit(solution)/shard_map/sum_source/ppermute | solution.py:117
  65.6 5.2 %collective-permute-start.5 = (bf16[16,1536]{1,0:T(8,128)(2,1)}, bf16[16,1536]{1,0:T(8,128)(2,1)}, u32[]{:S(2)}, u32[]{:S(2)}) collective-permute-start(bf16[16,1536]{1,0:T(8,128)(2,1)} %add_convert_fusion.7), channel_id=1, source_target_pairs={{0,28},{1,29},{2,30},{3,31},{4,24},{5,25},{6,26},{7,27},{8,20},{9,... | collective-permute-start | bytes 147464 | tf_op jit(solution)/shard_map/sum_source/ppermute | solution.py:117
  71.7 7.4 %collective-permute-start.8 = (bf16[16,1536]{1,0:T(8,128)(2,1)S(1)}, bf16[16,1536]{1,0:T(8,128)(2,1)S(1)}, u32[]{:S(2)}, u32[]{:S(2)}) collective-permute-start(bf16[16,1536]{1,0:T(8,128)(2,1)S(1)} %add_convert_fusion.6), channel_id=1, source_target_pairs={{0,3},{1,2},{2,1},{3,0},{4,7},{5,6},{6,5},{7,4},{8,11},{9,10},{10,... | collective-permute-start | bytes 147464 | tf_op jit(solution)/shard_map/sum_source/ppermute | solution.py:117
  72.1 7.1 %collective-permute-start.7 = (bf16[16,1536]{1,0:T(8,128)(2,1)S(1)}, bf16[16,1536]{1,0:T(8,128)(2,1)S(1)}, u32[]{:S(2)}, u32[]{:S(2)}) collective-permute-start(bf16[16,1536]{1,0:T(8,128)(2,1)S(1)} %add_convert_fusion.6), channel_id=1, source_target_pairs={{0,2},{1,3},{2,0},{3,1},{4,6},{5,7},{6,4},{7,5},{8,10},{9,11},{10,... | collective-permute-start | bytes 147464 | tf_op jit(solution)/shard_map/sum_source/ppermute | solution.py:117
  73.8 5.4 %collective-permute-start.6 = (bf16[16,1536]{1,0:T(8,128)(2,1)S(1)}, bf16[16,1536]{1,0:T(8,128)(2,1)S(1)}, u32[]{:S(2)}, u32[]{:S(2)}) collective-permute-start(bf16[16,1536]{1,0:T(8,128)(2,1)S(1)} %add_convert_fusion.6), channel_id=1, source_target_pairs={{0,1},{1,0},{2,3},{3,2},{4,5},{5,4},{6,7},{7,6},{8,9},{9,8},{10,11... | collective-permute-start | bytes 147464 | tf_op jit(solution)/shard_map/sum_source/ppermute | solution.py:117
  79.1 5.7 %collective-permute-start.11 = (bf16[96,1536]{1,0:T(8,128)(2,1)S(1)}, bf16[96,1536]{1,0:T(8,128)(2,1)S(1)}, u32[]{:S(2)}, u32[]{:S(2)}) collective-permute-start(bf16[96,1536]{1,0:T(8,128)(2,1)S(1)} %constant_dynamic-slice_fusion.3), channel_id=1, source_target_pairs={{0,4},{1,5},{2,6},{3,7},{4,0},{5,1},{6,2},{7,3},{8,12},{9,13},{10,... | collective-permute-start | bytes 884744 | tf_op jit(solution)/shard_map/sum_z/ppermute | solution.py:117
  79.3 10.6 %collective-permute-start.17 = (bf16[96,1536]{1,0:T(8,128)(2,1)S(1)}, bf16[96,1536]{1,0:T(8,128)(2,1)S(1)}, u32[]{:S(2)}, u32[]{:S(2)}) collective-permute-start(bf16[96,1536]{1,0:T(8,128)(2,1)S(1)} %constant_dynamic-slice_fusion.1), channel_id=1, source_target_pairs={{0,28},{1,29},{2,30},{3,31},{4,8},{5,9},{6,10},{7,11},{8,4},{9,5},... | collective-permute-start | bytes 884744 | tf_op jit(solution)/shard_map/sum_z/ppermute | solution.py:117
  84.8 36.1 %collective-permute-start.12 = (bf16[16,384]{1,0:T(8,128)(2,1)S(1)}, bf16[16,384]{1,0:T(8,128)(2,1)S(1)}, u32[]{:S(2)}, u32[]{:S(2)}) collective-permute-start(bf16[16,384]{1,0:T(8,128)(2,1)S(1)} %dynamic-slice_convert_fusion), channel_id=1, source_target_pairs={{0,32},{1,33},{2,34},{3,35},{4,36},{5,37},{6,38},{7,39},{8,40},{9,... | collective-permute-start | bytes 36872 | tf_op jit(solution)/shard_map/stage0/ppermute | solution.py:117
  90.0 4.1 %collective-permute-start.18 = (bf16[48,1536]{1,0:T(8,128)(2,1)S(1)}, bf16[48,1536]{1,0:T(8,128)(2,1)S(1)}, u32[]{:S(2)}, u32[]{:S(2)}) collective-permute-start(bf16[48,1536]{1,0:T(8,128)(2,1)S(1)} %constant_dynamic-slice_fusion), channel_id=1, source_target_pairs={{0,4},{1,5},{2,6},{3,7},{4,0},{5,1},{6,2},{7,3},{8,12},{9,13},{10,... | collective-permute-start | bytes 442376 | tf_op jit(solution)/shard_map/sum_z/ppermute | solution.py:117
  90.3 7.4 %collective-permute-start.13 = (bf16[48,1536]{1,0:T(8,128)(2,1)S(1)}, bf16[48,1536]{1,0:T(8,128)(2,1)S(1)}, u32[]{:S(2)}, u32[]{:S(2)}) collective-permute-start(bf16[48,1536]{1,0:T(8,128)(2,1)S(1)} %constant_dynamic-slice_fusion.2), channel_id=1, source_target_pairs={{0,28},{1,29},{2,30},{3,31},{4,8},{5,9},{6,10},{7,11},{8,4},{9,5},... | collective-permute-start | bytes 442376 | tf_op jit(solution)/shard_map/sum_z/ppermute | solution.py:117
  94.1 8.9 %collective-permute-start.19 = (bf16[48,1536]{1,0:T(8,128)(2,1)S(1)}, bf16[48,1536]{1,0:T(8,128)(2,1)S(1)}, u32[]{:S(2)}, u32[]{:S(2)}) collective-permute-start(bf16[48,1536]{1,0:T(8,128)(2,1)S(1)} %add_convert_fusion.3), channel_id=1, source_target_pairs={{0,20},{1,21},{2,22},{3,23},{4,16},{5,17},{6,18},{7,19},{8,28},{9,... | collective-permute-start | bytes 442376 | tf_op jit(solution)/shard_map/sum_z/ppermute | solution.py:117
  97.7 8.8 %collective-permute-start.14 = (bf16[48,1536]{1,0:T(8,128)(2,1)S(1)}, bf16[48,1536]{1,0:T(8,128)(2,1)S(1)}, u32[]{:S(2)}, u32[]{:S(2)}) collective-permute-start(bf16[48,1536]{1,0:T(8,128)(2,1)S(1)} %add_convert_fusion.5), channel_id=1, source_target_pairs={{0,12},{1,13},{2,14},{3,15},{4,24},{5,25},{6,26},{7,27},{8,20},{9,... | collective-permute-start | bytes 442376 | tf_op jit(solution)/shard_map/sum_z/ppermute | solution.py:117
  103.1 8.3 %collective-permute-start.20 = (bf16[48,1536]{1,0:T(8,128)(2,1)S(1)}, bf16[48,1536]{1,0:T(8,128)(2,1)S(1)}, u32[]{:S(2)}, u32[]{:S(2)}) collective-permute-start(bf16[48,1536]{1,0:T(8,128)(2,1)S(1)} %add_convert_fusion.2), channel_id=1, source_target_pairs={{0,4},{1,5},{2,6},{3,7},{4,0},{5,1},{6,2},{7,3},{8,12},{9,13},{10,... | collective-permute-start | bytes 442376 | tf_op jit(solution)/shard_map/sum_z/ppermute | solution.py:117
  106.6 6.2 %collective-permute-start.15 = (bf16[48,1536]{1,0:T(8,128)(2,1)S(1)}, bf16[48,1536]{1,0:T(8,128)(2,1)S(1)}, u32[]{:S(2)}, u32[]{:S(2)}) collective-permute-start(bf16[48,1536]{1,0:T(8,128)(2,1)S(1)} %add_convert_fusion.4), channel_id=1, source_target_pairs={{0,28},{1,29},{2,30},{3,31},{4,8},{5,9},{6,10},{7,11},{8,4},{9,5},... | collective-permute-start | bytes 442376 | tf_op jit(solution)/shard_map/sum_z/ppermute | solution.py:117
  111.4 9.5 %collective-permute-start.21 = (bf16[96,1536]{1,0:T(8,128)(2,1)S(1)}, bf16[96,1536]{1,0:T(8,128)(2,1)S(1)}, u32[]{:S(2)}, u32[]{:S(2)}) collective-permute-start(bf16[96,1536]{1,0:T(8,128)(2,1)S(1)} %constant_dynamic-update-slice_fusion.5), channel_id=1, source_target_pairs={{0,28},{1,29},{2,30},{3,31},{4,8},{5,9},{6,10},{7,11},{8,4},{9,5},... | collective-permute-start | bytes 884744 | tf_op jit(solution)/shard_map/sum_z/ppermute | solution.py:117
  112.8 8.1 %collective-permute-start.16 = (bf16[96,1536]{1,0:T(8,128)(2,1)S(1)}, bf16[96,1536]{1,0:T(8,128)(2,1)S(1)}, u32[]{:S(2)}, u32[]{:S(2)}) collective-permute-start(bf16[96,1536]{1,0:T(8,128)(2,1)S(1)} %constant_dynamic-update-slice_fusion.7), channel_id=1, source_target_pairs={{0,4},{1,5},{2,6},{3,7},{4,0},{5,1},{6,2},{7,3},{8,12},{9,13},{10,... | collective-permute-start | bytes 884744 | tf_op jit(solution)/shard_map/sum_z/ppermute | solution.py:117
  121.2 11.3 %collective-permute-start.25 = (bf16[16,1536]{1,0:T(8,128)(2,1)S(1)}, bf16[16,1536]{1,0:T(8,128)(2,1)S(1)}, u32[]{:S(2)}, u32[]{:S(2)}) collective-permute-start(bf16[16,1536]{1,0:T(8,128)(2,1)S(1)} %fusion.3), channel_id=1, source_target_pairs={{0,227},{1,226},{2,225},{3,224},{4,231},{5,230},{6,229},{7,228},{8... | collective-permute-start | bytes 147464 | tf_op jit(solution)/shard_map/stage1/ppermute | solution.py:117
  129.5 5.9 %collective-permute-start.24 = (bf16[16,1536]{1,0:T(8,128)(2,1)S(1)}, bf16[16,1536]{1,0:T(8,128)(2,1)S(1)}, u32[]{:S(2)}, u32[]{:S(2)}) collective-permute-start(bf16[16,1536]{1,0:T(8,128)(2,1)S(1)} %fusion.3), channel_id=1, source_target_pairs={{0,226},{1,227},{2,224},{3,225},{4,230},{5,231},{6,228},{7,229},{8... | collective-permute-start | bytes 147464 | tf_op jit(solution)/shard_map/stage1/ppermute | solution.py:117
  129.9 5.5 %collective-permute-start.23 = (bf16[16,1536]{1,0:T(8,128)(2,1)S(1)}, bf16[16,1536]{1,0:T(8,128)(2,1)S(1)}, u32[]{:S(2)}, u32[]{:S(2)}) collective-permute-start(bf16[16,1536]{1,0:T(8,128)(2,1)S(1)} %fusion.3), channel_id=1, source_target_pairs={{0,225},{1,224},{2,227},{3,226},{4,229},{5,228},{6,231},{7,230},{8... | collective-permute-start | bytes 147464 | tf_op jit(solution)/shard_map/stage1/ppermute | solution.py:117
  132.3 3.9 %collective-permute-start.22 = (bf16[16,1536]{1,0:T(8,128)(2,1)S(1)}, bf16[16,1536]{1,0:T(8,128)(2,1)S(1)}, u32[]{:S(2)}, u32[]{:S(2)}) collective-permute-start(bf16[16,1536]{1,0:T(8,128)(2,1)S(1)} %fusion.3), channel_id=1, source_target_pairs={{0,224},{1,225},{2,226},{3,227},{4,228},{5,229},{6,230},{7,231},{8... | collective-permute-start | bytes 147464 | tf_op jit(solution)/shard_map/stage1/ppermute | solution.py:117
  136.5 2.3 %collective-permute-start.26 = (bf16[16,384]{1,0:T(8,128)(2,1)S(1)}, bf16[16,384]{1,0:T(8,128)(2,1)S(1)}, u32[]{:S(2)}, u32[]{:S(2)}) collective-permute-start(bf16[16,384]{1,0:T(8,128)(2,1)S(1)} %fusion.8), channel_id=1, source_target_pairs={{0,32},{1,33},{2,34},{3,35},{4,36},{5,37},{6,38},{7,39},{8,40},{9,... | collective-permute-start | bytes 36872 | tf_op jit(solution)/shard_map/stage2/ppermute | solution.py:117
  139.0 6.0 %collective-permute-start.30 = (bf16[16,1536]{1,0:T(8,128)(2,1)S(1)}, bf16[16,1536]{1,0:T(8,128)(2,1)S(1)}, u32[]{:S(2)}, u32[]{:S(2)}) collective-permute-start(bf16[16,1536]{1,0:T(8,128)(2,1)S(1)} %fusion.4), channel_id=1, source_target_pairs={{0,227},{1,226},{2,225},{3,224},{4,231},{5,230},{6,229},{7,228},{8... | collective-permute-start | bytes 147464 | tf_op jit(solution)/shard_map/stage3/ppermute | solution.py:117
  140.3 6.1 %collective-permute-start.29 = (bf16[16,1536]{1,0:T(8,128)(2,1)S(1)}, bf16[16,1536]{1,0:T(8,128)(2,1)S(1)}, u32[]{:S(2)}, u32[]{:S(2)}) collective-permute-start(bf16[16,1536]{1,0:T(8,128)(2,1)S(1)} %fusion.4), channel_id=1, source_target_pairs={{0,226},{1,227},{2,224},{3,225},{4,230},{5,231},{6,228},{7,229},{8... | collective-permute-start | bytes 147464 | tf_op jit(solution)/shard_map/stage3/ppermute | solution.py:117
  142.7 4.5 %collective-permute-start.28 = (bf16[16,1536]{1,0:T(8,128)(2,1)S(1)}, bf16[16,1536]{1,0:T(8,128)(2,1)S(1)}, u32[]{:S(2)}, u32[]{:S(2)}) collective-permute-start(bf16[16,1536]{1,0:T(8,128)(2,1)S(1)} %fusion.4), channel_id=1, source_target_pairs={{0,225},{1,224},{2,227},{3,226},{4,229},{5,228},{6,231},{7,230},{8... | collective-permute-start | bytes 147464 | tf_op jit(solution)/shard_map/stage3/ppermute | solution.py:117
  143.3 4.2 %collective-permute-start.27 = (bf16[16,1536]{1,0:T(8,128)(2,1)S(1)}, bf16[16,1536]{1,0:T(8,128)(2,1)S(1)}, u32[]{:S(2)}, u32[]{:S(2)}) collective-permute-start(bf16[16,1536]{1,0:T(8,128)(2,1)S(1)} %fusion.4), channel_id=1, source_target_pairs={{0,224},{1,225},{2,226},{3,227},{4,228},{5,229},{6,230},{7,231},{8... | collective-permute-start | bytes 147464 | tf_op jit(solution)/shard_map/stage3/ppermute | solution.py:117
  147.8 5.6 %collective-permute-start.31 = (bf16[16,384]{1,0:T(8,128)(2,1)S(1)}, bf16[16,384]{1,0:T(8,128)(2,1)S(1)}, u32[]{:S(2)}, u32[]{:S(2)}) collective-permute-start(bf16[16,384]{1,0:T(8,128)(2,1)S(1)} %fusion.9), channel_id=1, source_target_pairs={{0,32},{1,33},{2,34},{3,35},{4,36},{5,37},{6,38},{7,39},{8,40},{9,... | collective-permute-start | bytes 36872 | tf_op jit(solution)/shard_map/stage4/ppermute | solution.py:117
  153.6 6.0 %collective-permute-start.35 = (bf16[16,1536]{1,0:T(8,128)(2,1)S(1)}, bf16[16,1536]{1,0:T(8,128)(2,1)S(1)}, u32[]{:S(2)}, u32[]{:S(2)}) collective-permute-start(bf16[16,1536]{1,0:T(8,128)(2,1)S(1)} %fusion.5), channel_id=1, source_target_pairs={{0,227},{1,226},{2,225},{3,224},{4,231},{5,230},{6,229},{7,228},{8... | collective-permute-start | bytes 147464 | tf_op jit(solution)/shard_map/stage5/ppermute | solution.py:117
  153.6 6.6 %collective-permute-start.34 = (bf16[16,1536]{1,0:T(8,128)(2,1)S(1)}, bf16[16,1536]{1,0:T(8,128)(2,1)S(1)}, u32[]{:S(2)}, u32[]{:S(2)}) collective-permute-start(bf16[16,1536]{1,0:T(8,128)(2,1)S(1)} %fusion.5), channel_id=1, source_target_pairs={{0,226},{1,227},{2,224},{3,225},{4,230},{5,231},{6,228},{7,229},{8... | collective-permute-start | bytes 147464 | tf_op jit(solution)/shard_map/stage5/ppermute | solution.py:117
  157.0 4.7 %collective-permute-start.33 = (bf16[16,1536]{1,0:T(8,128)(2,1)S(1)}, bf16[16,1536]{1,0:T(8,128)(2,1)S(1)}, u32[]{:S(2)}, u32[]{:S(2)}) collective-permute-start(bf16[16,1536]{1,0:T(8,128)(2,1)S(1)} %fusion.5), channel_id=1, source_target_pairs={{0,225},{1,224},{2,227},{3,226},{4,229},{5,228},{6,231},{7,230},{8... | collective-permute-start | bytes 147464 | tf_op jit(solution)/shard_map/stage5/ppermute | solution.py:117
  157.1 5.0 %collective-permute-start.32 = (bf16[16,1536]{1,0:T(8,128)(2,1)S(1)}, bf16[16,1536]{1,0:T(8,128)(2,1)S(1)}, u32[]{:S(2)}, u32[]{:S(2)}) collective-permute-start(bf16[16,1536]{1,0:T(8,128)(2,1)S(1)} %fusion.5), channel_id=1, source_target_pairs={{0,224},{1,225},{2,226},{3,227},{4,228},{5,229},{6,230},{7,231},{8... | collective-permute-start | bytes 147464 | tf_op jit(solution)/shard_map/stage5/ppermute | solution.py:117
  162.2 10.6 %copy-start.4 = (f32[16,1536]{1,0:T(8,128)S(1)}, f32[16,1536]{1,0:T(8,128)}, u32[]{:S(2)}) copy-start(f32[16,1536]{1,0:T(8,128)} %get-tuple-element.21) | copy-start | bytes 294916
  162.4 6.8 %collective-permute-start.36 = (bf16[16,384]{1,0:T(8,128)(2,1)S(1)}, bf16[16,384]{1,0:T(8,128)(2,1)S(1)}, u32[]{:S(2)}, u32[]{:S(2)}) collective-permute-start(bf16[16,384]{1,0:T(8,128)(2,1)S(1)} %fusion.10), channel_id=1, source_target_pairs={{0,32},{1,33},{2,34},{3,35},{4,36},{5,37},{6,38},{7,39},{8,40},{9,... | collective-permute-start | bytes 36872 | tf_op jit(solution)/shard_map/spread/ppermute | solution.py:117
  165.1 4.2 %collective-permute-start.37 = (bf16[16,384]{1,0:T(8,128)(2,1)S(1)}, bf16[16,384]{1,0:T(8,128)(2,1)S(1)}, u32[]{:S(2)}, u32[]{:S(2)}) collective-permute-start(bf16[16,384]{1,0:T(8,128)(2,1)S(1)} %fusion.10), channel_id=1, source_target_pairs={{0,33},{1,32},{2,35},{3,34},{4,37},{5,36},{6,39},{7,38},{8,41},{9,... | collective-permute-start | bytes 36872 | tf_op jit(solution)/shard_map/spread/ppermute | solution.py:117
  166.2 4.6 %collective-permute-start.38 = (bf16[16,384]{1,0:T(8,128)(2,1)S(1)}, bf16[16,384]{1,0:T(8,128)(2,1)S(1)}, u32[]{:S(2)}, u32[]{:S(2)}) collective-permute-start(bf16[16,384]{1,0:T(8,128)(2,1)S(1)} %fusion.10), channel_id=1, source_target_pairs={{0,34},{1,35},{2,32},{3,33},{4,38},{5,39},{6,36},{7,37},{8,42},{9,... | collective-permute-start | bytes 36872 | tf_op jit(solution)/shard_map/spread/ppermute | solution.py:117
  168.4 4.3 %collective-permute-start.39 = (bf16[16,384]{1,0:T(8,128)(2,1)S(1)}, bf16[16,384]{1,0:T(8,128)(2,1)S(1)}, u32[]{:S(2)}, u32[]{:S(2)}) collective-permute-start(bf16[16,384]{1,0:T(8,128)(2,1)S(1)} %fusion.10), channel_id=1, source_target_pairs={{0,35},{1,34},{2,33},{3,32},{4,39},{5,38},{6,37},{7,36},{8,43},{9,... | collective-permute-start | bytes 36872 | tf_op jit(solution)/shard_map/spread/ppermute | solution.py:117
  172.7 3.2 %copy-start.3 = (bf16[1,4,384,384]{3,2,1,0:T(8,128)(2,1)S(1)}, bf16[1,4,384,384]{3,2,1,0:T(8,128)(2,1)}, u32[]{:S(2)}) copy-start(bf16[1,4,384,384]{3,2,1,0:T(8,128)(2,1)} %param.11) | copy-start | bytes 3538948

commit v6 on v5

--- a/solution.py
+++ b/solution.py
@@ -91,6 +91,16 @@
     piece_ref[0] = jnp.dot(
         in_ref[...], outward_ref[...], preferred_element_type=F32
     ).astype(BF)
+
+
+def solve_kernel(panel_ref, in_ref, assembled_ref, inv_ref, out_ref):
+    coupled = jnp.dot(panel_ref[...], in_ref[...], preferred_element_type=F32)
+    local = (assembled_ref[...] - coupled).astype(BF)
+    width = inv_ref.shape[1]
+    for face in range(inv_ref.shape[0]):
+        out_ref[:, face, :] = jnp.dot(
+            local[:, face * width : (face + 1) * width], inv_ref[face], preferred_element_type=F32
+        )
 
 
 def on_device(shape, face_rhs, res_rows, row_owner, row_slot, inv_blocks, couple_in, couple_out):
@@ -316,9 +326,13 @@
             spread = lax.dynamic_update_slice_in_dim(spread, part, (here_x ^ m) * slab, 1)
         panel = jnp.where(odd, spread, panel)
     with jax.named_scope("solve"):
-        coupled = jnp.dot(panel, coupling_in, preferred_element_type=F32)
-        local = (assembled - coupled).astype(BF).reshape(rhs_count, face_dev, width)
-        solved = jnp.einsum("rfw,fwv->rfv", local, inverse, preferred_element_type=F32)
+        solved = pl.pallas_call(
+            solve_kernel,
+            in_specs=[vmem] * 4,
+            out_specs=vmem,
+            out_shape=jax.ShapeDtypeStruct((rhs_count, face_dev, width), F32),
+            name="solve",
+        )(panel, coupling_in, assembled, inverse)
     return solved[None]
 
 

time: 177 us -> 182 us (1.028)
  starting transfers between devices: 78.5 us -> 90.8 us
  waiting for transfers between devices: 51.2 us -> 45.7 us
  Pallas kernels: 28.1 us -> 32.3 us
  matrix products: 5.05 us -> 1.61 us
  other arithmetic: 7.87 us -> 6.01 us
    ppermute x40, starting transfers between devices: 66.3 us -> 78.8 us  [exchange(): return lax.ppermute(value, ('sweep', 'z', 'x'), pairs)]
    ppermute x40, waiting for transfers between devices: 51.2 us -> 45.7 us  [exchange(): return lax.ppermute(value, ('sweep', 'z', 'x'), pairs)]
    pallas_call x0 -> x1, Pallas kernels: none -> 4.28 us  [on_device(): pl.pallas_call(solve_kernel, in_specs=[vmem] * 4, out_specs=vmem, out_sha...]
    dot_general x2 -> x0, matrix products: 3.44 us -> none  [the longest x1 3.15 us: on_device(): coupled = jnp.dot(panel, coupling_in, preferred_element_type=F32)]
  transfers between devices with their start and end apart: 41 -> 41, of which waited for: 25 -> 21; matrix products, arithmetic and copies ran while one was open for 5% -> 3% of each run, Pallas kernels for 14% -> 14%
where the time goes in v6:
time: 182 us
  starting transfers between devices  90.8 us (50%)
  waiting for transfers between devices  45.7 us (25%)
  Pallas kernels  32.3 us (18%)
  other arithmetic  6.01 us (3%)
  local copies, waits for them, and re-layouts  5.16 us (3%)
    ppermute x40, starting transfers between devices, exchange(): return lax.ppermute(value, ('sweep', 'z', 'x'), pairs)  78.8 us
    ppermute x40, waiting for transfers between devices, exchange(): return lax.ppermute(value, ('sweep', 'z', 'x'), pairs)  45.7 us
    all_to_all x1, starting transfers between devices, on_device(): lax.all_to_all(packed.reshape(group_size, capacity, width + LANES), ('z',...  12 us
    pallas_call x1, Pallas kernels, on_device(): pl.pallas_call(fold_kernel, grid_spec=pltpu.PrefetchScalarGridSpec(num_sc...  11.9 us
    pallas_call x1, Pallas kernels, on_device(): pl.pallas_call(lambda *refs: outward_kernel(face_dev, *refs), grid_spec=p...  8.46 us
    unnamed x14, local copies, waits for them, and re-layouts  4.69 us
    pallas_call x1, Pallas kernels, on_device(): pl.pallas_call(lambda *refs: source_kernel(face_dev, *refs), in_specs=[vm...  4.51 us
    pallas_call x1, Pallas kernels, on_device(): pl.pallas_call(solve_kernel, in_specs=[vmem] * 4, out_specs=vmem, out_sha...  4.28 us
  transfers between devices with their start and end apart: 41, of which 21 were waited for; matrix products, arithmetic and copies ran while one was open for 3% of the time, Pallas kernels for 14%

profile of v6, /device:TPU:1, one launch (start us, length us, event | category | flops | bytes accessed | tf_op | source)
XLA Modules:
  0.0 181.9 jit_solution(9868749894166513276)
XLA Ops:
  0.0 3.1 %pack.1 = bf16[1024,512]{1,0:T(8,128)(2,1)} custom-call(s32[1,512]{1,0:T(1,128)} %bitcast.45, s32[1,512]{1,0:T(1,128)} %bitcast.46, f32[512,384]{1,0:T(8,128)} %refs_2_.1), custom_call_target="tpu_custom_call" | custom-call | tf_op jit(solution)/shard_map/pack/pack/pallas_call | solution.py:149
  3.1 12.0 %all-to-all-start = ((bf16[32,32,512]{2,1,0:T(8,128)(2,1)}), bf16[32,32,512]{2,1,0:T(8,128)(2,1)S(1)}, u32[]{:S(2)}, u32[]{:S(2)}) async-start(bf16[32,32,512]{2,1,0:T(8,128)(2,1)} %bitcast.42), calls=%async_computation | async-start | bytes 2097152 | tf_op jit(solution)/shard_map/route/all_to_all | solution.py:156
  15.3 2.5 %copy-done.2 = bf16[1,1536,1536]{2,1,0:T(8,128)(2,1)S(1)} copy-done((bf16[1,1536,1536]{2,1,0:T(8,128)(2,1)S(1)}, bf16[1,1536,1536]{2,1,0:T(8,128)(2,1)}, u32[]{:S(2)}) %copy-start.2) | copy-done | bytes 4718616
  17.7 8.5 %outward.1 = (bf16[1536,1536]{1,0:T(8,128)(2,1)S(1)}, bf16[384,1536]{1,0:T(8,128)(2,1)S(1)}) custom-call(s32[2]{0:T(128)S(1)} %pad_add_fusion.refs_0_.side_ref, bf16[4,384,384]{2,1,0:T(8,128)(2,1)S(1)} %bitcast.41, bf16[1536,1536]{1,0:T(8,128)(2,1)S(1)} %bitcast.39, bf16[1536,1536]{1,0:T(8,128)(2,1)} %bitcast.34), custom_call_target="tpu_custom_call" | custom-call | tf_op jit(solution)/shard_map/fold/outward/pallas_call | solution.py:170
  26.3 1.3 collective-permute-start
  27.6 1.8 collective-permute-start.1
  29.4 11.9 %fold.1 = bf16[3,384,1536]{2,1,0:T(8,128)(2,1)S(1)} custom-call(s32[2]{0:T(128)S(1)} %pad_add_fusion.refs_0_.side_ref, bf16[1536,1536]{1,0:T(8,128)(2,1)S(1)} %bitcast.38, bf16[1536,1536]{1,0:T(8,128)(2,1)S(1)} %get-tuple-element.18.outward_ref.refs_2_), custom_call_target="tpu_custom_call" | custom-call | tf_op jit(solution)/shard_map/fold/fold/pallas_call | solution.py:209
  41.3 2.2 %copy-done = bf16[1536,1536]{1,0:T(8,128)(2,1)} copy-done((bf16[1536,1536]{1,0:T(8,128)(2,1)}, bf16[1536,1536]{1,0:T(8,128)(2,1)S(1)}, u32[]{:S(2)}) %copy-start) | copy-done | bytes 4718616
  43.6 2.2 %collective-permute-done = bf16[192,1536]{1,0:T(8,128)(2,1)S(1)} collective-permute-done((bf16[192,1536]{1,0:T(8,128)(2,1)S(1)}, bf16[192,1536]{1,0:T(8,128)(2,1)S(1)}, u32[]{:S(2)}, u32[]{:S(2)}) %collective-permute-start) | collective-permute-done | bytes 589856 | tf_op jit(solution)/shard_map/sum_x/ppermute | solution.py:127
  45.8 1.5 collective-permute-done.1
  47.2 0.3 fusion.5
  47.7 0.4 collective-permute-start.10
  48.2 1.0 collective-permute-start.9
  49.1 4.5 %source.1 = (f32[16,1536]{1,0:T(8,128)}, f32[16,1536]{1,0:T(8,128)}) custom-call(bf16[1024,512]{1,0:T(8,128)(2,1)} %bitcast.43, f32[16,4,384]{2,1,0:T(4,128)} %bitcast.44, bf16[1536,1536]{1,0:T(8,128)(2,1)} %copy-done), custom_call_target="tpu_custom_call" | custom-call | tf_op jit(solution)/shard_map/source/source/pallas_call | solution.py:249
  53.7 0.9 convert_element_type.207
  54.6 0.5 collective-permute-start.2
  55.1 3.3 %collective-permute-start.3 = (bf16[16,1536]{1,0:T(8,128)(2,1)S(1)}, bf16[16,1536]{1,0:T(8,128)(2,1)S(1)}, u32[]{:S(2)}, u32[]{:S(2)}) collective-permute-start(bf16[16,1536]{1,0:T(8,128)(2,1)S(1)} %convert_element_type.207), channel_id=1, source_target_pairs={{0,8},{1,9},{2,10},{3,11},{4,12},{5,13},{6,14},{7,15},{8,0},{9,1},... | collective-permute-start | bytes 147464 | tf_op jit(solution)/shard_map/sum_source/ppermute | solution.py:127
  58.6 1.6 collective-permute-done.3
  60.3 3.3 %collective-permute-done.4 = bf16[16,1536]{1,0:T(8,128)(2,1)S(1)} collective-permute-done((bf16[16,1536]{1,0:T(8,128)(2,1)S(1)}, bf16[16,1536]{1,0:T(8,128)(2,1)S(1)}, u32[]{:S(2)}, u32[]{:S(2)}) %collective-permute-start.4) | collective-permute-done | bytes 49184 | tf_op jit(solution)/shard_map/sum_source/ppermute | solution.py:127
  63.6 0.9 add_convert_fusion.7
  64.5 1.7 collective-permute-start.5
  66.2 2.9 %collective-permute-done.5 = bf16[16,1536]{1,0:T(8,128)(2,1)S(1)} collective-permute-done((bf16[16,1536]{1,0:T(8,128)(2,1)S(1)}, bf16[16,1536]{1,0:T(8,128)(2,1)S(1)}, u32[]{:S(2)}, u32[]{:S(2)}) %collective-permute-start.5) | collective-permute-done | bytes 49184 | tf_op jit(solution)/shard_map/sum_source/ppermute | solution.py:127
  69.4 2.2 %collective-permute-start.7 = (bf16[16,1536]{1,0:T(8,128)(2,1)S(1)}, bf16[16,1536]{1,0:T(8,128)(2,1)S(1)}, u32[]{:S(2)}, u32[]{:S(2)}) collective-permute-start(bf16[16,1536]{1,0:T(8,128)(2,1)S(1)} %add_convert_fusion.6), channel_id=1, source_target_pairs={{0,2},{1,3},{2,0},{3,1},{4,6},{5,7},{6,4},{7,5},{8,10},{9,11},{10,... | collective-permute-start | bytes 147464 | tf_op jit(solution)/shard_map/sum_source/ppermute | solution.py:127
  71.6 1.5 collective-permute-start.8
  73.1 1.6 collective-permute-done.9
  74.7 2.4 %fusion.1 = bf16[384,1536]{1,0:T(8,128)(2,1)S(1)} fusion(bf16[384,1536]{1,0:T(8,128)(2,1)} %collective-permute-done.10, bf16[384,1536]{1,0:T(8,128)(2,1)} %collective-permute-done.9, bf16[3,384,1536]{2,1,0:T(8,128)(2,1)} %copy-done.1), kind=kLoop, calls=%fused_computation.2 | loop fusion | flops 3538944 | bytes 4718592 | tf_op jit(solution)/shard_map/sum_x/convert_element_type | solution.py:246
  77.3 0.4 collective-permute-start.11
  77.8 2.2 %collective-permute-start.17 = (bf16[96,1536]{1,0:T(8,128)(2,1)S(1)}, bf16[96,1536]{1,0:T(8,128)(2,1)S(1)}, u32[]{:S(2)}, u32[]{:S(2)}) collective-permute-start(bf16[96,1536]{1,0:T(8,128)(2,1)S(1)} %constant_dynamic-slice_fusion.1), channel_id=1, source_target_pairs={{0,28},{1,29},{2,30},{3,31},{4,8},{5,9},{6,10},{7,11},{8,4},{9,5},... | collective-permute-start | bytes 884744 | tf_op jit(solution)/shard_map/sum_z/ppermute | solution.py:127
  80.0 2.9 %collective-permute-done.11 = bf16[96,1536]{1,0:T(8,128)(2,1)S(1)} collective-permute-done((bf16[96,1536]{1,0:T(8,128)(2,1)S(1)}, bf16[96,1536]{1,0:T(8,128)(2,1)S(1)}, u32[]{:S(2)}, u32[]{:S(2)}) %collective-permute-start.11) | collective-permute-done | bytes 294944 | tf_op jit(solution)/shard_map/sum_z/ppermute | solution.py:127
  83.0 2.4 %collective-permute-start.13 = (bf16[48,1536]{1,0:T(8,128)(2,1)S(1)}, bf16[48,1536]{1,0:T(8,128)(2,1)S(1)}, u32[]{:S(2)}, u32[]{:S(2)}) collective-permute-start(bf16[48,1536]{1,0:T(8,128)(2,1)S(1)} %constant_dynamic-slice_fusion.2), channel_id=1, source_target_pairs={{0,28},{1,29},{2,30},{3,31},{4,8},{5,9},{6,10},{7,11},{8,4},{9,5},... | collective-permute-start | bytes 442376 | tf_op jit(solution)/shard_map/sum_z/ppermute | solution.py:127
  85.5 1.1 collective-permute-start.18
  86.6 5.9 %collective-permute-start.12 = (bf16[16,384]{1,0:T(8,128)(2,1)S(1)}, bf16[16,384]{1,0:T(8,128)(2,1)S(1)}, u32[]{:S(2)}, u32[]{:S(2)}) collective-permute-start(bf16[16,384]{1,0:T(8,128)(2,1)S(1)} %dynamic-slice_convert_fusion), channel_id=1, source_target_pairs={{0,32},{1,33},{2,34},{3,35},{4,36},{5,37},{6,38},{7,39},{8,40},{9,... | collective-permute-start | bytes 36872 | tf_op jit(solution)/shard_map/stage0/ppermute | solution.py:127
  92.5 2.8 %collective-permute-start.14 = (bf16[48,1536]{1,0:T(8,128)(2,1)S(1)}, bf16[48,1536]{1,0:T(8,128)(2,1)S(1)}, u32[]{:S(2)}, u32[]{:S(2)}) collective-permute-start(bf16[48,1536]{1,0:T(8,128)(2,1)S(1)} %add_convert_fusion.5), channel_id=1, source_target_pairs={{0,12},{1,13},{2,14},{3,15},{4,24},{5,25},{6,26},{7,27},{8,20},{9,... | collective-permute-start | bytes 442376 | tf_op jit(solution)/shard_map/sum_z/ppermute | solution.py:127
  95.4 3.8 %collective-permute-start.19 = (bf16[48,1536]{1,0:T(8,128)(2,1)S(1)}, bf16[48,1536]{1,0:T(8,128)(2,1)S(1)}, u32[]{:S(2)}, u32[]{:S(2)}) collective-permute-start(bf16[48,1536]{1,0:T(8,128)(2,1)S(1)} %add_convert_fusion.3), channel_id=1, source_target_pairs={{0,20},{1,21},{2,22},{3,23},{4,16},{5,17},{6,18},{7,19},{8,28},{9,... | collective-permute-start | bytes 442376 | tf_op jit(solution)/shard_map/sum_z/ppermute | solution.py:127
  99.6 1.6 collective-permute-start.15
  101.2 6.4 %collective-permute-done.19 = bf16[48,1536]{1,0:T(8,128)(2,1)S(1)} collective-permute-done((bf16[48,1536]{1,0:T(8,128)(2,1)S(1)}, bf16[48,1536]{1,0:T(8,128)(2,1)S(1)}, u32[]{:S(2)}, u32[]{:S(2)}) %collective-permute-start.19) | collective-permute-done | bytes 147488 | tf_op jit(solution)/shard_map/sum_z/ppermute | solution.py:127
  107.6 4.6 %collective-permute-start.20 = (bf16[48,1536]{1,0:T(8,128)(2,1)S(1)}, bf16[48,1536]{1,0:T(8,128)(2,1)S(1)}, u32[]{:S(2)}, u32[]{:S(2)}) collective-permute-start(bf16[48,1536]{1,0:T(8,128)(2,1)S(1)} %add_convert_fusion.2), channel_id=1, source_target_pairs={{0,4},{1,5},{2,6},{3,7},{4,0},{5,1},{6,2},{7,3},{8,12},{9,13},{10,... | collective-permute-start | bytes 442376 | tf_op jit(solution)/shard_map/sum_z/ppermute | solution.py:127
  112.3 2.1 %collective-permute-start.16 = (bf16[96,1536]{1,0:T(8,128)(2,1)S(1)}, bf16[96,1536]{1,0:T(8,128)(2,1)S(1)}, u32[]{:S(2)}, u32[]{:S(2)}) collective-permute-start(bf16[96,1536]{1,0:T(8,128)(2,1)S(1)} %constant_dynamic-update-slice_fusion.7), channel_id=1, source_target_pairs={{0,4},{1,5},{2,6},{3,7},{4,0},{5,1},{6,2},{7,3},{8,12},{9,13},{10,... | collective-permute-start | bytes 884744 | tf_op jit(solution)/shard_map/sum_z/ppermute | solution.py:127
  114.4 1.5 collective-permute-done.20
  116.2 6.1 %collective-permute-done.16 = bf16[96,1536]{1,0:T(8,128)(2,1)S(1)} collective-permute-done((bf16[96,1536]{1,0:T(8,128)(2,1)S(1)}, bf16[96,1536]{1,0:T(8,128)(2,1)S(1)}, u32[]{:S(2)}, u32[]{:S(2)}) %collective-permute-start.16) | collective-permute-done | bytes 294944 | tf_op jit(solution)/shard_map/sum_z/ppermute | solution.py:127
  122.3 1.7 collective-permute-done.21
  124.2 4.0 %collective-permute-start.22 = (bf16[16,1536]{1,0:T(8,128)(2,1)S(1)}, bf16[16,1536]{1,0:T(8,128)(2,1)S(1)}, u32[]{:S(2)}, u32[]{:S(2)}) collective-permute-start(bf16[16,1536]{1,0:T(8,128)(2,1)S(1)} %fusion.2), channel_id=1, source_target_pairs={{0,224},{1,225},{2,226},{3,227},{4,228},{5,229},{6,230},{7,231},{8... | collective-permute-start | bytes 147464 | tf_op jit(solution)/shard_map/stage1/ppermute | solution.py:127
  128.2 3.3 %collective-permute-start.24 = (bf16[16,1536]{1,0:T(8,128)(2,1)S(1)}, bf16[16,1536]{1,0:T(8,128)(2,1)S(1)}, u32[]{:S(2)}, u32[]{:S(2)}) collective-permute-start(bf16[16,1536]{1,0:T(8,128)(2,1)S(1)} %fusion.2), channel_id=1, source_target_pairs={{0,226},{1,227},{2,224},{3,225},{4,230},{5,231},{6,228},{7,229},{8... | collective-permute-start | bytes 147464 | tf_op jit(solution)/shard_map/stage1/ppermute | solution.py:127
  131.5 1.6 collective-permute-start.25
  133.2 1.2 collective-permute-done.24
  134.4 2.7 %collective-permute-done.25 = bf16[16,1536]{1,0:T(8,128)(2,1)S(1)} collective-permute-done((bf16[16,1536]{1,0:T(8,128)(2,1)S(1)}, bf16[16,1536]{1,0:T(8,128)(2,1)S(1)}, u32[]{:S(2)}, u32[]{:S(2)}) %collective-permute-start.25) | collective-permute-done | bytes 49184 | tf_op jit(solution)/shard_map/stage1/ppermute | solution.py:127
  137.4 2.3 %collective-permute-start.26 = (bf16[16,384]{1,0:T(8,128)(2,1)S(1)}, bf16[16,384]{1,0:T(8,128)(2,1)S(1)}, u32[]{:S(2)}, u32[]{:S(2)}) collective-permute-start(bf16[16,384]{1,0:T(8,128)(2,1)S(1)} %fusion.7), channel_id=1, source_target_pairs={{0,32},{1,33},{2,34},{3,35},{4,36},{5,37},{6,38},{7,39},{8,40},{9,... | collective-permute-start | bytes 36872 | tf_op jit(solution)/shard_map/stage2/ppermute | solution.py:127
  139.7 0.8 collective-permute-done.26
  140.9 0.8 collective-permute-start.28
  141.6 2.7 %collective-permute-start.29 = (bf16[16,1536]{1,0:T(8,128)(2,1)S(1)}, bf16[16,1536]{1,0:T(8,128)(2,1)S(1)}, u32[]{:S(2)}, u32[]{:S(2)}) collective-permute-start(bf16[16,1536]{1,0:T(8,128)(2,1)S(1)} %fusion.3), channel_id=1, source_target_pairs={{0,226},{1,227},{2,224},{3,225},{4,230},{5,231},{6,228},{7,229},{8... | collective-permute-start | bytes 147464 | tf_op jit(solution)/shard_map/stage3/ppermute | solution.py:127
  144.4 3.0 %collective-permute-start.30 = (bf16[16,1536]{1,0:T(8,128)(2,1)S(1)}, bf16[16,1536]{1,0:T(8,128)(2,1)S(1)}, u32[]{:S(2)}, u32[]{:S(2)}) collective-permute-start(bf16[16,1536]{1,0:T(8,128)(2,1)S(1)} %fusion.3), channel_id=1, source_target_pairs={{0,227},{1,226},{2,225},{3,224},{4,231},{5,230},{6,229},{7,228},{8... | collective-permute-start | bytes 147464 | tf_op jit(solution)/shard_map/stage3/ppermute | solution.py:127
  147.6 2.9 %collective-permute-done.30 = bf16[16,1536]{1,0:T(8,128)(2,1)S(1)} collective-permute-done((bf16[16,1536]{1,0:T(8,128)(2,1)S(1)}, bf16[16,1536]{1,0:T(8,128)(2,1)S(1)}, u32[]{:S(2)}, u32[]{:S(2)}) %collective-permute-start.30) | collective-permute-done | bytes 49184 | tf_op jit(solution)/shard_map/stage3/ppermute | solution.py:127
  150.7 5.1 %collective-permute-start.31 = (bf16[16,384]{1,0:T(8,128)(2,1)S(1)}, bf16[16,384]{1,0:T(8,128)(2,1)S(1)}, u32[]{:S(2)}, u32[]{:S(2)}) collective-permute-start(bf16[16,384]{1,0:T(8,128)(2,1)S(1)} %fusion.8), channel_id=1, source_target_pairs={{0,32},{1,33},{2,34},{3,35},{4,36},{5,37},{6,38},{7,39},{8,40},{9,... | collective-permute-start | bytes 36872 | tf_op jit(solution)/shard_map/stage4/ppermute | solution.py:127
  155.9 0.8 collective-permute-done.31
  157.1 3.2 %collective-permute-start.34 = (bf16[16,1536]{1,0:T(8,128)(2,1)S(1)}, bf16[16,1536]{1,0:T(8,128)(2,1)S(1)}, u32[]{:S(2)}, u32[]{:S(2)}) collective-permute-start(bf16[16,1536]{1,0:T(8,128)(2,1)S(1)} %fusion.4), channel_id=1, source_target_pairs={{0,226},{1,227},{2,224},{3,225},{4,230},{5,231},{6,228},{7,229},{8... | collective-permute-start | bytes 147464 | tf_op jit(solution)/shard_map/stage5/ppermute | solution.py:127
  160.3 3.2 %collective-permute-start.35 = (bf16[16,1536]{1,0:T(8,128)(2,1)S(1)}, bf16[16,1536]{1,0:T(8,128)(2,1)S(1)}, u32[]{:S(2)}, u32[]{:S(2)}) collective-permute-start(bf16[16,1536]{1,0:T(8,128)(2,1)S(1)} %fusion.4), channel_id=1, source_target_pairs={{0,227},{1,226},{2,225},{3,224},{4,231},{5,230},{6,229},{7,228},{8... | collective-permute-start | bytes 147464 | tf_op jit(solution)/shard_map/stage5/ppermute | solution.py:127
  163.5 2.4 %collective-permute-done.35 = bf16[16,1536]{1,0:T(8,128)(2,1)S(1)} collective-permute-done((bf16[16,1536]{1,0:T(8,128)(2,1)S(1)}, bf16[16,1536]{1,0:T(8,128)(2,1)S(1)}, u32[]{:S(2)}, u32[]{:S(2)}) %collective-permute-start.35) | collective-permute-done | bytes 49184 | tf_op jit(solution)/shard_map/stage5/ppermute | solution.py:127
  166.3 3.8 %collective-permute-start.36 = (bf16[16,384]{1,0:T(8,128)(2,1)S(1)}, bf16[16,384]{1,0:T(8,128)(2,1)S(1)}, u32[]{:S(2)}, u32[]{:S(2)}) collective-permute-start(bf16[16,384]{1,0:T(8,128)(2,1)S(1)} %fusion.9), channel_id=1, source_target_pairs={{0,32},{1,33},{2,34},{3,35},{4,36},{5,37},{6,38},{7,39},{8,40},{9,... | collective-permute-start | bytes 36872 | tf_op jit(solution)/shard_map/spread/ppermute | solution.py:127
  170.1 2.5 %collective-permute-start.38 = (bf16[16,384]{1,0:T(8,128)(2,1)S(1)}, bf16[16,384]{1,0:T(8,128)(2,1)S(1)}, u32[]{:S(2)}, u32[]{:S(2)}) collective-permute-start(bf16[16,384]{1,0:T(8,128)(2,1)S(1)} %fusion.9), channel_id=1, source_target_pairs={{0,34},{1,35},{2,32},{3,33},{4,38},{5,39},{6,36},{7,37},{8,42},{9,... | collective-permute-start | bytes 36872 | tf_op jit(solution)/shard_map/spread/ppermute | solution.py:127
  172.6 1.7 collective-permute-start.39
  174.3 0.4 collective-permute-done.38
  174.7 2.2 %collective-permute-done.39 = bf16[16,384]{1,0:T(8,128)(2,1)S(1)} collective-permute-done((bf16[16,384]{1,0:T(8,128)(2,1)S(1)}, bf16[16,384]{1,0:T(8,128)(2,1)S(1)}, u32[]{:S(2)}, u32[]{:S(2)}) %collective-permute-start.39) | collective-permute-done | bytes 12320 | tf_op jit(solution)/shard_map/spread/ppermute | solution.py:127
  176.9 0.6 broadcast_select_fusion.panel_ref
  177.6 4.3 %solve.1 = f32[16,4,384]{2,1,0:T(4,128)} custom-call(bf16[16,1536]{1,0:T(8,128)(2,1)} %broadcast_select_fusion.panel_ref, bf16[1536,1536]{1,0:T(8,128)(2,1)} %bitcast.35, f32[16,1536]{1,0:T(8,128)} %get-tuple-element.26.assembled_ref, bf16[4,384,384]{2,1,0:T(8,128)(2,1)} %bitcast.40), custom_call_target="tpu_custom_call" | custom-call | tf_op jit(solution)/shard_map/solve/solve/pallas_call | solution.py:329
  (82 shorter events, 4.4 us)
Async XLA Ops:
  3.1 12.1 %copy-start.3 = (bf16[1,4,384,384]{3,2,1,0:T(8,128)(2,1)S(1)}, bf16[1,4,384,384]{3,2,1,0:T(8,128)(2,1)}, u32[]{:S(2)}) copy-start(bf16[1,4,384,384]{3,2,1,0:T(8,128)(2,1)} %param.11) | copy-start | bytes 3538948
  3.1 44.6 %all-to-all-start = ((bf16[32,32,512]{2,1,0:T(8,128)(2,1)}), bf16[32,32,512]{2,1,0:T(8,128)(2,1)S(1)}, u32[]{:S(2)}, u32[]{:S(2)}) async-start(bf16[32,32,512]{2,1,0:T(8,128)(2,1)} %bitcast.42), calls=%async_computation | async-start | bytes 2097152 | tf_op jit(solution)/shard_map/route/all_to_all | solution.py:156
  15.2 14.2 %slice-start = ((s8[4718592]{0:T(1024)(128)(4,1)}), s8[4194304]{0:T(1024)(128)(4,1)S(1)}, s32[]{:S(2)}) async-start(s8[4718592]{0:T(1024)(128)(4,1)} %bitcast.36), calls=%async_computation.1 | async-start | bytes 8388608
  15.2 2.5 %copy-start.2 = (bf16[1,1536,1536]{2,1,0:T(8,128)(2,1)S(1)}, bf16[1,1536,1536]{2,1,0:T(8,128)(2,1)}, u32[]{:S(2)}) copy-start(bf16[1,1536,1536]{2,1,0:T(8,128)(2,1)} %param.13) | copy-start | bytes 14155780
  17.7 11.7 %slice-start.1 = ((s8[4718592]{0:T(1024)(128)(4,1)}), s8[524288]{0:T(1024)(128)(4,1)S(1)}, s32[]{:S(2)}) async-start(s8[4718592]{0:T(1024)(128)(4,1)} %bitcast.36), calls=%async_computation.2 | async-start | bytes 1048576
  26.3 19.5 %collective-permute-start = (bf16[192,1536]{1,0:T(8,128)(2,1)S(1)}, bf16[192,1536]{1,0:T(8,128)(2,1)S(1)}, u32[]{:S(2)}, u32[]{:S(2)}) collective-permute-start(bf16[192,1536]{1,0:T(8,128)(2,1)S(1)} %get-tuple-element.38), channel_id=1, source_target_pairs={{0,1},{1,0},{2,3},{3,2},{4,5},{5,4},{6,7},{7,6},{8,9},{9,8},{10,11... | collective-permute-start | bytes 1769480 | tf_op jit(solution)/shard_map/sum_x/ppermute | solution.py:127
  27.6 19.6 %collective-permute-start.1 = (bf16[192,1536]{1,0:T(8,128)(2,1)S(1)}, bf16[192,1536]{1,0:T(8,128)(2,1)S(1)}, u32[]{:S(2)}, u32[]{:S(2)}) collective-permute-start(bf16[192,1536]{1,0:T(8,128)(2,1)S(1)} %get-tuple-element.37), channel_id=1, source_target_pairs={{0,3},{1,2},{2,1},{3,0},{4,7},{5,6},{6,5},{7,4},{8,11},{9,10},{10,... | collective-permute-start | bytes 1769480 | tf_op jit(solution)/shard_map/sum_x/ppermute | solution.py:127
  41.3 2.2 %copy-start = (bf16[1536,1536]{1,0:T(8,128)(2,1)}, bf16[1536,1536]{1,0:T(8,128)(2,1)S(1)}, u32[]{:S(2)}) copy-start(bf16[1536,1536]{1,0:T(8,128)(2,1)S(1)} %get-tuple-element.18.outward_ref.refs_2_) | copy-start | bytes 14155780
  43.5 3.8 %copy-start.1 = (bf16[3,384,1536]{2,1,0:T(8,128)(2,1)}, bf16[3,384,1536]{2,1,0:T(8,128)(2,1)S(1)}, u32[]{:S(2)}) copy-start(bf16[3,384,1536]{2,1,0:T(8,128)(2,1)S(1)} %fold.1) | copy-start | bytes 10616836
  47.7 1.4 copy-start.4
  47.7 25.4 %collective-permute-start.10 = (bf16[384,1536]{1,0:T(8,128)(2,1)S(1)}, bf16[384,1536]{1,0:T(8,128)(2,1)}, u32[]{:S(2)}, u32[]{:S(2)}) collective-permute-start(bf16[384,1536]{1,0:T(8,128)(2,1)S(1)} %get-tuple-element.23), channel_id=1, source_target_pairs={{0,1},{1,0},{2,3},{3,2},{4,5},{5,4},{6,7},{7,6},{8,9},{9,8},{10,11... | collective-permute-start | bytes 3538952 | tf_op jit(solution)/shard_map/sum_x/ppermute | solution.py:127
  48.2 26.6 %collective-permute-start.9 = (bf16[384,1536]{1,0:T(8,128)(2,1)S(1)}, bf16[384,1536]{1,0:T(8,128)(2,1)}, u32[]{:S(2)}, u32[]{:S(2)}) collective-permute-start(bf16[384,1536]{1,0:T(8,128)(2,1)S(1)} %get-tuple-element.22), channel_id=1, source_target_pairs={{0,3},{1,2},{2,1},{3,0},{4,7},{5,6},{6,5},{7,4},{8,11},{9,10},{10,... | collective-permute-start | bytes 3538952 | tf_op jit(solution)/shard_map/sum_x/ppermute | solution.py:127
  54.6 4.1 %collective-permute-start.2 = (bf16[16,1536]{1,0:T(8,128)(2,1)S(1)}, bf16[16,1536]{1,0:T(8,128)(2,1)S(1)}, u32[]{:S(2)}, u32[]{:S(2)}) collective-permute-start(bf16[16,1536]{1,0:T(8,128)(2,1)S(1)} %convert_element_type.207), channel_id=1, source_target_pairs={{0,4},{1,5},{2,6},{3,7},{4,0},{5,1},{6,2},{7,3},{8,12},{9,13},{10,... | collective-permute-start | bytes 147464 | tf_op jit(solution)/shard_map/sum_source/ppermute | solution.py:127
  55.1 5.2 %collective-permute-start.3 = (bf16[16,1536]{1,0:T(8,128)(2,1)S(1)}, bf16[16,1536]{1,0:T(8,128)(2,1)S(1)}, u32[]{:S(2)}, u32[]{:S(2)}) collective-permute-start(bf16[16,1536]{1,0:T(8,128)(2,1)S(1)} %convert_element_type.207), channel_id=1, source_target_pairs={{0,8},{1,9},{2,10},{3,11},{4,12},{5,13},{6,14},{7,15},{8,0},{9,1},... | collective-permute-start | bytes 147464 | tf_op jit(solution)/shard_map/sum_source/ppermute | solution.py:127
  58.4 5.2 %collective-permute-start.4 = (bf16[16,1536]{1,0:T(8,128)(2,1)S(1)}, bf16[16,1536]{1,0:T(8,128)(2,1)S(1)}, u32[]{:S(2)}, u32[]{:S(2)}) collective-permute-start(bf16[16,1536]{1,0:T(8,128)(2,1)S(1)} %convert_element_type.207), channel_id=1, source_target_pairs={{0,12},{1,13},{2,14},{3,15},{4,8},{5,9},{6,10},{7,11},{8,4},{9,5},... | collective-permute-start | bytes 147464 | tf_op jit(solution)/shard_map/sum_source/ppermute | solution.py:127
  64.5 4.6 %collective-permute-start.5 = (bf16[16,1536]{1,0:T(8,128)(2,1)S(1)}, bf16[16,1536]{1,0:T(8,128)(2,1)S(1)}, u32[]{:S(2)}, u32[]{:S(2)}) collective-permute-start(bf16[16,1536]{1,0:T(8,128)(2,1)S(1)} %add_convert_fusion.7), channel_id=1, source_target_pairs={{0,28},{1,29},{2,30},{3,31},{4,24},{5,25},{6,26},{7,27},{8,20},{9,... | collective-permute-start | bytes 147464 | tf_op jit(solution)/shard_map/sum_source/ppermute | solution.py:127
  69.2 8.5 %collective-permute-start.6 = (bf16[16,1536]{1,0:T(8,128)(2,1)S(1)}, bf16[16,1536]{1,0:T(8,128)(2,1)S(1)}, u32[]{:S(2)}, u32[]{:S(2)}) collective-permute-start(bf16[16,1536]{1,0:T(8,128)(2,1)S(1)} %add_convert_fusion.6), channel_id=1, source_target_pairs={{0,1},{1,0},{2,3},{3,2},{4,5},{5,4},{6,7},{7,6},{8,9},{9,8},{10,11... | collective-permute-start | bytes 147464 | tf_op jit(solution)/shard_map/sum_source/ppermute | solution.py:127
  69.4 8.2 %collective-permute-start.7 = (bf16[16,1536]{1,0:T(8,128)(2,1)S(1)}, bf16[16,1536]{1,0:T(8,128)(2,1)S(1)}, u32[]{:S(2)}, u32[]{:S(2)}) collective-permute-start(bf16[16,1536]{1,0:T(8,128)(2,1)S(1)} %add_convert_fusion.6), channel_id=1, source_target_pairs={{0,2},{1,3},{2,0},{3,1},{4,6},{5,7},{6,4},{7,5},{8,10},{9,11},{10,... | collective-permute-start | bytes 147464 | tf_op jit(solution)/shard_map/sum_source/ppermute | solution.py:127
  71.6 6.1 %collective-permute-start.8 = (bf16[16,1536]{1,0:T(8,128)(2,1)S(1)}, bf16[16,1536]{1,0:T(8,128)(2,1)S(1)}, u32[]{:S(2)}, u32[]{:S(2)}) collective-permute-start(bf16[16,1536]{1,0:T(8,128)(2,1)S(1)} %add_convert_fusion.6), channel_id=1, source_target_pairs={{0,3},{1,2},{2,1},{3,0},{4,7},{5,6},{6,5},{7,4},{8,11},{9,10},{10,... | collective-permute-start | bytes 147464 | tf_op jit(solution)/shard_map/sum_source/ppermute | solution.py:127
  77.3 5.7 %collective-permute-start.11 = (bf16[96,1536]{1,0:T(8,128)(2,1)S(1)}, bf16[96,1536]{1,0:T(8,128)(2,1)S(1)}, u32[]{:S(2)}, u32[]{:S(2)}) collective-permute-start(bf16[96,1536]{1,0:T(8,128)(2,1)S(1)} %constant_dynamic-slice_fusion.3), channel_id=1, source_target_pairs={{0,4},{1,5},{2,6},{3,7},{4,0},{5,1},{6,2},{7,3},{8,12},{9,13},{10,... | collective-permute-start | bytes 884744 | tf_op jit(solution)/shard_map/sum_z/ppermute | solution.py:127
  77.8 7.6 %collective-permute-start.17 = (bf16[96,1536]{1,0:T(8,128)(2,1)S(1)}, bf16[96,1536]{1,0:T(8,128)(2,1)S(1)}, u32[]{:S(2)}, u32[]{:S(2)}) collective-permute-start(bf16[96,1536]{1,0:T(8,128)(2,1)S(1)} %constant_dynamic-slice_fusion.1), channel_id=1, source_target_pairs={{0,28},{1,29},{2,30},{3,31},{4,8},{5,9},{6,10},{7,11},{8,4},{9,5},... | collective-permute-start | bytes 884744 | tf_op jit(solution)/shard_map/sum_z/ppermute | solution.py:127
  83.0 9.5 %collective-permute-start.13 = (bf16[48,1536]{1,0:T(8,128)(2,1)S(1)}, bf16[48,1536]{1,0:T(8,128)(2,1)S(1)}, u32[]{:S(2)}, u32[]{:S(2)}) collective-permute-start(bf16[48,1536]{1,0:T(8,128)(2,1)S(1)} %constant_dynamic-slice_fusion.2), channel_id=1, source_target_pairs={{0,28},{1,29},{2,30},{3,31},{4,8},{5,9},{6,10},{7,11},{8,4},{9,5},... | collective-permute-start | bytes 442376 | tf_op jit(solution)/shard_map/sum_z/ppermute | solution.py:127
  85.5 9.9 %collective-permute-start.18 = (bf16[48,1536]{1,0:T(8,128)(2,1)S(1)}, bf16[48,1536]{1,0:T(8,128)(2,1)S(1)}, u32[]{:S(2)}, u32[]{:S(2)}) collective-permute-start(bf16[48,1536]{1,0:T(8,128)(2,1)S(1)} %constant_dynamic-slice_fusion), channel_id=1, source_target_pairs={{0,4},{1,5},{2,6},{3,7},{4,0},{5,1},{6,2},{7,3},{8,12},{9,13},{10,... | collective-permute-start | bytes 442376 | tf_op jit(solution)/shard_map/sum_z/ppermute | solution.py:127
  86.6 37.3 %collective-permute-start.12 = (bf16[16,384]{1,0:T(8,128)(2,1)S(1)}, bf16[16,384]{1,0:T(8,128)(2,1)S(1)}, u32[]{:S(2)}, u32[]{:S(2)}) collective-permute-start(bf16[16,384]{1,0:T(8,128)(2,1)S(1)} %dynamic-slice_convert_fusion), channel_id=1, source_target_pairs={{0,32},{1,33},{2,34},{3,35},{4,36},{5,37},{6,38},{7,39},{8,40},{9,... | collective-permute-start | bytes 36872 | tf_op jit(solution)/shard_map/stage0/ppermute | solution.py:127
  92.5 7.0 %collective-permute-start.14 = (bf16[48,1536]{1,0:T(8,128)(2,1)S(1)}, bf16[48,1536]{1,0:T(8,128)(2,1)S(1)}, u32[]{:S(2)}, u32[]{:S(2)}) collective-permute-start(bf16[48,1536]{1,0:T(8,128)(2,1)S(1)} %add_convert_fusion.5), channel_id=1, source_target_pairs={{0,12},{1,13},{2,14},{3,15},{4,24},{5,25},{6,26},{7,27},{8,20},{9,... | collective-permute-start | bytes 442376 | tf_op jit(solution)/shard_map/sum_z/ppermute | solution.py:127
  95.4 12.1 %collective-permute-start.19 = (bf16[48,1536]{1,0:T(8,128)(2,1)S(1)}, bf16[48,1536]{1,0:T(8,128)(2,1)S(1)}, u32[]{:S(2)}, u32[]{:S(2)}) collective-permute-start(bf16[48,1536]{1,0:T(8,128)(2,1)S(1)} %add_convert_fusion.3), channel_id=1, source_target_pairs={{0,20},{1,21},{2,22},{3,23},{4,16},{5,17},{6,18},{7,19},{8,28},{9,... | collective-permute-start | bytes 442376 | tf_op jit(solution)/shard_map/sum_z/ppermute | solution.py:127
  99.6 12.7 %collective-permute-start.15 = (bf16[48,1536]{1,0:T(8,128)(2,1)S(1)}, bf16[48,1536]{1,0:T(8,128)(2,1)S(1)}, u32[]{:S(2)}, u32[]{:S(2)}) collective-permute-start(bf16[48,1536]{1,0:T(8,128)(2,1)S(1)} %add_convert_fusion.4), channel_id=1, source_target_pairs={{0,28},{1,29},{2,30},{3,31},{4,8},{5,9},{6,10},{7,11},{8,4},{9,5},... | collective-permute-start | bytes 442376 | tf_op jit(solution)/shard_map/sum_z/ppermute | solution.py:127
  107.6 8.3 %collective-permute-start.20 = (bf16[48,1536]{1,0:T(8,128)(2,1)S(1)}, bf16[48,1536]{1,0:T(8,128)(2,1)S(1)}, u32[]{:S(2)}, u32[]{:S(2)}) collective-permute-start(bf16[48,1536]{1,0:T(8,128)(2,1)S(1)} %add_convert_fusion.2), channel_id=1, source_target_pairs={{0,4},{1,5},{2,6},{3,7},{4,0},{5,1},{6,2},{7,3},{8,12},{9,13},{10,... | collective-permute-start | bytes 442376 | tf_op jit(solution)/shard_map/sum_z/ppermute | solution.py:127
  112.3 10.0 %collective-permute-start.16 = (bf16[96,1536]{1,0:T(8,128)(2,1)S(1)}, bf16[96,1536]{1,0:T(8,128)(2,1)S(1)}, u32[]{:S(2)}, u32[]{:S(2)}) collective-permute-start(bf16[96,1536]{1,0:T(8,128)(2,1)S(1)} %constant_dynamic-update-slice_fusion.7), channel_id=1, source_target_pairs={{0,4},{1,5},{2,6},{3,7},{4,0},{5,1},{6,2},{7,3},{8,12},{9,13},{10,... | collective-permute-start | bytes 884744 | tf_op jit(solution)/shard_map/sum_z/ppermute | solution.py:127
  115.9 8.0 %collective-permute-start.21 = (bf16[96,1536]{1,0:T(8,128)(2,1)S(1)}, bf16[96,1536]{1,0:T(8,128)(2,1)S(1)}, u32[]{:S(2)}, u32[]{:S(2)}) collective-permute-start(bf16[96,1536]{1,0:T(8,128)(2,1)S(1)} %constant_dynamic-update-slice_fusion.5), channel_id=1, source_target_pairs={{0,28},{1,29},{2,30},{3,31},{4,8},{5,9},{6,10},{7,11},{8,4},{9,5},... | collective-permute-start | bytes 884744 | tf_op jit(solution)/shard_map/sum_z/ppermute | solution.py:127
  124.2 8.9 %collective-permute-start.22 = (bf16[16,1536]{1,0:T(8,128)(2,1)S(1)}, bf16[16,1536]{1,0:T(8,128)(2,1)S(1)}, u32[]{:S(2)}, u32[]{:S(2)}) collective-permute-start(bf16[16,1536]{1,0:T(8,128)(2,1)S(1)} %fusion.2), channel_id=1, source_target_pairs={{0,224},{1,225},{2,226},{3,227},{4,228},{5,229},{6,230},{7,231},{8... | collective-permute-start | bytes 147464 | tf_op jit(solution)/shard_map/stage1/ppermute | solution.py:127
  128.2 5.0 %collective-permute-start.23 = (bf16[16,1536]{1,0:T(8,128)(2,1)S(1)}, bf16[16,1536]{1,0:T(8,128)(2,1)S(1)}, u32[]{:S(2)}, u32[]{:S(2)}) collective-permute-start(bf16[16,1536]{1,0:T(8,128)(2,1)S(1)} %fusion.2), channel_id=1, source_target_pairs={{0,225},{1,224},{2,227},{3,226},{4,229},{5,228},{6,231},{7,230},{8... | collective-permute-start | bytes 147464 | tf_op jit(solution)/shard_map/stage1/ppermute | solution.py:127
  128.2 6.2 %collective-permute-start.24 = (bf16[16,1536]{1,0:T(8,128)(2,1)S(1)}, bf16[16,1536]{1,0:T(8,128)(2,1)S(1)}, u32[]{:S(2)}, u32[]{:S(2)}) collective-permute-start(bf16[16,1536]{1,0:T(8,128)(2,1)S(1)} %fusion.2), channel_id=1, source_target_pairs={{0,226},{1,227},{2,224},{3,225},{4,230},{5,231},{6,228},{7,229},{8... | collective-permute-start | bytes 147464 | tf_op jit(solution)/shard_map/stage1/ppermute | solution.py:127
  131.5 5.6 %collective-permute-start.25 = (bf16[16,1536]{1,0:T(8,128)(2,1)S(1)}, bf16[16,1536]{1,0:T(8,128)(2,1)S(1)}, u32[]{:S(2)}, u32[]{:S(2)}) collective-permute-start(bf16[16,1536]{1,0:T(8,128)(2,1)S(1)} %fusion.2), channel_id=1, source_target_pairs={{0,227},{1,226},{2,225},{3,224},{4,231},{5,230},{6,229},{7,228},{8... | collective-permute-start | bytes 147464 | tf_op jit(solution)/shard_map/stage1/ppermute | solution.py:127
  137.4 3.2 %collective-permute-start.26 = (bf16[16,384]{1,0:T(8,128)(2,1)S(1)}, bf16[16,384]{1,0:T(8,128)(2,1)S(1)}, u32[]{:S(2)}, u32[]{:S(2)}) collective-permute-start(bf16[16,384]{1,0:T(8,128)(2,1)S(1)} %fusion.7), channel_id=1, source_target_pairs={{0,32},{1,33},{2,34},{3,35},{4,36},{5,37},{6,38},{7,39},{8,40},{9,... | collective-permute-start | bytes 36872 | tf_op jit(solution)/shard_map/stage2/ppermute | solution.py:127
  140.8 6.6 %collective-permute-start.27 = (bf16[16,1536]{1,0:T(8,128)(2,1)S(1)}, bf16[16,1536]{1,0:T(8,128)(2,1)S(1)}, u32[]{:S(2)}, u32[]{:S(2)}) collective-permute-start(bf16[16,1536]{1,0:T(8,128)(2,1)S(1)} %fusion.3), channel_id=1, source_target_pairs={{0,224},{1,225},{2,226},{3,227},{4,228},{5,229},{6,230},{7,231},{8... | collective-permute-start | bytes 147464 | tf_op jit(solution)/shard_map/stage3/ppermute | solution.py:127
  140.9 6.5 %collective-permute-start.28 = (bf16[16,1536]{1,0:T(8,128)(2,1)S(1)}, bf16[16,1536]{1,0:T(8,128)(2,1)S(1)}, u32[]{:S(2)}, u32[]{:S(2)}) collective-permute-start(bf16[16,1536]{1,0:T(8,128)(2,1)S(1)} %fusion.3), channel_id=1, source_target_pairs={{0,225},{1,224},{2,227},{3,226},{4,229},{5,228},{6,231},{7,230},{8... | collective-permute-start | bytes 147464 | tf_op jit(solution)/shard_map/stage3/ppermute | solution.py:127
  141.6 5.9 %collective-permute-start.29 = (bf16[16,1536]{1,0:T(8,128)(2,1)S(1)}, bf16[16,1536]{1,0:T(8,128)(2,1)S(1)}, u32[]{:S(2)}, u32[]{:S(2)}) collective-permute-start(bf16[16,1536]{1,0:T(8,128)(2,1)S(1)} %fusion.3), channel_id=1, source_target_pairs={{0,226},{1,227},{2,224},{3,225},{4,230},{5,231},{6,228},{7,229},{8... | collective-permute-start | bytes 147464 | tf_op jit(solution)/shard_map/stage3/ppermute | solution.py:127
  144.4 6.1 %collective-permute-start.30 = (bf16[16,1536]{1,0:T(8,128)(2,1)S(1)}, bf16[16,1536]{1,0:T(8,128)(2,1)S(1)}, u32[]{:S(2)}, u32[]{:S(2)}) collective-permute-start(bf16[16,1536]{1,0:T(8,128)(2,1)S(1)} %fusion.3), channel_id=1, source_target_pairs={{0,227},{1,226},{2,225},{3,224},{4,231},{5,230},{6,229},{7,228},{8... | collective-permute-start | bytes 147464 | tf_op jit(solution)/shard_map/stage3/ppermute | solution.py:127
  150.7 6.0 %collective-permute-start.31 = (bf16[16,384]{1,0:T(8,128)(2,1)S(1)}, bf16[16,384]{1,0:T(8,128)(2,1)S(1)}, u32[]{:S(2)}, u32[]{:S(2)}) collective-permute-start(bf16[16,384]{1,0:T(8,128)(2,1)S(1)} %fusion.8), channel_id=1, source_target_pairs={{0,32},{1,33},{2,34},{3,35},{4,36},{5,37},{6,38},{7,39},{8,40},{9,... | collective-permute-start | bytes 36872 | tf_op jit(solution)/shard_map/stage4/ppermute | solution.py:127
  157.0 6.6 %collective-permute-start.32 = (bf16[16,1536]{1,0:T(8,128)(2,1)S(1)}, bf16[16,1536]{1,0:T(8,128)(2,1)S(1)}, u32[]{:S(2)}, u32[]{:S(2)}) collective-permute-start(bf16[16,1536]{1,0:T(8,128)(2,1)S(1)} %fusion.4), channel_id=1, source_target_pairs={{0,224},{1,225},{2,226},{3,227},{4,228},{5,229},{6,230},{7,231},{8... | collective-permute-start | bytes 147464 | tf_op jit(solution)/shard_map/stage5/ppermute | solution.py:127
  157.0 6.5 %collective-permute-start.33 = (bf16[16,1536]{1,0:T(8,128)(2,1)S(1)}, bf16[16,1536]{1,0:T(8,128)(2,1)S(1)}, u32[]{:S(2)}, u32[]{:S(2)}) collective-permute-start(bf16[16,1536]{1,0:T(8,128)(2,1)S(1)} %fusion.4), channel_id=1, source_target_pairs={{0,225},{1,224},{2,227},{3,226},{4,229},{5,228},{6,231},{7,230},{8... | collective-permute-start | bytes 147464 | tf_op jit(solution)/shard_map/stage5/ppermute | solution.py:127
  157.1 6.4 %collective-permute-start.34 = (bf16[16,1536]{1,0:T(8,128)(2,1)S(1)}, bf16[16,1536]{1,0:T(8,128)(2,1)S(1)}, u32[]{:S(2)}, u32[]{:S(2)}) collective-permute-start(bf16[16,1536]{1,0:T(8,128)(2,1)S(1)} %fusion.4), channel_id=1, source_target_pairs={{0,226},{1,227},{2,224},{3,225},{4,230},{5,231},{6,228},{7,229},{8... | collective-permute-start | bytes 147464 | tf_op jit(solution)/shard_map/stage5/ppermute | solution.py:127
  160.3 5.6 %collective-permute-start.35 = (bf16[16,1536]{1,0:T(8,128)(2,1)S(1)}, bf16[16,1536]{1,0:T(8,128)(2,1)S(1)}, u32[]{:S(2)}, u32[]{:S(2)}) collective-permute-start(bf16[16,1536]{1,0:T(8,128)(2,1)S(1)} %fusion.4), channel_id=1, source_target_pairs={{0,227},{1,226},{2,225},{3,224},{4,231},{5,230},{6,229},{7,228},{8... | collective-permute-start | bytes 147464 | tf_op jit(solution)/shard_map/stage5/ppermute | solution.py:127
  166.3 8.0 %collective-permute-start.36 = (bf16[16,384]{1,0:T(8,128)(2,1)S(1)}, bf16[16,384]{1,0:T(8,128)(2,1)S(1)}, u32[]{:S(2)}, u32[]{:S(2)}) collective-permute-start(bf16[16,384]{1,0:T(8,128)(2,1)S(1)} %fusion.9), channel_id=1, source_target_pairs={{0,32},{1,33},{2,34},{3,35},{4,36},{5,37},{6,38},{7,39},{8,40},{9,... | collective-permute-start | bytes 36872 | tf_op jit(solution)/shard_map/spread/ppermute | solution.py:127
  170.1 4.2 %collective-permute-start.37 = (bf16[16,384]{1,0:T(8,128)(2,1)S(1)}, bf16[16,384]{1,0:T(8,128)(2,1)S(1)}, u32[]{:S(2)}, u32[]{:S(2)}) collective-permute-start(bf16[16,384]{1,0:T(8,128)(2,1)S(1)} %fusion.9), channel_id=1, source_target_pairs={{0,33},{1,32},{2,35},{3,34},{4,37},{5,36},{6,39},{7,38},{8,41},{9,... | collective-permute-start | bytes 36872 | tf_op jit(solution)/shard_map/spread/ppermute | solution.py:127
  170.1 4.6 %collective-permute-start.38 = (bf16[16,384]{1,0:T(8,128)(2,1)S(1)}, bf16[16,384]{1,0:T(8,128)(2,1)S(1)}, u32[]{:S(2)}, u32[]{:S(2)}) collective-permute-start(bf16[16,384]{1,0:T(8,128)(2,1)S(1)} %fusion.9), channel_id=1, source_target_pairs={{0,34},{1,35},{2,32},{3,33},{4,38},{5,39},{6,36},{7,37},{8,42},{9,... | collective-permute-start | bytes 36872 | tf_op jit(solution)/shard_map/spread/ppermute | solution.py:127
  172.6 4.3 %collective-permute-start.39 = (bf16[16,384]{1,0:T(8,128)(2,1)S(1)}, bf16[16,384]{1,0:T(8,128)(2,1)S(1)}, u32[]{:S(2)}, u32[]{:S(2)}) collective-permute-start(bf16[16,384]{1,0:T(8,128)(2,1)S(1)} %fusion.9), channel_id=1, source_target_pairs={{0,35},{1,34},{2,33},{3,32},{4,39},{5,38},{6,37},{7,36},{8,43},{9,... | collective-permute-start | bytes 36872 | tf_op jit(solution)/shard_map/spread/ppermute | solution.py:127

commit v7 on v6

--- a/solution.py
+++ b/solution.py
@@ -317,7 +317,7 @@
             else:
                 part = source_once - jnp.dot(panel_slab, through, preferred_element_type=F32)
                 part = part.astype(BF)
-                part = total([exchange(part, m, 0, after_odd) for m in range(x_count)])
+                part = total([exchange(part, m, 0, after_odd) for m in reversed(range(x_count))])
                 panel = jnp.where(own_layer == 0, 0.0, part).astype(BF)
     with jax.named_scope("spread"):
         spread = jnp.zeros((rhs_count, panel_size), BF)

time: 182 us -> 177 us (0.973)
  starting transfers between devices: 90.8 us -> 86.4 us
    ppermute x40, starting transfers between devices: 78.8 us -> 74.4 us  [exchange(): return lax.ppermute(value, ('sweep', 'z', 'x'), pairs)]
  transfers between devices with their start and end apart: 41 -> 41, of which waited for: 21 -> 25; matrix products, arithmetic and copies ran while one was open for 3% -> 3% of each run, Pallas kernels for 14% -> 14%
where the time goes in v7:
time: 177 us
  starting transfers between devices  86.4 us (49%)
  waiting for transfers between devices  45.1 us (25%)
  Pallas kernels  32.3 us (18%)
  other arithmetic  6.01 us (3%)
  local copies, waits for them, and re-layouts  5.16 us (3%)
    ppermute x40, starting transfers between devices, exchange(): return lax.ppermute(value, ('sweep', 'z', 'x'), pairs)  74.4 us
    ppermute x40, waiting for transfers between devices, exchange(): return lax.ppermute(value, ('sweep', 'z', 'x'), pairs)  45.1 us
    all_to_all x1, starting transfers between devices, on_device(): lax.all_to_all(packed.reshape(group_size, capacity, width + LANES), ('z',...  12 us
    pallas_call x1, Pallas kernels, on_device(): pl.pallas_call(fold_kernel, grid_spec=pltpu.PrefetchScalarGridSpec(num_sc...  11.9 us
    pallas_call x1, Pallas kernels, on_device(): pl.pallas_call(lambda *refs: outward_kernel(face_dev, *refs), grid_spec=p...  8.46 us
    unnamed x14, local copies, waits for them, and re-layouts  4.69 us
    pallas_call x1, Pallas kernels, on_device(): pl.pallas_call(lambda *refs: source_kernel(face_dev, *refs), in_specs=[vm...  4.51 us
    pallas_call x1, Pallas kernels, on_device(): pl.pallas_call(solve_kernel, in_specs=[vmem] * 4, out_specs=vmem, out_sha...  4.28 us
  transfers between devices with their start and end apart: 41, of which 25 were waited for; matrix products, arithmetic and copies ran while one was open for 3% of the time, Pallas kernels for 14%

profile of v7, /device:TPU:1, one launch (start us, length us, event | category | flops | bytes accessed | tf_op | source)
XLA Modules:
  0.0 176.8 jit_solution(7483173425486097104)
XLA Ops:
  0.0 3.1 %pack.1 = bf16[1024,512]{1,0:T(8,128)(2,1)} custom-call(s32[1,512]{1,0:T(1,128)} %bitcast.45, s32[1,512]{1,0:T(1,128)} %bitcast.46, f32[512,384]{1,0:T(8,128)} %refs_2_.1), custom_call_target="tpu_custom_call" | custom-call | tf_op jit(solution)/shard_map/pack/pack/pallas_call | solution.py:149
  3.1 12.0 %all-to-all-start = ((bf16[32,32,512]{2,1,0:T(8,128)(2,1)}), bf16[32,32,512]{2,1,0:T(8,128)(2,1)S(1)}, u32[]{:S(2)}, u32[]{:S(2)}) async-start(bf16[32,32,512]{2,1,0:T(8,128)(2,1)} %bitcast.42), calls=%async_computation | async-start | bytes 2097152 | tf_op jit(solution)/shard_map/route/all_to_all | solution.py:156
  15.3 2.5 %copy-done.2 = bf16[1,1536,1536]{2,1,0:T(8,128)(2,1)S(1)} copy-done((bf16[1,1536,1536]{2,1,0:T(8,128)(2,1)S(1)}, bf16[1,1536,1536]{2,1,0:T(8,128)(2,1)}, u32[]{:S(2)}) %copy-start.2) | copy-done | bytes 4718616
  17.7 8.5 %outward.1 = (bf16[1536,1536]{1,0:T(8,128)(2,1)S(1)}, bf16[384,1536]{1,0:T(8,128)(2,1)S(1)}) custom-call(s32[2]{0:T(128)S(1)} %pad_add_fusion.refs_0_.side_ref, bf16[4,384,384]{2,1,0:T(8,128)(2,1)S(1)} %bitcast.41, bf16[1536,1536]{1,0:T(8,128)(2,1)S(1)} %bitcast.39, bf16[1536,1536]{1,0:T(8,128)(2,1)} %bitcast.34), custom_call_target="tpu_custom_call" | custom-call | tf_op jit(solution)/shard_map/fold/outward/pallas_call | solution.py:170
  26.3 1.3 collective-permute-start
  27.6 1.8 %collective-permute-start.1 = (bf16[192,1536]{1,0:T(8,128)(2,1)S(1)}, bf16[192,1536]{1,0:T(8,128)(2,1)S(1)}, u32[]{:S(2)}, u32[]{:S(2)}) collective-permute-start(bf16[192,1536]{1,0:T(8,128)(2,1)S(1)} %get-tuple-element.37), channel_id=1, source_target_pairs={{0,3},{1,2},{2,1},{3,0},{4,7},{5,6},{6,5},{7,4},{8,11},{9,10},{10,... | collective-permute-start | bytes 1769480 | tf_op jit(solution)/shard_map/sum_x/ppermute | solution.py:127
  29.4 11.9 %fold.1 = bf16[3,384,1536]{2,1,0:T(8,128)(2,1)S(1)} custom-call(s32[2]{0:T(128)S(1)} %pad_add_fusion.refs_0_.side_ref, bf16[1536,1536]{1,0:T(8,128)(2,1)S(1)} %bitcast.38, bf16[1536,1536]{1,0:T(8,128)(2,1)S(1)} %get-tuple-element.18.outward_ref.refs_2_), custom_call_target="tpu_custom_call" | custom-call | tf_op jit(solution)/shard_map/fold/fold/pallas_call | solution.py:209
  41.3 2.2 %copy-done = bf16[1536,1536]{1,0:T(8,128)(2,1)} copy-done((bf16[1536,1536]{1,0:T(8,128)(2,1)}, bf16[1536,1536]{1,0:T(8,128)(2,1)S(1)}, u32[]{:S(2)}) %copy-start) | copy-done | bytes 4718616
  43.6 2.2 %collective-permute-done = bf16[192,1536]{1,0:T(8,128)(2,1)S(1)} collective-permute-done((bf16[192,1536]{1,0:T(8,128)(2,1)S(1)}, bf16[192,1536]{1,0:T(8,128)(2,1)S(1)}, u32[]{:S(2)}, u32[]{:S(2)}) %collective-permute-start) | collective-permute-done | bytes 589856 | tf_op jit(solution)/shard_map/sum_x/ppermute | solution.py:127
  45.8 1.5 collective-permute-done.1
  48.2 1.0 collective-permute-start.9
  49.1 4.5 %source.1 = (f32[16,1536]{1,0:T(8,128)}, f32[16,1536]{1,0:T(8,128)}) custom-call(bf16[1024,512]{1,0:T(8,128)(2,1)} %bitcast.43, f32[16,4,384]{2,1,0:T(4,128)} %bitcast.44, bf16[1536,1536]{1,0:T(8,128)(2,1)} %copy-done), custom_call_target="tpu_custom_call" | custom-call | tf_op jit(solution)/shard_map/source/source/pallas_call | solution.py:249
  53.7 0.9 convert_element_type.207
  54.6 0.5 collective-permute-start.2
  55.1 3.3 %collective-permute-start.3 = (bf16[16,1536]{1,0:T(8,128)(2,1)S(1)}, bf16[16,1536]{1,0:T(8,128)(2,1)S(1)}, u32[]{:S(2)}, u32[]{:S(2)}) collective-permute-start(bf16[16,1536]{1,0:T(8,128)(2,1)S(1)} %convert_element_type.207), channel_id=1, source_target_pairs={{0,8},{1,9},{2,10},{3,11},{4,12},{5,13},{6,14},{7,15},{8,0},{9,1},... | collective-permute-start | bytes 147464 | tf_op jit(solution)/shard_map/sum_source/ppermute | solution.py:127
  58.6 1.6 collective-permute-done.3
  60.3 3.3 %collective-permute-done.4 = bf16[16,1536]{1,0:T(8,128)(2,1)S(1)} collective-permute-done((bf16[16,1536]{1,0:T(8,128)(2,1)S(1)}, bf16[16,1536]{1,0:T(8,128)(2,1)S(1)}, u32[]{:S(2)}, u32[]{:S(2)}) %collective-permute-start.4) | collective-permute-done | bytes 49184 | tf_op jit(solution)/shard_map/sum_source/ppermute | solution.py:127
  63.6 0.9 add_convert_fusion.7
  64.5 1.7 collective-permute-start.5
  66.2 2.9 %collective-permute-done.5 = bf16[16,1536]{1,0:T(8,128)(2,1)S(1)} collective-permute-done((bf16[16,1536]{1,0:T(8,128)(2,1)S(1)}, bf16[16,1536]{1,0:T(8,128)(2,1)S(1)}, u32[]{:S(2)}, u32[]{:S(2)}) %collective-permute-start.5) | collective-permute-done | bytes 49184 | tf_op jit(solution)/shard_map/sum_source/ppermute | solution.py:127
  69.4 2.2 %collective-permute-start.7 = (bf16[16,1536]{1,0:T(8,128)(2,1)S(1)}, bf16[16,1536]{1,0:T(8,128)(2,1)S(1)}, u32[]{:S(2)}, u32[]{:S(2)}) collective-permute-start(bf16[16,1536]{1,0:T(8,128)(2,1)S(1)} %add_convert_fusion.6), channel_id=1, source_target_pairs={{0,2},{1,3},{2,0},{3,1},{4,6},{5,7},{6,4},{7,5},{8,10},{9,11},{10,... | collective-permute-start | bytes 147464 | tf_op jit(solution)/shard_map/sum_source/ppermute | solution.py:127
  71.6 1.5 collective-permute-start.8
  73.1 1.6 collective-permute-done.9
  74.7 2.4 %fusion.1 = bf16[384,1536]{1,0:T(8,128)(2,1)S(1)} fusion(bf16[384,1536]{1,0:T(8,128)(2,1)} %collective-permute-done.10, bf16[384,1536]{1,0:T(8,128)(2,1)} %collective-permute-done.9, bf16[3,384,1536]{2,1,0:T(8,128)(2,1)} %copy-done.1), kind=kLoop, calls=%fused_computation.2 | loop fusion | flops 3538944 | bytes 4718592 | tf_op jit(solution)/shard_map/sum_x/convert_element_type | solution.py:246
  77.8 2.2 %collective-permute-start.17 = (bf16[96,1536]{1,0:T(8,128)(2,1)S(1)}, bf16[96,1536]{1,0:T(8,128)(2,1)S(1)}, u32[]{:S(2)}, u32[]{:S(2)}) collective-permute-start(bf16[96,1536]{1,0:T(8,128)(2,1)S(1)} %constant_dynamic-slice_fusion.1), channel_id=1, source_target_pairs={{0,28},{1,29},{2,30},{3,31},{4,8},{5,9},{6,10},{7,11},{8,4},{9,5},... | collective-permute-start | bytes 884744 | tf_op jit(solution)/shard_map/sum_z/ppermute | solution.py:127
  80.0 2.9 %collective-permute-done.11 = bf16[96,1536]{1,0:T(8,128)(2,1)S(1)} collective-permute-done((bf16[96,1536]{1,0:T(8,128)(2,1)S(1)}, bf16[96,1536]{1,0:T(8,128)(2,1)S(1)}, u32[]{:S(2)}, u32[]{:S(2)}) %collective-permute-start.11) | collective-permute-done | bytes 294944 | tf_op jit(solution)/shard_map/sum_z/ppermute | solution.py:127
  83.0 2.4 %collective-permute-start.13 = (bf16[48,1536]{1,0:T(8,128)(2,1)S(1)}, bf16[48,1536]{1,0:T(8,128)(2,1)S(1)}, u32[]{:S(2)}, u32[]{:S(2)}) collective-permute-start(bf16[48,1536]{1,0:T(8,128)(2,1)S(1)} %constant_dynamic-slice_fusion.2), channel_id=1, source_target_pairs={{0,28},{1,29},{2,30},{3,31},{4,8},{5,9},{6,10},{7,11},{8,4},{9,5},... | collective-permute-start | bytes 442376 | tf_op jit(solution)/shard_map/sum_z/ppermute | solution.py:127
  85.5 1.1 collective-permute-start.18
  86.6 5.9 %collective-permute-start.12 = (bf16[16,384]{1,0:T(8,128)(2,1)S(1)}, bf16[16,384]{1,0:T(8,128)(2,1)S(1)}, u32[]{:S(2)}, u32[]{:S(2)}) collective-permute-start(bf16[16,384]{1,0:T(8,128)(2,1)S(1)} %dynamic-slice_convert_fusion), channel_id=1, source_target_pairs={{0,32},{1,33},{2,34},{3,35},{4,36},{5,37},{6,38},{7,39},{8,40},{9,... | collective-permute-start | bytes 36872 | tf_op jit(solution)/shard_map/stage0/ppermute | solution.py:127
  92.5 2.8 %collective-permute-start.14 = (bf16[48,1536]{1,0:T(8,128)(2,1)S(1)}, bf16[48,1536]{1,0:T(8,128)(2,1)S(1)}, u32[]{:S(2)}, u32[]{:S(2)}) collective-permute-start(bf16[48,1536]{1,0:T(8,128)(2,1)S(1)} %add_convert_fusion.5), channel_id=1, source_target_pairs={{0,12},{1,13},{2,14},{3,15},{4,24},{5,25},{6,26},{7,27},{8,20},{9,... | collective-permute-start | bytes 442376 | tf_op jit(solution)/shard_map/sum_z/ppermute | solution.py:127
  95.4 3.8 %collective-permute-start.19 = (bf16[48,1536]{1,0:T(8,128)(2,1)S(1)}, bf16[48,1536]{1,0:T(8,128)(2,1)S(1)}, u32[]{:S(2)}, u32[]{:S(2)}) collective-permute-start(bf16[48,1536]{1,0:T(8,128)(2,1)S(1)} %add_convert_fusion.3), channel_id=1, source_target_pairs={{0,20},{1,21},{2,22},{3,23},{4,16},{5,17},{6,18},{7,19},{8,28},{9,... | collective-permute-start | bytes 442376 | tf_op jit(solution)/shard_map/sum_z/ppermute | solution.py:127
  99.6 1.6 collective-permute-start.15
  101.2 6.4 %collective-permute-done.19 = bf16[48,1536]{1,0:T(8,128)(2,1)S(1)} collective-permute-done((bf16[48,1536]{1,0:T(8,128)(2,1)S(1)}, bf16[48,1536]{1,0:T(8,128)(2,1)S(1)}, u32[]{:S(2)}, u32[]{:S(2)}) %collective-permute-start.19) | collective-permute-done | bytes 147488 | tf_op jit(solution)/shard_map/sum_z/ppermute | solution.py:127
  107.6 4.6 %collective-permute-start.20 = (bf16[48,1536]{1,0:T(8,128)(2,1)S(1)}, bf16[48,1536]{1,0:T(8,128)(2,1)S(1)}, u32[]{:S(2)}, u32[]{:S(2)}) collective-permute-start(bf16[48,1536]{1,0:T(8,128)(2,1)S(1)} %add_convert_fusion.2), channel_id=1, source_target_pairs={{0,4},{1,5},{2,6},{3,7},{4,0},{5,1},{6,2},{7,3},{8,12},{9,13},{10,... | collective-permute-start | bytes 442376 | tf_op jit(solution)/shard_map/sum_z/ppermute | solution.py:127
  112.3 2.1 %collective-permute-start.16 = (bf16[96,1536]{1,0:T(8,128)(2,1)S(1)}, bf16[96,1536]{1,0:T(8,128)(2,1)S(1)}, u32[]{:S(2)}, u32[]{:S(2)}) collective-permute-start(bf16[96,1536]{1,0:T(8,128)(2,1)S(1)} %constant_dynamic-update-slice_fusion.7), channel_id=1, source_target_pairs={{0,4},{1,5},{2,6},{3,7},{4,0},{5,1},{6,2},{7,3},{8,12},{9,13},{10,... | collective-permute-start | bytes 884744 | tf_op jit(solution)/shard_map/sum_z/ppermute | solution.py:127
  114.4 1.5 collective-permute-done.20
  116.2 6.1 %collective-permute-done.16 = bf16[96,1536]{1,0:T(8,128)(2,1)S(1)} collective-permute-done((bf16[96,1536]{1,0:T(8,128)(2,1)S(1)}, bf16[96,1536]{1,0:T(8,128)(2,1)S(1)}, u32[]{:S(2)}, u32[]{:S(2)}) %collective-permute-start.16) | collective-permute-done | bytes 294944 | tf_op jit(solution)/shard_map/sum_z/ppermute | solution.py:127
  122.3 1.7 collective-permute-done.21
  124.2 4.6 %collective-permute-start.22 = (bf16[16,1536]{1,0:T(8,128)(2,1)S(1)}, bf16[16,1536]{1,0:T(8,128)(2,1)S(1)}, u32[]{:S(2)}, u32[]{:S(2)}) collective-permute-start(bf16[16,1536]{1,0:T(8,128)(2,1)S(1)} %fusion.2), channel_id=1, source_target_pairs={{0,227},{1,226},{2,225},{3,224},{4,231},{5,230},{6,229},{7,228},{8... | collective-permute-start | bytes 147464 | tf_op jit(solution)/shard_map/stage1/ppermute | solution.py:127
  128.8 3.5 %collective-permute-start.24 = (bf16[16,1536]{1,0:T(8,128)(2,1)S(1)}, bf16[16,1536]{1,0:T(8,128)(2,1)S(1)}, u32[]{:S(2)}, u32[]{:S(2)}) collective-permute-start(bf16[16,1536]{1,0:T(8,128)(2,1)S(1)} %fusion.2), channel_id=1, source_target_pairs={{0,225},{1,224},{2,227},{3,226},{4,229},{5,228},{6,231},{7,230},{8... | collective-permute-start | bytes 147464 | tf_op jit(solution)/shard_map/stage1/ppermute | solution.py:127
  132.5 2.6 %collective-permute-done.23 = bf16[16,1536]{1,0:T(8,128)(2,1)S(1)} collective-permute-done((bf16[16,1536]{1,0:T(8,128)(2,1)S(1)}, bf16[16,1536]{1,0:T(8,128)(2,1)S(1)}, u32[]{:S(2)}, u32[]{:S(2)}) %collective-permute-start.23) | collective-permute-done | bytes 49184 | tf_op jit(solution)/shard_map/stage1/ppermute | solution.py:127
  135.5 0.7 collective-permute-done.25
  136.4 1.3 collective-permute-start.26
  137.7 0.8 collective-permute-done.26
  138.8 1.2 collective-permute-start.27
  140.0 2.7 %collective-permute-start.28 = (bf16[16,1536]{1,0:T(8,128)(2,1)S(1)}, bf16[16,1536]{1,0:T(8,128)(2,1)S(1)}, u32[]{:S(2)}, u32[]{:S(2)}) collective-permute-start(bf16[16,1536]{1,0:T(8,128)(2,1)S(1)} %fusion.3), channel_id=1, source_target_pairs={{0,226},{1,227},{2,224},{3,225},{4,230},{5,231},{6,228},{7,229},{8... | collective-permute-start | bytes 147464 | tf_op jit(solution)/shard_map/stage3/ppermute | solution.py:127
  143.2 1.6 collective-permute-start.30
  144.8 1.7 collective-permute-done.28
  146.5 0.8 collective-permute-done.29
  147.9 4.6 %collective-permute-start.31 = (bf16[16,384]{1,0:T(8,128)(2,1)S(1)}, bf16[16,384]{1,0:T(8,128)(2,1)S(1)}, u32[]{:S(2)}, u32[]{:S(2)}) collective-permute-start(bf16[16,384]{1,0:T(8,128)(2,1)S(1)} %fusion.8), channel_id=1, source_target_pairs={{0,32},{1,33},{2,34},{3,35},{4,36},{5,37},{6,38},{7,39},{8,40},{9,... | collective-permute-start | bytes 36872 | tf_op jit(solution)/shard_map/stage4/ppermute | solution.py:127
  152.5 0.8 collective-permute-done.31
  153.7 2.5 %collective-permute-start.33 = (bf16[16,1536]{1,0:T(8,128)(2,1)S(1)}, bf16[16,1536]{1,0:T(8,128)(2,1)S(1)}, u32[]{:S(2)}, u32[]{:S(2)}) collective-permute-start(bf16[16,1536]{1,0:T(8,128)(2,1)S(1)} %fusion.4), channel_id=1, source_target_pairs={{0,226},{1,227},{2,224},{3,225},{4,230},{5,231},{6,228},{7,229},{8... | collective-permute-start | bytes 147464 | tf_op jit(solution)/shard_map/stage5/ppermute | solution.py:127
  156.4 3.2 %collective-permute-start.35 = (bf16[16,1536]{1,0:T(8,128)(2,1)S(1)}, bf16[16,1536]{1,0:T(8,128)(2,1)S(1)}, u32[]{:S(2)}, u32[]{:S(2)}) collective-permute-start(bf16[16,1536]{1,0:T(8,128)(2,1)S(1)} %fusion.4), channel_id=1, source_target_pairs={{0,224},{1,225},{2,226},{3,227},{4,228},{5,229},{6,230},{7,231},{8... | collective-permute-start | bytes 147464 | tf_op jit(solution)/shard_map/stage5/ppermute | solution.py:127
  159.6 0.5 collective-permute-done.32
  160.1 0.4 collective-permute-done.34
  160.6 1.1 collective-permute-done.35
  162.0 2.9 %collective-permute-start.36 = (bf16[16,384]{1,0:T(8,128)(2,1)S(1)}, bf16[16,384]{1,0:T(8,128)(2,1)S(1)}, u32[]{:S(2)}, u32[]{:S(2)}) collective-permute-start(bf16[16,384]{1,0:T(8,128)(2,1)S(1)} %fusion.9), channel_id=1, source_target_pairs={{0,32},{1,33},{2,34},{3,35},{4,36},{5,37},{6,38},{7,39},{8,40},{9,... | collective-permute-start | bytes 36872 | tf_op jit(solution)/shard_map/spread/ppermute | solution.py:127
  164.8 1.4 collective-permute-start.37
  166.2 1.3 collective-permute-start.38
  167.6 1.4 collective-permute-start.39
  169.1 1.8 %collective-permute-done.38 = bf16[16,384]{1,0:T(8,128)(2,1)S(1)} collective-permute-done((bf16[16,384]{1,0:T(8,128)(2,1)S(1)}, bf16[16,384]{1,0:T(8,128)(2,1)S(1)}, u32[]{:S(2)}, u32[]{:S(2)}) %collective-permute-start.38) | collective-permute-done | bytes 12320 | tf_op jit(solution)/shard_map/spread/ppermute | solution.py:127
  170.9 1.0 collective-permute-done.39
  171.9 0.6 broadcast_select_fusion.panel_ref
  172.6 4.3 %solve.1 = f32[16,4,384]{2,1,0:T(4,128)} custom-call(bf16[16,1536]{1,0:T(8,128)(2,1)} %broadcast_select_fusion.panel_ref, bf16[1536,1536]{1,0:T(8,128)(2,1)} %bitcast.35, f32[16,1536]{1,0:T(8,128)} %get-tuple-element.26.assembled_ref, bf16[4,384,384]{2,1,0:T(8,128)(2,1)} %bitcast.40), custom_call_target="tpu_custom_call" | custom-call | tf_op jit(solution)/shard_map/solve/solve/pallas_call | solution.py:329
  (82 shorter events, 6.6 us)
Async XLA Ops:
  3.1 12.1 %copy-start.3 = (bf16[1,4,384,384]{3,2,1,0:T(8,128)(2,1)S(1)}, bf16[1,4,384,384]{3,2,1,0:T(8,128)(2,1)}, u32[]{:S(2)}) copy-start(bf16[1,4,384,384]{3,2,1,0:T(8,128)(2,1)} %param.11) | copy-start | bytes 3538948
  3.1 44.6 %all-to-all-start = ((bf16[32,32,512]{2,1,0:T(8,128)(2,1)}), bf16[32,32,512]{2,1,0:T(8,128)(2,1)S(1)}, u32[]{:S(2)}, u32[]{:S(2)}) async-start(bf16[32,32,512]{2,1,0:T(8,128)(2,1)} %bitcast.42), calls=%async_computation | async-start | bytes 2097152 | tf_op jit(solution)/shard_map/route/all_to_all | solution.py:156
  15.2 14.2 %slice-start = ((s8[4718592]{0:T(1024)(128)(4,1)}), s8[4194304]{0:T(1024)(128)(4,1)S(1)}, s32[]{:S(2)}) async-start(s8[4718592]{0:T(1024)(128)(4,1)} %bitcast.36), calls=%async_computation.1 | async-start | bytes 8388608
  15.2 2.5 %copy-start.2 = (bf16[1,1536,1536]{2,1,0:T(8,128)(2,1)S(1)}, bf16[1,1536,1536]{2,1,0:T(8,128)(2,1)}, u32[]{:S(2)}) copy-start(bf16[1,1536,1536]{2,1,0:T(8,128)(2,1)} %param.13) | copy-start | bytes 14155780
  17.7 11.7 %slice-start.1 = ((s8[4718592]{0:T(1024)(128)(4,1)}), s8[524288]{0:T(1024)(128)(4,1)S(1)}, s32[]{:S(2)}) async-start(s8[4718592]{0:T(1024)(128)(4,1)} %bitcast.36), calls=%async_computation.2 | async-start | bytes 1048576
  26.3 19.5 %collective-permute-start = (bf16[192,1536]{1,0:T(8,128)(2,1)S(1)}, bf16[192,1536]{1,0:T(8,128)(2,1)S(1)}, u32[]{:S(2)}, u32[]{:S(2)}) collective-permute-start(bf16[192,1536]{1,0:T(8,128)(2,1)S(1)} %get-tuple-element.38), channel_id=1, source_target_pairs={{0,1},{1,0},{2,3},{3,2},{4,5},{5,4},{6,7},{7,6},{8,9},{9,8},{10,11... | collective-permute-start | bytes 1769480 | tf_op jit(solution)/shard_map/sum_x/ppermute | solution.py:127
  27.6 19.6 %collective-permute-start.1 = (bf16[192,1536]{1,0:T(8,128)(2,1)S(1)}, bf16[192,1536]{1,0:T(8,128)(2,1)S(1)}, u32[]{:S(2)}, u32[]{:S(2)}) collective-permute-start(bf16[192,1536]{1,0:T(8,128)(2,1)S(1)} %get-tuple-element.37), channel_id=1, source_target_pairs={{0,3},{1,2},{2,1},{3,0},{4,7},{5,6},{6,5},{7,4},{8,11},{9,10},{10,... | collective-permute-start | bytes 1769480 | tf_op jit(solution)/shard_map/sum_x/ppermute | solution.py:127
  41.3 2.2 %copy-start = (bf16[1536,1536]{1,0:T(8,128)(2,1)}, bf16[1536,1536]{1,0:T(8,128)(2,1)S(1)}, u32[]{:S(2)}) copy-start(bf16[1536,1536]{1,0:T(8,128)(2,1)S(1)} %get-tuple-element.18.outward_ref.refs_2_) | copy-start | bytes 14155780
  43.5 3.8 %copy-start.1 = (bf16[3,384,1536]{2,1,0:T(8,128)(2,1)}, bf16[3,384,1536]{2,1,0:T(8,128)(2,1)S(1)}, u32[]{:S(2)}) copy-start(bf16[3,384,1536]{2,1,0:T(8,128)(2,1)S(1)} %fold.1) | copy-start | bytes 10616836
  47.7 1.4 copy-start.4
  47.7 25.4 %collective-permute-start.10 = (bf16[384,1536]{1,0:T(8,128)(2,1)S(1)}, bf16[384,1536]{1,0:T(8,128)(2,1)}, u32[]{:S(2)}, u32[]{:S(2)}) collective-permute-start(bf16[384,1536]{1,0:T(8,128)(2,1)S(1)} %get-tuple-element.23), channel_id=1, source_target_pairs={{0,1},{1,0},{2,3},{3,2},{4,5},{5,4},{6,7},{7,6},{8,9},{9,8},{10,11... | collective-permute-start | bytes 3538952 | tf_op jit(solution)/shard_map/sum_x/ppermute | solution.py:127
  48.2 26.6 %collective-permute-start.9 = (bf16[384,1536]{1,0:T(8,128)(2,1)S(1)}, bf16[384,1536]{1,0:T(8,128)(2,1)}, u32[]{:S(2)}, u32[]{:S(2)}) collective-permute-start(bf16[384,1536]{1,0:T(8,128)(2,1)S(1)} %get-tuple-element.22), channel_id=1, source_target_pairs={{0,3},{1,2},{2,1},{3,0},{4,7},{5,6},{6,5},{7,4},{8,11},{9,10},{10,... | collective-permute-start | bytes 3538952 | tf_op jit(solution)/shard_map/sum_x/ppermute | solution.py:127
  54.6 4.1 %collective-permute-start.2 = (bf16[16,1536]{1,0:T(8,128)(2,1)S(1)}, bf16[16,1536]{1,0:T(8,128)(2,1)S(1)}, u32[]{:S(2)}, u32[]{:S(2)}) collective-permute-start(bf16[16,1536]{1,0:T(8,128)(2,1)S(1)} %convert_element_type.207), channel_id=1, source_target_pairs={{0,4},{1,5},{2,6},{3,7},{4,0},{5,1},{6,2},{7,3},{8,12},{9,13},{10,... | collective-permute-start | bytes 147464 | tf_op jit(solution)/shard_map/sum_source/ppermute | solution.py:127
  55.1 5.2 %collective-permute-start.3 = (bf16[16,1536]{1,0:T(8,128)(2,1)S(1)}, bf16[16,1536]{1,0:T(8,128)(2,1)S(1)}, u32[]{:S(2)}, u32[]{:S(2)}) collective-permute-start(bf16[16,1536]{1,0:T(8,128)(2,1)S(1)} %convert_element_type.207), channel_id=1, source_target_pairs={{0,8},{1,9},{2,10},{3,11},{4,12},{5,13},{6,14},{7,15},{8,0},{9,1},... | collective-permute-start | bytes 147464 | tf_op jit(solution)/shard_map/sum_source/ppermute | solution.py:127
  58.4 5.2 %collective-permute-start.4 = (bf16[16,1536]{1,0:T(8,128)(2,1)S(1)}, bf16[16,1536]{1,0:T(8,128)(2,1)S(1)}, u32[]{:S(2)}, u32[]{:S(2)}) collective-permute-start(bf16[16,1536]{1,0:T(8,128)(2,1)S(1)} %convert_element_type.207), channel_id=1, source_target_pairs={{0,12},{1,13},{2,14},{3,15},{4,8},{5,9},{6,10},{7,11},{8,4},{9,5},... | collective-permute-start | bytes 147464 | tf_op jit(solution)/shard_map/sum_source/ppermute | solution.py:127
  64.5 4.6 %collective-permute-start.5 = (bf16[16,1536]{1,0:T(8,128)(2,1)S(1)}, bf16[16,1536]{1,0:T(8,128)(2,1)S(1)}, u32[]{:S(2)}, u32[]{:S(2)}) collective-permute-start(bf16[16,1536]{1,0:T(8,128)(2,1)S(1)} %add_convert_fusion.7), channel_id=1, source_target_pairs={{0,28},{1,29},{2,30},{3,31},{4,24},{5,25},{6,26},{7,27},{8,20},{9,... | collective-permute-start | bytes 147464 | tf_op jit(solution)/shard_map/sum_source/ppermute | solution.py:127
  69.2 8.5 %collective-permute-start.6 = (bf16[16,1536]{1,0:T(8,128)(2,1)S(1)}, bf16[16,1536]{1,0:T(8,128)(2,1)S(1)}, u32[]{:S(2)}, u32[]{:S(2)}) collective-permute-start(bf16[16,1536]{1,0:T(8,128)(2,1)S(1)} %add_convert_fusion.6), channel_id=1, source_target_pairs={{0,1},{1,0},{2,3},{3,2},{4,5},{5,4},{6,7},{7,6},{8,9},{9,8},{10,11... | collective-permute-start | bytes 147464 | tf_op jit(solution)/shard_map/sum_source/ppermute | solution.py:127
  69.4 8.2 %collective-permute-start.7 = (bf16[16,1536]{1,0:T(8,128)(2,1)S(1)}, bf16[16,1536]{1,0:T(8,128)(2,1)S(1)}, u32[]{:S(2)}, u32[]{:S(2)}) collective-permute-start(bf16[16,1536]{1,0:T(8,128)(2,1)S(1)} %add_convert_fusion.6), channel_id=1, source_target_pairs={{0,2},{1,3},{2,0},{3,1},{4,6},{5,7},{6,4},{7,5},{8,10},{9,11},{10,... | collective-permute-start | bytes 147464 | tf_op jit(solution)/shard_map/sum_source/ppermute | solution.py:127
  71.6 6.1 %collective-permute-start.8 = (bf16[16,1536]{1,0:T(8,128)(2,1)S(1)}, bf16[16,1536]{1,0:T(8,128)(2,1)S(1)}, u32[]{:S(2)}, u32[]{:S(2)}) collective-permute-start(bf16[16,1536]{1,0:T(8,128)(2,1)S(1)} %add_convert_fusion.6), channel_id=1, source_target_pairs={{0,3},{1,2},{2,1},{3,0},{4,7},{5,6},{6,5},{7,4},{8,11},{9,10},{10,... | collective-permute-start | bytes 147464 | tf_op jit(solution)/shard_map/sum_source/ppermute | solution.py:127
  77.3 5.7 %collective-permute-start.11 = (bf16[96,1536]{1,0:T(8,128)(2,1)S(1)}, bf16[96,1536]{1,0:T(8,128)(2,1)S(1)}, u32[]{:S(2)}, u32[]{:S(2)}) collective-permute-start(bf16[96,1536]{1,0:T(8,128)(2,1)S(1)} %constant_dynamic-slice_fusion.3), channel_id=1, source_target_pairs={{0,4},{1,5},{2,6},{3,7},{4,0},{5,1},{6,2},{7,3},{8,12},{9,13},{10,... | collective-permute-start | bytes 884744 | tf_op jit(solution)/shard_map/sum_z/ppermute | solution.py:127
  77.8 7.6 %collective-permute-start.17 = (bf16[96,1536]{1,0:T(8,128)(2,1)S(1)}, bf16[96,1536]{1,0:T(8,128)(2,1)S(1)}, u32[]{:S(2)}, u32[]{:S(2)}) collective-permute-start(bf16[96,1536]{1,0:T(8,128)(2,1)S(1)} %constant_dynamic-slice_fusion.1), channel_id=1, source_target_pairs={{0,28},{1,29},{2,30},{3,31},{4,8},{5,9},{6,10},{7,11},{8,4},{9,5},... | collective-permute-start | bytes 884744 | tf_op jit(solution)/shard_map/sum_z/ppermute | solution.py:127
  83.0 9.5 %collective-permute-start.13 = (bf16[48,1536]{1,0:T(8,128)(2,1)S(1)}, bf16[48,1536]{1,0:T(8,128)(2,1)S(1)}, u32[]{:S(2)}, u32[]{:S(2)}) collective-permute-start(bf16[48,1536]{1,0:T(8,128)(2,1)S(1)} %constant_dynamic-slice_fusion.2), channel_id=1, source_target_pairs={{0,28},{1,29},{2,30},{3,31},{4,8},{5,9},{6,10},{7,11},{8,4},{9,5},... | collective-permute-start | bytes 442376 | tf_op jit(solution)/shard_map/sum_z/ppermute | solution.py:127
  85.5 9.9 %collective-permute-start.18 = (bf16[48,1536]{1,0:T(8,128)(2,1)S(1)}, bf16[48,1536]{1,0:T(8,128)(2,1)S(1)}, u32[]{:S(2)}, u32[]{:S(2)}) collective-permute-start(bf16[48,1536]{1,0:T(8,128)(2,1)S(1)} %constant_dynamic-slice_fusion), channel_id=1, source_target_pairs={{0,4},{1,5},{2,6},{3,7},{4,0},{5,1},{6,2},{7,3},{8,12},{9,13},{10,... | collective-permute-start | bytes 442376 | tf_op jit(solution)/shard_map/sum_z/ppermute | solution.py:127
  86.6 37.3 %collective-permute-start.12 = (bf16[16,384]{1,0:T(8,128)(2,1)S(1)}, bf16[16,384]{1,0:T(8,128)(2,1)S(1)}, u32[]{:S(2)}, u32[]{:S(2)}) collective-permute-start(bf16[16,384]{1,0:T(8,128)(2,1)S(1)} %dynamic-slice_convert_fusion), channel_id=1, source_target_pairs={{0,32},{1,33},{2,34},{3,35},{4,36},{5,37},{6,38},{7,39},{8,40},{9,... | collective-permute-start | bytes 36872 | tf_op jit(solution)/shard_map/stage0/ppermute | solution.py:127
  92.5 7.0 %collective-permute-start.14 = (bf16[48,1536]{1,0:T(8,128)(2,1)S(1)}, bf16[48,1536]{1,0:T(8,128)(2,1)S(1)}, u32[]{:S(2)}, u32[]{:S(2)}) collective-permute-start(bf16[48,1536]{1,0:T(8,128)(2,1)S(1)} %add_convert_fusion.5), channel_id=1, source_target_pairs={{0,12},{1,13},{2,14},{3,15},{4,24},{5,25},{6,26},{7,27},{8,20},{9,... | collective-permute-start | bytes 442376 | tf_op jit(solution)/shard_map/sum_z/ppermute | solution.py:127
  95.4 12.1 %collective-permute-start.19 = (bf16[48,1536]{1,0:T(8,128)(2,1)S(1)}, bf16[48,1536]{1,0:T(8,128)(2,1)S(1)}, u32[]{:S(2)}, u32[]{:S(2)}) collective-permute-start(bf16[48,1536]{1,0:T(8,128)(2,1)S(1)} %add_convert_fusion.3), channel_id=1, source_target_pairs={{0,20},{1,21},{2,22},{3,23},{4,16},{5,17},{6,18},{7,19},{8,28},{9,... | collective-permute-start | bytes 442376 | tf_op jit(solution)/shard_map/sum_z/ppermute | solution.py:127
  99.6 12.7 %collective-permute-start.15 = (bf16[48,1536]{1,0:T(8,128)(2,1)S(1)}, bf16[48,1536]{1,0:T(8,128)(2,1)S(1)}, u32[]{:S(2)}, u32[]{:S(2)}) collective-permute-start(bf16[48,1536]{1,0:T(8,128)(2,1)S(1)} %add_convert_fusion.4), channel_id=1, source_target_pairs={{0,28},{1,29},{2,30},{3,31},{4,8},{5,9},{6,10},{7,11},{8,4},{9,5},... | collective-permute-start | bytes 442376 | tf_op jit(solution)/shard_map/sum_z/ppermute | solution.py:127
  107.6 8.3 %collective-permute-start.20 = (bf16[48,1536]{1,0:T(8,128)(2,1)S(1)}, bf16[48,1536]{1,0:T(8,128)(2,1)S(1)}, u32[]{:S(2)}, u32[]{:S(2)}) collective-permute-start(bf16[48,1536]{1,0:T(8,128)(2,1)S(1)} %add_convert_fusion.2), channel_id=1, source_target_pairs={{0,4},{1,5},{2,6},{3,7},{4,0},{5,1},{6,2},{7,3},{8,12},{9,13},{10,... | collective-permute-start | bytes 442376 | tf_op jit(solution)/shard_map/sum_z/ppermute | solution.py:127
  112.3 10.0 %collective-permute-start.16 = (bf16[96,1536]{1,0:T(8,128)(2,1)S(1)}, bf16[96,1536]{1,0:T(8,128)(2,1)S(1)}, u32[]{:S(2)}, u32[]{:S(2)}) collective-permute-start(bf16[96,1536]{1,0:T(8,128)(2,1)S(1)} %constant_dynamic-update-slice_fusion.7), channel_id=1, source_target_pairs={{0,4},{1,5},{2,6},{3,7},{4,0},{5,1},{6,2},{7,3},{8,12},{9,13},{10,... | collective-permute-start | bytes 884744 | tf_op jit(solution)/shard_map/sum_z/ppermute | solution.py:127
  115.9 8.0 %collective-permute-start.21 = (bf16[96,1536]{1,0:T(8,128)(2,1)S(1)}, bf16[96,1536]{1,0:T(8,128)(2,1)S(1)}, u32[]{:S(2)}, u32[]{:S(2)}) collective-permute-start(bf16[96,1536]{1,0:T(8,128)(2,1)S(1)} %constant_dynamic-update-slice_fusion.5), channel_id=1, source_target_pairs={{0,28},{1,29},{2,30},{3,31},{4,8},{5,9},{6,10},{7,11},{8,4},{9,5},... | collective-permute-start | bytes 884744 | tf_op jit(solution)/shard_map/sum_z/ppermute | solution.py:127
  124.2 8.2 %collective-permute-start.22 = (bf16[16,1536]{1,0:T(8,128)(2,1)S(1)}, bf16[16,1536]{1,0:T(8,128)(2,1)S(1)}, u32[]{:S(2)}, u32[]{:S(2)}) collective-permute-start(bf16[16,1536]{1,0:T(8,128)(2,1)S(1)} %fusion.2), channel_id=1, source_target_pairs={{0,227},{1,226},{2,225},{3,224},{4,231},{5,230},{6,229},{7,228},{8... | collective-permute-start | bytes 147464 | tf_op jit(solution)/shard_map/stage1/ppermute | solution.py:127
  128.8 6.2 %collective-permute-start.23 = (bf16[16,1536]{1,0:T(8,128)(2,1)S(1)}, bf16[16,1536]{1,0:T(8,128)(2,1)S(1)}, u32[]{:S(2)}, u32[]{:S(2)}) collective-permute-start(bf16[16,1536]{1,0:T(8,128)(2,1)S(1)} %fusion.2), channel_id=1, source_target_pairs={{0,226},{1,227},{2,224},{3,225},{4,230},{5,231},{6,228},{7,229},{8... | collective-permute-start | bytes 147464 | tf_op jit(solution)/shard_map/stage1/ppermute | solution.py:127
  128.8 6.6 %collective-permute-start.24 = (bf16[16,1536]{1,0:T(8,128)(2,1)S(1)}, bf16[16,1536]{1,0:T(8,128)(2,1)S(1)}, u32[]{:S(2)}, u32[]{:S(2)}) collective-permute-start(bf16[16,1536]{1,0:T(8,128)(2,1)S(1)} %fusion.2), channel_id=1, source_target_pairs={{0,225},{1,224},{2,227},{3,226},{4,229},{5,228},{6,231},{7,230},{8... | collective-permute-start | bytes 147464 | tf_op jit(solution)/shard_map/stage1/ppermute | solution.py:127
  132.3 3.8 %collective-permute-start.25 = (bf16[16,1536]{1,0:T(8,128)(2,1)S(1)}, bf16[16,1536]{1,0:T(8,128)(2,1)S(1)}, u32[]{:S(2)}, u32[]{:S(2)}) collective-permute-start(bf16[16,1536]{1,0:T(8,128)(2,1)S(1)} %fusion.2), channel_id=1, source_target_pairs={{0,224},{1,225},{2,226},{3,227},{4,228},{5,229},{6,230},{7,231},{8... | collective-permute-start | bytes 147464 | tf_op jit(solution)/shard_map/stage1/ppermute | solution.py:127
  136.4 2.2 %collective-permute-start.26 = (bf16[16,384]{1,0:T(8,128)(2,1)S(1)}, bf16[16,384]{1,0:T(8,128)(2,1)S(1)}, u32[]{:S(2)}, u32[]{:S(2)}) collective-permute-start(bf16[16,384]{1,0:T(8,128)(2,1)S(1)} %fusion.7), channel_id=1, source_target_pairs={{0,32},{1,33},{2,34},{3,35},{4,36},{5,37},{6,38},{7,39},{8,40},{9,... | collective-permute-start | bytes 36872 | tf_op jit(solution)/shard_map/stage2/ppermute | solution.py:127
  138.8 6.0 %collective-permute-start.27 = (bf16[16,1536]{1,0:T(8,128)(2,1)S(1)}, bf16[16,1536]{1,0:T(8,128)(2,1)S(1)}, u32[]{:S(2)}, u32[]{:S(2)}) collective-permute-start(bf16[16,1536]{1,0:T(8,128)(2,1)S(1)} %fusion.3), channel_id=1, source_target_pairs={{0,227},{1,226},{2,225},{3,224},{4,231},{5,230},{6,229},{7,228},{8... | collective-permute-start | bytes 147464 | tf_op jit(solution)/shard_map/stage3/ppermute | solution.py:127
  140.0 6.4 %collective-permute-start.28 = (bf16[16,1536]{1,0:T(8,128)(2,1)S(1)}, bf16[16,1536]{1,0:T(8,128)(2,1)S(1)}, u32[]{:S(2)}, u32[]{:S(2)}) collective-permute-start(bf16[16,1536]{1,0:T(8,128)(2,1)S(1)} %fusion.3), channel_id=1, source_target_pairs={{0,226},{1,227},{2,224},{3,225},{4,230},{5,231},{6,228},{7,229},{8... | collective-permute-start | bytes 147464 | tf_op jit(solution)/shard_map/stage3/ppermute | solution.py:127
  142.7 4.5 %collective-permute-start.29 = (bf16[16,1536]{1,0:T(8,128)(2,1)S(1)}, bf16[16,1536]{1,0:T(8,128)(2,1)S(1)}, u32[]{:S(2)}, u32[]{:S(2)}) collective-permute-start(bf16[16,1536]{1,0:T(8,128)(2,1)S(1)} %fusion.3), channel_id=1, source_target_pairs={{0,225},{1,224},{2,227},{3,226},{4,229},{5,228},{6,231},{7,230},{8... | collective-permute-start | bytes 147464 | tf_op jit(solution)/shard_map/stage3/ppermute | solution.py:127
  143.2 4.5 %collective-permute-start.30 = (bf16[16,1536]{1,0:T(8,128)(2,1)S(1)}, bf16[16,1536]{1,0:T(8,128)(2,1)S(1)}, u32[]{:S(2)}, u32[]{:S(2)}) collective-permute-start(bf16[16,1536]{1,0:T(8,128)(2,1)S(1)} %fusion.3), channel_id=1, source_target_pairs={{0,224},{1,225},{2,226},{3,227},{4,228},{5,229},{6,230},{7,231},{8... | collective-permute-start | bytes 147464 | tf_op jit(solution)/shard_map/stage3/ppermute | solution.py:127
  147.9 5.4 %collective-permute-start.31 = (bf16[16,384]{1,0:T(8,128)(2,1)S(1)}, bf16[16,384]{1,0:T(8,128)(2,1)S(1)}, u32[]{:S(2)}, u32[]{:S(2)}) collective-permute-start(bf16[16,384]{1,0:T(8,128)(2,1)S(1)} %fusion.8), channel_id=1, source_target_pairs={{0,32},{1,33},{2,34},{3,35},{4,36},{5,37},{6,38},{7,39},{8,40},{9,... | collective-permute-start | bytes 36872 | tf_op jit(solution)/shard_map/stage4/ppermute | solution.py:127
  153.6 6.5 %collective-permute-start.32 = (bf16[16,1536]{1,0:T(8,128)(2,1)S(1)}, bf16[16,1536]{1,0:T(8,128)(2,1)S(1)}, u32[]{:S(2)}, u32[]{:S(2)}) collective-permute-start(bf16[16,1536]{1,0:T(8,128)(2,1)S(1)} %fusion.4), channel_id=1, source_target_pairs={{0,227},{1,226},{2,225},{3,224},{4,231},{5,230},{6,229},{7,228},{8... | collective-permute-start | bytes 147464 | tf_op jit(solution)/shard_map/stage5/ppermute | solution.py:127
  153.7 6.4 %collective-permute-start.33 = (bf16[16,1536]{1,0:T(8,128)(2,1)S(1)}, bf16[16,1536]{1,0:T(8,128)(2,1)S(1)}, u32[]{:S(2)}, u32[]{:S(2)}) collective-permute-start(bf16[16,1536]{1,0:T(8,128)(2,1)S(1)} %fusion.4), channel_id=1, source_target_pairs={{0,226},{1,227},{2,224},{3,225},{4,230},{5,231},{6,228},{7,229},{8... | collective-permute-start | bytes 147464 | tf_op jit(solution)/shard_map/stage5/ppermute | solution.py:127
  156.2 4.4 %collective-permute-start.34 = (bf16[16,1536]{1,0:T(8,128)(2,1)S(1)}, bf16[16,1536]{1,0:T(8,128)(2,1)S(1)}, u32[]{:S(2)}, u32[]{:S(2)}) collective-permute-start(bf16[16,1536]{1,0:T(8,128)(2,1)S(1)} %fusion.4), channel_id=1, source_target_pairs={{0,225},{1,224},{2,227},{3,226},{4,229},{5,228},{6,231},{7,230},{8... | collective-permute-start | bytes 147464 | tf_op jit(solution)/shard_map/stage5/ppermute | solution.py:127
  156.4 5.3 %collective-permute-start.35 = (bf16[16,1536]{1,0:T(8,128)(2,1)S(1)}, bf16[16,1536]{1,0:T(8,128)(2,1)S(1)}, u32[]{:S(2)}, u32[]{:S(2)}) collective-permute-start(bf16[16,1536]{1,0:T(8,128)(2,1)S(1)} %fusion.4), channel_id=1, source_target_pairs={{0,224},{1,225},{2,226},{3,227},{4,228},{5,229},{6,230},{7,231},{8... | collective-permute-start | bytes 147464 | tf_op jit(solution)/shard_map/stage5/ppermute | solution.py:127
  162.0 7.0 %collective-permute-start.36 = (bf16[16,384]{1,0:T(8,128)(2,1)S(1)}, bf16[16,384]{1,0:T(8,128)(2,1)S(1)}, u32[]{:S(2)}, u32[]{:S(2)}) collective-permute-start(bf16[16,384]{1,0:T(8,128)(2,1)S(1)} %fusion.9), channel_id=1, source_target_pairs={{0,32},{1,33},{2,34},{3,35},{4,36},{5,37},{6,38},{7,39},{8,40},{9,... | collective-permute-start | bytes 36872 | tf_op jit(solution)/shard_map/spread/ppermute | solution.py:127
  164.8 4.2 %collective-permute-start.37 = (bf16[16,384]{1,0:T(8,128)(2,1)S(1)}, bf16[16,384]{1,0:T(8,128)(2,1)S(1)}, u32[]{:S(2)}, u32[]{:S(2)}) collective-permute-start(bf16[16,384]{1,0:T(8,128)(2,1)S(1)} %fusion.9), channel_id=1, source_target_pairs={{0,33},{1,32},{2,35},{3,34},{4,37},{5,36},{6,39},{7,38},{8,41},{9,... | collective-permute-start | bytes 36872 | tf_op jit(solution)/shard_map/spread/ppermute | solution.py:127
  166.2 4.6 %collective-permute-start.38 = (bf16[16,384]{1,0:T(8,128)(2,1)S(1)}, bf16[16,384]{1,0:T(8,128)(2,1)S(1)}, u32[]{:S(2)}, u32[]{:S(2)}) collective-permute-start(bf16[16,384]{1,0:T(8,128)(2,1)S(1)} %fusion.9), channel_id=1, source_target_pairs={{0,34},{1,35},{2,32},{3,33},{4,38},{5,39},{6,36},{7,37},{8,42},{9,... | collective-permute-start | bytes 36872 | tf_op jit(solution)/shard_map/spread/ppermute | solution.py:127
  167.6 4.3 %collective-permute-start.39 = (bf16[16,384]{1,0:T(8,128)(2,1)S(1)}, bf16[16,384]{1,0:T(8,128)(2,1)S(1)}, u32[]{:S(2)}, u32[]{:S(2)}) collective-permute-start(bf16[16,384]{1,0:T(8,128)(2,1)S(1)} %fusion.9), channel_id=1, source_target_pairs={{0,35},{1,34},{2,33},{3,32},{4,39},{5,38},{6,37},{7,36},{8,43},{9,... | collective-permute-start | bytes 36872 | tf_op jit(solution)/shard_map/spread/ppermute | solution.py:127
